TPU v7x, 32 devices: a whole 2x2x4 slice. The times are simulated.
32 devices in a mesh: dp: 8 (over y, x, core), band: 4 (over z).
Axes of the slice: x: 2, y: 2, z: 4, core: 2. Of those that a mesh axis runs over, the one named last changes fastest.
Arguments:
- tokens_in: bfloat16 [24, 64, 64, 384], P('dp', 'band'), may hold values from -6 to 6
- cond: bfloat16 [24, 768], P('dp'), may hold values from -6 to 6
- loss_weight: float32 [24], P('dp'), may hold values from 0.3 to 3
- cotangent: bfloat16 [24, 64, 64, 384], P('dp', 'band'), may hold values from -6 to 6
- norm1_map: bfloat16 [768, 384], P(('dp', 'band')), may hold values from -0.15625 to 0.15625
- qkv_weight: bfloat16 [384, 1152], P(('dp', 'band')), may hold values from -0.3125 to 0.3125
- attn_scale: float32 [6], replicated, may hold values from 8 to 24
- out_weight: bfloat16 [384, 384], P(('dp', 'band')), may hold values from -1 to 1
- norm2_map: bfloat16 [768, 384], P(('dp', 'band')), may hold values from -0.15625 to 0.15625
- up_weight: bfloat16 [384, 3072], P(('dp', 'band')), may hold values from -0.3125 to 0.3125
- down_weight: bfloat16 [1536, 384], P(('dp', 'band')), may hold values from -0.21875 to 0.21875
Outputs:
- result: bfloat16 [24, 64, 64, 384], P('dp', 'band')
- grad_input: float32 [24, 64, 64, 384], P('dp', 'band')
- grad_cond: float32 [24, 768], P('dp')
- grad_norm1_map: float32 [768, 384], P(('dp', 'band'))
- grad_qkv_weight: float32 [384, 1152], P(('dp', 'band'))
- grad_attn_scale: float32 [6], replicated
- grad_out_weight: float32 [384, 384], P(('dp', 'band'))
- grad_norm2_map: float32 [768, 384], P(('dp', 'band'))
- grad_up_weight: float32 [384, 3072], P(('dp', 'band'))
- grad_down_weight: float32 [1536, 384], P(('dp', 'band'))
All inputs are finite; a program needn't handle non-finite values.
Results may differ from a plain program's by a relative error of at most 0.025.
The roundings to bfloat16 on the way count: a program that leaves them out, or rounds other values in their place, can miss the bound.
Values may be sent and summed in bfloat16 or wider, within the bound.
A program may use at most 384 MiB of HBM per device.

v0:
```python
import math

import jax
import jax.numpy as jnp
from jax import lax
from jax.sharding import PartitionSpec as P

KERNEL = 7


NORM_EPS = 1e-06


def extended_2(cells, sides, width):
    for axis, dim in sides:
        count = lax.axis_size(axis)
        ends = count - 1
        head = lax.slice_in_dim(cells, 0, width, axis=dim)
        tail = lax.slice_in_dim(cells, cells.shape[dim] - width, cells.shape[dim], axis=dim)
        cells = jnp.concatenate(
            [
                lax.ppermute(tail, axis, [(i, (i + 1) % count) for i in range(ends)]),
                cells,
                lax.ppermute(head, axis, [((i + 1) % count, i) for i in range(ends)]),
            ],
            axis=dim,
        )
    return cells


def shifted(x, axis, by):
    devices = lax.axis_size(axis)
    pairs = [(i, i + by) for i in range(devices) if 0 <= i + by < devices]
    return lax.ppermute(x, axis, pairs)


def ada_norm(values, scale):
    return values * scale * lax.rsqrt(jnp.mean(values * values, axis=-1, keepdims=True) + NORM_EPS)


def rope_table(row_place, col_place, height, width):
    freqs = math.pi * 10.0 ** (jnp.arange(8, dtype=jnp.float32) / 7.0)
    row_angle = ((2.0 * row_place + 1.0) / height - 1.0)[:, None] * freqs[None, :]
    col_angle = ((2.0 * col_place + 1.0) / width - 1.0)[:, None] * freqs[None, :]
    return (
        jnp.cos(row_angle)[:, None, :],
        jnp.sin(row_angle)[:, None, :],
        jnp.cos(col_angle)[:, None, :],
        jnp.sin(col_angle)[:, None, :],
    )


def rotate(tensor, tables):
    row_cos, row_sin, col_cos, col_sin = tables
    first = tensor[..., 0:8]
    second = tensor[..., 8:16]
    third = tensor[..., 16:24]
    fourth = tensor[..., 24:32]
    return jnp.concatenate(
        [
            first * row_cos - second * row_sin,
            second * row_cos + first * row_sin,
            third * col_cos - fourth * col_sin,
            fourth * col_cos + third * col_sin,
            tensor[..., 32:],
        ],
        axis=-1,
    )


def shape_qk(paired, scale, tables, model_dim):
    head_count = scale.shape[0]
    head_size = model_dim // head_count
    leading = paired.shape[:-1]
    query = paired[..., :model_dim].reshape(leading + (head_count, head_size))
    keys_part = paired[..., model_dim:].reshape(leading + (head_count, head_size))
    factor = jnp.sqrt(scale)[:, None]
    query = query * factor * lax.rsqrt(jnp.sum(query * query, axis=-1, keepdims=True) + NORM_EPS)
    keys_part = (
        keys_part
        * factor
        * lax.rsqrt(jnp.sum(keys_part * keys_part, axis=-1, keepdims=True) + NORM_EPS)
    )
    return (rotate(query, tables), rotate(keys_part, tables))


def gated_gelu(lifted):
    hidden_units = lifted.shape[-1] // 2
    return lifted[..., :hidden_units] * jax.nn.gelu(lifted[..., hidden_units:], approximate=False)


def shards(
    tokens_in,
    cond,
    loss_weight,
    cotangent,
    norm1_map,
    qkv_weight,
    attn_scale,
    out_weight,
    norm2_map,
    up_weight,
    down_weight,
):
    precise = lax.Precision.HIGHEST
    gathered = (
        lax.all_gather(norm1_map, ("dp", "band"), axis=0, tiled=True),
        lax.all_gather(qkv_weight, ("dp", "band"), axis=0, tiled=True),
        lax.all_gather(out_weight, ("dp", "band"), axis=0, tiled=True),
        lax.all_gather(norm2_map, ("dp", "band"), axis=0, tiled=True),
        lax.all_gather(up_weight, ("dp", "band"), axis=0, tiled=True),
        lax.all_gather(down_weight, ("dp", "band"), axis=0, tiled=True),
    )
    map_one, w_qkv, w_out, map_two, w_up, w_down = gathered
    image_count, band_rows, row_width, model_dim = tokens_in.shape
    head_count = attn_scale.shape[0]
    head_size = model_dim // head_count
    token_count = band_rows * row_width
    radius = KERNEL // 2
    span = 2 * radius + 2
    group_count = band_rows // 2
    query_block = 2 * row_width
    key_block = span * row_width
    band_index = lax.axis_index("band")
    height = band_rows * lax.axis_size("band")
    first_row = band_index * band_rows
    query_place = jnp.arange(token_count)
    tables = rope_table(
        (first_row + query_place // row_width).astype(jnp.float32),
        (query_place % row_width).astype(jnp.float32),
        height,
        row_width,
    )
    query_index = jnp.arange(query_block)
    query_row = query_index // row_width
    query_col = query_index % row_width
    key_index = jnp.arange(key_block)
    key_row = key_index // row_width
    key_col = key_index % row_width
    groups = jnp.arange(group_count)
    global_key = first_row + 2 * groups[:, None] + key_row[None, :] - radius
    nearby = (jnp.abs(key_row[None, :] - radius - query_row[:, None]) <= radius) & (
        jnp.abs(key_col[None, :] - query_col[:, None]) <= radius
    )
    inside = (global_key >= 0) & (global_key < height)
    window_mask = nearby[None, :, :] & inside[:, None, :]
    inputs_f = tokens_in.astype(jnp.float32).reshape(image_count, token_count, model_dim)
    cond_f = cond.astype(jnp.float32)
    scale_one = 1.0 + jnp.dot(cond, map_one, preferred_element_type=jnp.float32)
    scale_two = 1.0 + jnp.dot(cond, map_two, preferred_element_type=jnp.float32)
    normed_one, pull_one = jax.vjp(ada_norm, inputs_f, scale_one[:, None, :])
    normed_low = normed_one.astype(jnp.bfloat16)
    mixed = jnp.dot(normed_low, w_qkv, preferred_element_type=jnp.float32)

    def make_qk(paired, scale):
        return shape_qk(paired, scale, tables, model_dim)

    (query_f, keys_f), pull_qk = jax.vjp(make_qk, mixed[..., : 2 * model_dim], attn_scale)
    query_blocks = query_f.astype(jnp.bfloat16).reshape(
        image_count, group_count, query_block, head_count, head_size
    )
    keys_low = keys_f.astype(jnp.bfloat16).reshape(image_count, band_rows, row_width, model_dim)
    values_low = (
        mixed[..., 2 * model_dim :]
        .astype(jnp.bfloat16)
        .reshape(image_count, band_rows, row_width, model_dim)
    )
    stacked = jnp.concatenate([keys_low, values_low], axis=-1)
    extended = extended_2(stacked, (("band", 1),), KERNEL // 2)
    pairs = extended.reshape(image_count, group_count + radius, 2, row_width, 2 * model_dim)
    windows = jnp.concatenate([pairs[:, j : j + group_count] for j in range(radius + 1)], axis=2)
    windows = windows.reshape(image_count, group_count, key_block, 2 * model_dim)
    keys_win = windows[..., :model_dim].reshape(
        image_count, group_count, key_block, head_count, head_size
    )
    values_win = windows[..., model_dim:].reshape(
        image_count, group_count, key_block, head_count, head_size
    )

    def attend_image(parts):
        query, keys, values = parts
        scores = jnp.einsum("gqhd,gkhd->ghqk", query, keys, preferred_element_type=jnp.float32)
        scores = jnp.where(window_mask[:, None], scores, -1e30)
        row_max = jnp.max(scores, axis=-1, keepdims=True)
        exponent = jnp.exp(scores - row_max)
        row_total = jnp.sum(exponent, axis=-1, keepdims=True)
        probs_low = (exponent / row_total).astype(jnp.bfloat16)
        attended = jnp.einsum(
            "ghqk,gkhd->gqhd", probs_low, values, preferred_element_type=jnp.float32
        )
        return (attended.astype(jnp.bfloat16), row_max + jnp.log(row_total))

    attended_blocks, log_total = lax.map(attend_image, (query_blocks, keys_win, values_win))
    attended_low = attended_blocks.reshape(image_count, token_count, model_dim)
    residual = inputs_f + jnp.dot(attended_low, w_out, preferred_element_type=jnp.float32)
    normed_two, pull_two = jax.vjp(ada_norm, residual, scale_two[:, None, :])
    normed_two_low = normed_two.astype(jnp.bfloat16)
    lifted = jnp.dot(normed_two_low, w_up, preferred_element_type=jnp.float32)
    hidden, pull_gate = jax.vjp(gated_gelu, lifted)
    hidden_low = hidden.astype(jnp.bfloat16)
    result = (residual + jnp.dot(hidden_low, w_down, preferred_element_type=jnp.float32)).astype(
        jnp.bfloat16
    )
    again = (
        lax.all_gather(norm1_map, ("dp", "band"), axis=0, tiled=True),
        lax.all_gather(qkv_weight, ("dp", "band"), axis=0, tiled=True),
        lax.all_gather(out_weight, ("dp", "band"), axis=0, tiled=True),
        lax.all_gather(norm2_map, ("dp", "band"), axis=0, tiled=True),
        lax.all_gather(up_weight, ("dp", "band"), axis=0, tiled=True),
        lax.all_gather(down_weight, ("dp", "band"), axis=0, tiled=True),
    )
    map_one, w_qkv, w_out, map_two, w_up, w_down = again
    loss_seed = (
        cotangent.astype(jnp.float32).reshape(image_count, token_count, model_dim)
        * loss_weight[:, None, None]
    )
    loss_seed_low = loss_seed.astype(jnp.bfloat16)
    grad_down = jnp.einsum(
        "itf,itd->fd", hidden_low, loss_seed_low, preferred_element_type=jnp.float32
    )
    d_hidden = jnp.einsum("itd,fd->itf", loss_seed_low, w_down, preferred_element_type=jnp.float32)
    d_lifted = pull_gate(d_hidden)[0].astype(jnp.bfloat16)
    grad_up = jnp.einsum(
        "itd,itf->df", normed_two_low, d_lifted, preferred_element_type=jnp.float32
    )
    d_normed_two = jnp.einsum("itf,df->itd", d_lifted, w_up, preferred_element_type=jnp.float32)
    d_resid_part, d_scale_two = pull_two(d_normed_two)
    d_residual = loss_seed + d_resid_part
    resid_low = d_residual.astype(jnp.bfloat16)
    grad_out = jnp.einsum(
        "itd,ite->de", attended_low, resid_low, preferred_element_type=jnp.float32
    )
    d_attended = jnp.einsum("ite,de->itd", resid_low, w_out, preferred_element_type=jnp.float32)
    d_attended_blocks = d_attended.astype(jnp.bfloat16).reshape(
        image_count, group_count, query_block, head_count, head_size
    )

    def attend_back(parts):
        query, keys, values, d_att, kept_log = parts
        again_scores = jnp.einsum(
            "gqhd,gkhd->ghqk", query, keys, preferred_element_type=jnp.float32
        )
        probs_again = jnp.exp(jnp.where(window_mask[:, None], again_scores, -1e30) - kept_log)
        probs_again_low = probs_again.astype(jnp.bfloat16)
        d_probs = jnp.einsum("gqhd,gkhd->ghqk", d_att, values, preferred_element_type=jnp.float32)
        inner = jnp.sum(probs_again * d_probs, axis=-1, keepdims=True)
        d_scores_low = (probs_again * (d_probs - inner)).astype(jnp.bfloat16)
        d_values = jnp.einsum(
            "ghqk,gqhd->gkhd", probs_again_low, d_att, preferred_element_type=jnp.float32
        )
        d_keys = jnp.einsum(
            "ghqk,gqhd->gkhd", d_scores_low, query, preferred_element_type=jnp.float32
        )
        d_query = jnp.einsum(
            "ghqk,gkhd->gqhd", d_scores_low, keys, preferred_element_type=jnp.float32
        )
        d_both = jnp.concatenate(
            [
                d_keys.reshape(group_count, key_block, model_dim),
                d_values.reshape(group_count, key_block, model_dim),
            ],
            axis=-1,
        )
        return (d_query, d_both)

    d_query_blocks, d_windows = lax.map(
        attend_back, (query_blocks, keys_win, values_win, d_attended_blocks, log_total)
    )
    d_query = d_query_blocks.reshape(image_count, token_count, head_count, head_size)
    d_windows = d_windows.reshape(image_count, group_count, radius + 1, 2, row_width, 2 * model_dim)
    d_pairs = jnp.zeros(
        (image_count, group_count + radius, 2, row_width, 2 * model_dim), jnp.float32
    )
    for j in range(radius + 1):
        d_pairs = d_pairs + jnp.pad(
            d_windows[:, :, j], ((0, 0), (j, radius - j), (0, 0), (0, 0), (0, 0))
        )
    d_stacked = d_pairs.reshape(image_count, band_rows + 2 * radius, row_width, 2 * model_dim)
    from_below = shifted(d_stacked[:, :radius].astype(jnp.bfloat16), "band", -1).astype(jnp.float32)
    from_above = shifted(d_stacked[:, band_rows + radius :].astype(jnp.bfloat16), "band", 1).astype(
        jnp.float32
    )
    own_rows = d_stacked[:, radius : band_rows + radius]
    own_rows = own_rows.at[:, :radius].add(from_above)
    own_rows = own_rows.at[:, band_rows - radius :].add(from_below)
    d_keys_own = own_rows[..., :model_dim].reshape(image_count, token_count, head_count, head_size)
    d_values_own = own_rows[..., model_dim:].reshape(image_count, token_count, model_dim)
    d_qk_part, d_scale_heads = pull_qk((d_query, d_keys_own))
    d_mixed_low = jnp.concatenate([d_qk_part, d_values_own], axis=-1).astype(jnp.bfloat16)
    grad_qkv = jnp.einsum(
        "itd,ite->de", normed_low, d_mixed_low, preferred_element_type=jnp.float32
    )
    d_normed_one = jnp.einsum("ite,de->itd", d_mixed_low, w_qkv, preferred_element_type=jnp.float32)
    d_input_part, d_scale_one = pull_one(d_normed_one)
    grad_input = d_residual + d_input_part
    scale_grad_one = d_scale_one[:, 0, :]
    scale_grad_two = d_scale_two[:, 0, :]
    grad_map_one = jnp.dot(cond_f.T, scale_grad_one, precision=precise)
    grad_map_two = jnp.dot(cond_f.T, scale_grad_two, precision=precise)
    cond_part = jnp.dot(scale_grad_one, map_one.astype(jnp.float32).T, precision=precise) + jnp.dot(
        scale_grad_two, map_two.astype(jnp.float32).T, precision=precise
    )
    grad_cond = lax.psum(cond_part, "band")
    grad_scale = lax.psum(d_scale_heads, ("dp", "band"))
    summed = (
        lax.psum_scatter(grad_map_one, ("dp", "band"), scatter_dimension=0, tiled=True),
        lax.psum_scatter(grad_qkv, ("dp", "band"), scatter_dimension=0, tiled=True),
        lax.psum_scatter(grad_out, ("dp", "band"), scatter_dimension=0, tiled=True),
        lax.psum_scatter(grad_map_two, ("dp", "band"), scatter_dimension=0, tiled=True),
        lax.psum_scatter(grad_up, ("dp", "band"), scatter_dimension=0, tiled=True),
        lax.psum_scatter(grad_down, ("dp", "band"), scatter_dimension=0, tiled=True),
    )
    return (
        result.reshape(tokens_in.shape),
        grad_input.reshape(tokens_in.shape),
        grad_cond,
        summed[0],
        summed[1],
        grad_scale,
        summed[2],
        summed[3],
        summed[4],
        summed[5],
    )


def solution(mesh):
    return jax.shard_map(
        shards,
        mesh=mesh,
        in_specs=(
            P("dp", "band", None, None),
            P("dp", None),
            P("dp"),
            P("dp", "band", None, None),
            P(("dp", "band"), None),
            P(("dp", "band"), None),
            P(),
            P(("dp", "band"), None),
            P(("dp", "band"), None),
            P(("dp", "band"), None),
            P(("dp", "band"), None),
        ),
        out_specs=(
            P("dp", "band", None, None),
            P("dp", "band", None, None),
            P("dp", None),
            P(("dp", "band"), None),
            P(("dp", "band"), None),
            P(),
            P(("dp", "band"), None),
            P(("dp", "band"), None),
            P(("dp", "band"), None),
            P(("dp", "band"), None),
        ),
        check_vma=False,
    )
```

profile of v0, /device:TPU:0, one launch (start us, length us, event | category | flops | bytes accessed | tf_op | source)
XLA Modules:
  0.0 1494.3 jit_solution(3932832242401293950)
XLA Ops:
  8.0 76.3 %all_gather.24 = bf16[768,384]{1,0:T(8,128)(2,1)S(1)} all-gather(bf16[24,384]{1,0:T(8,128)(2,1)} %param.23), channel_id=1, replica_groups=mesh['dp'=8,'band'=4] {'dp','band'}, dimensions={0}, use_global_device_ids=true | all-gather | bytes 608256 | tf_op jit(solution)/shard_map/all_gather | solution.py:107
  86.8 79.9 %all-gather = bf16[32,12,1152]{2,1,0:T(8,128)(2,1)} all-gather(bf16[1,12,1152]{2,1,0:T(8,128)(2,1)} %bitcast.308), channel_id=1, replica_groups=mesh['dp'=8,'band'=4] {'dp','band'}, dimensions={0}, use_global_device_ids=true | all-gather | bytes 912384 | tf_op jit(solution)/shard_map/all_gather | solution.py:108
  250.3 69.2 %all-gather.1 = bf16[32,12,384]{2,1,0:T(8,128)(2,1)S(1)} all-gather(bf16[1,12,384]{2,1,0:T(8,128)(2,1)S(1)} %bitcast.309), channel_id=1, replica_groups=mesh['dp'=8,'band'=4] {'dp','band'}, dimensions={0}, use_global_device_ids=true | all-gather | bytes 304128 | tf_op jit(solution)/shard_map/all_gather | solution.py:109
  322.2 11.8 copy.98
  334.8 68.9 %all_gather.27 = bf16[768,384]{1,0:T(8,128)(2,1)S(1)} all-gather(bf16[24,384]{1,0:T(8,128)(2,1)S(1)} %copy-done.60), channel_id=1, replica_groups=mesh['dp'=8,'band'=4] {'dp','band'}, dimensions={0}, use_global_device_ids=true | all-gather | bytes 608256 | tf_op jit(solution)/shard_map/all_gather | solution.py:110
  416.7 17.0 %pad_maximum_fusion = bf16[3,8,8,64,768]{4,3,2,1,0:T(8,128)(2,1)} fusion(bf16[3,8,2,64,768]{4,3,2,1,0:T(8,128)(2,1)} %get-tuple-element.345, bf16[3,8,2,64,768]{4,3,2,1,0:T(8,128)(2,1)} %get-tuple-element.346, bf16[3,8,2,64,768]{4,3,2,1,0:T(8,128)(2,1)} %get-tuple-element.347, bf16[3,8,2,64,768]{4,3,2,1,0:T(8,128)(2,1)} %get-tuple-element.344), kind=kLoop, calls=%fused_computation.60 | loop fusion | flops 28311552 | bytes 37748736 | tf_op jit(solution)/shard_map/concatenate | solution.py:171
  433.7 15.1 %fusion.127 = (bf16[3,8,512,384]{3,2,1,0:T(8,128)(2,1)}, bf16[3,8,512,384]{3,2,1,0:T(8,128)(2,1)}) fusion(bf16[3,8,512,768]{3,2,1,0:T(8,128)(2,1)} %bitcast.285), kind=kLoop, calls=%fused_computation.253 | loop fusion | bytes 37748736 | tf_op jit(solution)/shard_map/slice | solution.py:173
  448.8 12.6 copy.99
  461.4 12.7 copy.101
  474.1 47.9 %while.28 = (s32[]{:T(128)}, bf16[3,8,128,6,64]{2,1,4,3,0:T(8,128)(2,1)}, f32[3,8,6,128,1]{3,2,1,4,0:T(8,128)}, bf16[3,8,512,6,64]{2,4,3,1,0:T(8,128)(2,1)}, bf1...) while((s32[]{:T(128)}, ...), condition=%wide.region_6.7_spmd.clone, body=%wide.region_3.6_spmd.clone.sunk | while | flops 834529280 | bytes 49560156 | solution.py:193
  535.9 30.2 %fusion.86 = f32[3,1024,3072]{2,1,0:T(8,128)} fusion(bf16[384,3072,1]{1,0,2:T(8,128)(2,1)S(1)} %reshape.605, f32[3,1024,384]{2,1,0:T(8,128)} %get-tuple-element.379, f32[3,1024]{1,0:T(4,128)S(1)} %fusion.95, f32[3,384]{1,0:T(4,128)S(1)} %copy-done.48), kind=kOutput, calls=%fused_computation.156 | convolution fusion | flops 7251296256 | bytes 44843520 | tf_op jit(solution)/shard_map/dot_general | solution.py:198
  566.1 52.4 %multiply_add_fusion = (f32[3,1024,1536]{2,1,0:T(8,128)}, f32[3,1024,1536]{2,1,0:T(8,128)}, f32[3,1024,1536]{2,1,0:T(8,128)}) fusion(f32[3,1024,3072]{2,1,0:T(8,128)} %fusion.86, bf16[3,1024,384]{2,1,0:T(8,128)(2,1)} %fusion.62, bf16[1536,384]{1,0:T(8,128)(2,1)} %all-gather.6.cloned.1.call-done), kind=kOutput, calls=%fused_computation.61 | convolution fusion | flops 3963617280 | bytes 97910784 | tf_op jit(solution)/shard_map/itd,fd->itf/dot_general | solution.py:221
  618.5 35.4 %fusion.60 = (f32[3,1024,1536]{2,1,0:T(8,128)}, bf16[3,1024,1536]{2,1,0:T(8,128)(2,1)}) fusion(f32[3,1024,1536]{2,1,0:T(8,128)} %get-tuple-element.380, f32[3,1024,1536]{2,1,0:T(8,128)} %get-tuple-element.325, f32[3,1024,3072]{2,1,0:T(8,128)} %fusion.86), kind=kLoop, calls=%fused_computation.91 | loop fusion | flops 23592960 | bytes 103809024 | tf_op jit(solution)/shard_map/transpose(jvp())/mul | solution.py:89
  654.0 20.3 %multiply_reduce_fusion.3 = (f32[3,384]{1,0:T(4,128)}, f32[3,1024]{1,0:T(4,128)S(1)}, f32[3,1024,384]{2,1,0:T(8,128)}) fusion(f32[3,1024,384]{2,1,0:T(8,128)} %get-tuple-element.379, f32[3,1024]{1,0:T(4,128)S(1)} %copy-done.40, f32[3,384]{1,0:T(4,128)S(1)} %copy-done.49, bf16[384,3072,1]{1,0,2:T(8,128)(2,1)S(1)} %copy-done.11, ...), kind=kOutput, calls=%fused_computation.116 | convolution fusion | flops 7273705472 | bytes 49579008 | tf_op jit(solution)/shard_map/itf,df->itd/dot_general | solution.py:226
  689.5 215.7 %while.29 = (s32[]{:T(128)}, f32[3,8,128,6,64]{2,1,4,3,0:T(8,128)}, f32[3,8,512,768]{3,2,1,0:T(8,128)}, bf16[3,8,512,6,64]{2,4,3,1,0:T(8,128)(2,1)}, bf16[3,8,12...) while((s32[]{:T(128)}, f32[3,8,128,6,64]{2,1,4,3,0:T(8,128)}, ...), condition=%wide.region_11.12_spmd.clone, body=%wide.region_9.11_spmd.clone.sunk | while | flops 2054678528 | bytes 247709392 | solution.py:266
  732.3 12.9 copy.191
  804.0 12.9 copy.191
  875.7 12.9 copy.191
  905.2 25.6 %slice_bitcast_fusion.3 = (f32[3,8,2,64,768]{4,3,2,1,0:T(8,128)}, f32[3,8,2,64,768]{4,3,2,1,0:T(8,128)}, f32[3,8,2,64,768]{4,3,2,1,0:T(8,128)}, f32[3,8,2,64,768]{4,3,2,1,0:T(8,128)}) fusion(f32[3,8,4,2,64,768]{5,4,3,2,1,0:T(8,128)} %bitcast.289), kind=kLoop, calls=%fused_computation.87 | loop fusion | bytes 75497472 | tf_op jit(solution)/shard_map/squeeze | solution.py:276
  930.9 18.2 %pad_add_fusion = f32[3,11,2,64,768]{4,3,2,1,0:T(8,128)} fusion(f32[3,8,2,64,768]{4,3,2,1,0:T(8,128)} %get-tuple-element.334, f32[3,8,2,64,768]{4,3,2,1,0:T(8,128)} %get-tuple-element.335, f32[3,8,2,64,768]{4,3,2,1,0:T(8,128)} %get-tuple-element.333, f32[3,8,2,64,768]{4,3,2,1,0:T(8,128)} %get-tuple-element.332), kind=kLoop, calls=%fused_computation.78 | loop fusion | flops 9732096 | bytes 50724864 | tf_op jit(solution)/shard_map/add | solution.py:275
  1068.6 18.8 %convolution_bitcast_fusion = f32[384,3072]{1,0:T(8,128)} fusion(f32[3,1024,1536]{2,1,0:T(8,128)} %get-tuple-element.330, f32[3,1024,1536]{2,1,0:T(8,128)} %get-tuple-element.324, f32[3,1024,384]{2,1,0:T(8,128)} %get-tuple-element.379, f32[3,1024]{1,0:T(4,128)S(1)} %copy-done.41, f32[3,384]{1,0:T(4,128)S(1)} %copy-done.50), kind=kOutput, calls=%fused_computation.129 | convolution fusion | flops 7270170624 | bytes 47202816 | tf_op jit(solution)/shard_map/itd,itf->df/dot_general | solution.py:223
  1104.3 232.2 %fusion.125 = (f32[16,1152]{1,0:T(8,128)S(1)}, f32[16,384]{1,0:T(8,128)S(1)}, f32[16,3072]{1,0:T(8,128)S(1)}) fusion(f32[384,1152]{1,0:T(8,128)} %fusion.74, f32[384,384]{1,0:T(8,128)S(1)} %copy-done.30, f32[384,3072]{1,0:T(8,128)} %convolution_bitcast_fusion), kind=kCustom, calls=%all-reduce-scatter.3 | all-reduce-scatter fusion | flops 2359297 | bytes 7372800
  1391.0 37.9 %psum.15 = f32[6]{0:T(128)} all-reduce(f32[6]{0:T(128)S(1)} %divide_multiply_fusion), channel_id=1, replica_groups=mesh['dp'=8,'band'=4] {'dp','band'}, use_global_device_ids=true, to_apply=%region_22.23 | all-reduce | flops 6 | bytes 48 | tf_op jit(solution)/shard_map/psum | solution.py:304
  1428.9 18.2 %psum.14 = f32[3,768]{1,0:T(4,128)} all-reduce(f32[3,768]{1,0:T(4,128)S(1)} %convolution_add_fusion), channel_id=1, replica_groups=mesh['dp'=8,'band'=4] {'band'}, use_global_device_ids=true, to_apply=%region_17.18 | all-reduce | flops 2304 | bytes 18432 | tf_op jit(solution)/shard_map/psum | solution.py:303
  (415 shorter events, 586.6 us)
Async XLA Ops:
  7.2 525.8 %all-gather.8.cloned.1.call-start = ((), (), s32[]{:S(2)}) async-start(), calls=%async_computation.3 | async-start | bytes 3244032 | tf_op jit(solution)/shard_map/all_gather | solution.py:111
  7.9 558.2 %all-gather.6.cloned.1.call-start = ((), (), s32[]{:S(2)}) async-start(), calls=%async_computation.1 | async-start | bytes 1216512 | tf_op jit(solution)/shard_map/all_gather | solution.py:112
  228.9 178.5 %collective-permute-start = (bf16[3,3,64,768]{3,2,1,0:T(8,128)(2,1)}, bf16[3,3,64,768]{3,2,1,0:T(8,128)(2,1)}, u32[]{:S(2)}, u32[]{:S(2)}) collective-permute-start(bf16[3,3,64,768]{3,2,1,0:T(8,128)(2,1)} %copy.96), channel_id=1, source_target_pairs={{0,1},{1,2},{2,3},{4,5},{5,6},{6,7},{8,9},{9,10},{10,11},{12,13},{... | collective-permute-start | bytes 2654216 | tf_op jit(solution)/shard_map/ppermute | solution.py:22
  235.2 172.2 %collective-permute-start.1 = (bf16[3,3,64,768]{3,2,1,0:T(8,128)(2,1)}, bf16[3,3,64,768]{3,2,1,0:T(8,128)(2,1)}, u32[]{:S(2)}, u32[]{:S(2)}) collective-permute-start(bf16[3,3,64,768]{3,2,1,0:T(8,128)(2,1)} %copy.97), channel_id=1, source_target_pairs={{1,0},{2,1},{3,2},{5,4},{6,5},{7,6},{9,8},{10,9},{11,10},{13,12},{... | collective-permute-start | bytes 2654216 | tf_op jit(solution)/shard_map/ppermute | solution.py:24
  236.6 1247.1 %all-reduce.30.cloned.1.call-start = ((), (), s32[]{:S(2)}) async-start(), calls=%async_computation.4 | async-start | bytes 4718592
  960.2 35.1 %collective-permute-start.2 = (bf16[3,3,64,768]{3,2,1,0:T(8,128)(2,1)}, bf16[3,3,64,768]{3,2,1,0:T(8,128)(2,1)}, u32[]{:S(2)}, u32[]{:S(2)}) collective-permute-start(bf16[3,3,64,768]{3,2,1,0:T(8,128)(2,1)} %get-tuple-element.343), channel_id=1, source_target_pairs={{0,1},{1,2},{2,3},{4,5},{5,6},{6,7},{8,9},{9,10},{10,11},{12,13},{... | collective-permute-start | bytes 2654216 | tf_op jit(solution)/shard_map/ppermute | solution.py:34
  964.4 32.8 %collective-permute-start.3 = (bf16[3,3,64,768]{3,2,1,0:T(8,128)(2,1)}, bf16[3,3,64,768]{3,2,1,0:T(8,128)(2,1)}, u32[]{:S(2)}, u32[]{:S(2)}) collective-permute-start(bf16[3,3,64,768]{3,2,1,0:T(8,128)(2,1)} %get-tuple-element.342), channel_id=1, source_target_pairs={{1,0},{2,1},{3,2},{5,4},{6,5},{7,6},{9,8},{10,9},{11,10},{13,12},{... | collective-permute-start | bytes 2654216 | tf_op jit(solution)/shard_map/ppermute | solution.py:34
  1068.5 418.8 %reduce-scatter.10.cloned.1.call-start = ((), (), s32[]{:S(2)}) async-start(), calls=%async_computation.2 | async-start | bytes 2433024 | tf_op jit(solution)/shard_map/reduce_scatter | solution.py:311
  1336.5 23.1 %collective-permute-start.12 = (f32[16,384]{1,0:T(8,128)S(1)}, f32[16,384]{1,0:T(8,128)S(1)}, u32[]{:S(2)}, u32[]{:S(2)}) collective-permute-start(f32[16,384]{1,0:T(8,128)S(1)} %get-tuple-element.322), channel_id=1, source_target_pairs={{0,1},{1,2},{2,3},{3,4},{4,5},{5,6},{6,7},{7,8},{8,9},{9,10},{10,1... | collective-permute-start | bytes 73736
  1338.1 24.8 %collective-permute-start.13 = (f32[16,384]{1,0:T(8,128)S(1)}, f32[16,384]{1,0:T(8,128)S(1)}, u32[]{:S(2)}, u32[]{:S(2)}) collective-permute-start(f32[16,384]{1,0:T(8,128)S(1)} %get-tuple-element.322), channel_id=1, source_target_pairs={{0,2},{1,3},{2,4},{3,5},{4,6},{5,7},{6,8},{7,9},{8,10},{9,11},{10,... | collective-permute-start | bytes 73736
  1339.4 27.3 %collective-permute-start.14 = (f32[16,384]{1,0:T(8,128)S(1)}, f32[16,384]{1,0:T(8,128)S(1)}, u32[]{:S(2)}, u32[]{:S(2)}) collective-permute-start(f32[16,384]{1,0:T(8,128)S(1)} %get-tuple-element.322), channel_id=1, source_target_pairs={{0,3},{1,4},{2,5},{3,6},{4,7},{5,8},{6,9},{7,10},{8,11},{9,12},{10... | collective-permute-start | bytes 73736
  1342.0 26.6 %collective-permute-start.15 = (f32[16,384]{1,0:T(8,128)S(1)}, f32[16,384]{1,0:T(8,128)S(1)}, u32[]{:S(2)}, u32[]{:S(2)}) collective-permute-start(f32[16,384]{1,0:T(8,128)S(1)} %get-tuple-element.322), channel_id=1, source_target_pairs={{0,4},{1,5},{2,6},{3,7},{4,8},{5,9},{6,10},{7,11},{8,12},{9,13},{1... | collective-permute-start | bytes 73736
  1343.3 14.4 collective-permute-start.19
  1366.7 13.7 collective-permute-start.10
  1368.7 14.9 collective-permute-start.4
  1370.0 18.2 %collective-permute-start.5 = (f32[16,1152]{1,0:T(8,128)S(1)}, f32[16,1152]{1,0:T(8,128)S(1)}, u32[]{:S(2)}, u32[]{:S(2)}) collective-permute-start(f32[16,1152]{1,0:T(8,128)S(1)} %get-tuple-element.321), channel_id=1, source_target_pairs={{0,2},{1,3},{2,4},{3,5},{4,6},{5,7},{6,8},{7,9},{8,10},{9,11},{10,... | collective-permute-start | bytes 221192
  1374.4 93.0 %collective-permute-start.20 = (f32[16,3072]{1,0:T(8,128)S(1)}, f32[16,3072]{1,0:T(8,128)S(1)}, u32[]{:S(2)}, u32[]{:S(2)}) collective-permute-start(f32[16,3072]{1,0:T(8,128)S(1)} %get-tuple-element.323), channel_id=1, source_target_pairs={{0,1},{1,2},{2,3},{3,4},{4,5},{5,6},{6,7},{7,8},{8,9},{9,10},{10,1... | collective-permute-start | bytes 589832
  1378.5 92.8 %collective-permute-start.21 = (f32[16,3072]{1,0:T(8,128)S(1)}, f32[16,3072]{1,0:T(8,128)S(1)}, u32[]{:S(2)}, u32[]{:S(2)}) collective-permute-start(f32[16,3072]{1,0:T(8,128)S(1)} %get-tuple-element.323), channel_id=1, source_target_pairs={{0,2},{1,3},{2,4},{3,5},{4,6},{5,7},{6,8},{7,9},{8,10},{9,11},{10,... | collective-permute-start | bytes 589832
  1380.4 67.6 %collective-permute-start.6 = (f32[16,1152]{1,0:T(8,128)S(1)}, f32[16,1152]{1,0:T(8,128)S(1)}, u32[]{:S(2)}, u32[]{:S(2)}) collective-permute-start(f32[16,1152]{1,0:T(8,128)S(1)} %get-tuple-element.321), channel_id=1, source_target_pairs={{0,3},{1,4},{2,5},{3,6},{4,7},{5,8},{6,9},{7,10},{8,11},{9,12},{10... | collective-permute-start | bytes 221192
  1383.6 65.8 %collective-permute-start.7 = (f32[16,1152]{1,0:T(8,128)S(1)}, f32[16,1152]{1,0:T(8,128)S(1)}, u32[]{:S(2)}, u32[]{:S(2)}) collective-permute-start(f32[16,1152]{1,0:T(8,128)S(1)} %get-tuple-element.321), channel_id=1, source_target_pairs={{0,4},{1,5},{2,6},{3,7},{4,8},{5,9},{6,10},{7,11},{8,12},{9,13},{1... | collective-permute-start | bytes 221192
  1388.2 74.2 %collective-permute-start.27 = (f32[12,3072]{1,0:T(8,128)S(1)}, f32[12,3072]{1,0:T(8,128)S(1)}, u32[]{:S(2)}, u32[]{:S(2)}) collective-permute-start(f32[12,3072]{1,0:T(8,128)S(1)} %slice.236), channel_id=1, source_target_pairs={{0,8},{1,9},{2,10},{3,11},{4,12},{5,13},{6,14},{7,15},{8,16},{9,17... | collective-permute-start | bytes 442376
  1454.3 21.8 %collective-permute-start.22 = (f32[16,3072]{1,0:T(8,128)S(1)}, f32[16,3072]{1,0:T(8,128)S(1)}, u32[]{:S(2)}, u32[]{:S(2)}) collective-permute-start(f32[16,3072]{1,0:T(8,128)S(1)} %get-tuple-element.323), channel_id=1, source_target_pairs={{0,3},{1,4},{2,5},{3,6},{4,7},{5,8},{6,9},{7,10},{8,11},{9,12},{10... | collective-permute-start | bytes 589832
  1459.4 16.6 %collective-permute-start.23 = (f32[16,3072]{1,0:T(8,128)S(1)}, f32[16,3072]{1,0:T(8,128)S(1)}, u32[]{:S(2)}, u32[]{:S(2)}) collective-permute-start(f32[16,3072]{1,0:T(8,128)S(1)} %get-tuple-element.323), channel_id=1, source_target_pairs={{0,4},{1,5},{2,6},{3,7},{4,8},{5,9},{6,10},{7,11},{8,12},{9,13},{1... | collective-permute-start | bytes 589832
  1462.4 13.6 collective-permute-start.24
  (94 other events, 2119.6 us)
Sparse Core Ops, SparseCore 0:
  10.9 62.3 all-gather.7
  236.7 53.3 all-gather.5
  1068.7 151.6 all-reduce.29
  1227.0 104.1 reduce-scatter.9
where the time goes:
time: 1510 us; the launch traced here: 1490 us
  blocking collectives  583 us (39%)
  local copies, waits for them, and re-layouts  302 us (20%)
  matrix products  287 us (19%)
  other arithmetic  218 us (14%)
  starting transfers between devices  82.6 us (5%)
  between operations  15.8 us (1%)
    unnamed x1, blocking collectives  232 us
    all_gather x1, blocking collectives, shards(): lax.all_gather(qkv_weight, ('dp', 'band'), axis=0, tiled=True)  79.9 us
    all_gather x1, blocking collectives, shards(): lax.all_gather(norm1_map, ('dp', 'band'), axis=0, tiled=True)  76.3 us
    dynamic_update_slice x9, local copies, waits for them, and re-layouts, shards(): lax.map(attend_back, (query_blocks, keys_win, values_win, d_attended_bloc...  75.6 us
    unnamed x25, starting transfers between devices  72.3 us
    all_gather x1, blocking collectives, shards(): lax.all_gather(out_weight, ('dp', 'band'), axis=0, tiled=True)  69.2 us
    all_gather x1, blocking collectives, shards(): lax.all_gather(norm2_map, ('dp', 'band'), axis=0, tiled=True)  68.9 us
    dot_general x1, matrix products, shards(): jnp.einsum('itd,fd->itf', loss_seed_low, w_down, preferred_element_type=j...  52.4 us
  transfers between devices with their start and end apart: 32, of which 2 were waited for; matrix products, arithmetic and copies ran while one was open for 38% of the time, Pallas kernels for 0%

commit v1 on v0

v1 whole, which is shorter than its diff:
```python
import functools
import math

import jax
import jax.numpy as jnp
import numpy as np
from jax import lax
from jax.experimental import pallas as pl
from jax.experimental.pallas import tpu as pltpu
from jax.sharding import PartitionSpec as P

KERNEL = 7
RADIUS = KERNEL // 2
NORM_EPS = 1e-06
MASKED = -10000.0
F32 = jnp.float32
BF16 = jnp.bfloat16
VMEM_LIMIT = 60 << 20


def nn(a, b):
    return lax.dot_general(a, b, (((1,), (0,)), ((), ())), preferred_element_type=F32)


def nt(a, b):
    return lax.dot_general(a, b, (((1,), (1,)), ((), ())), preferred_element_type=F32)


def tn(a, b):
    return lax.dot_general(a, b, (((0,), (0,)), ((), ())), preferred_element_type=F32)


def lanes(shape):
    return lax.broadcasted_iota(jnp.int32, shape, len(shape) - 1)


def halves(value):
    high = value.astype(BF16)
    low = (value - high.astype(F32)).astype(BF16)
    return high, low


def thirds(value):
    high = value.astype(BF16)
    rest = value - high.astype(F32)
    middle = rest.astype(BF16)
    return high.astype(F32), middle.astype(F32), rest - middle.astype(F32)


def head_sums(value, pool):
    high, low = halves(value)
    return nn(jnp.concatenate([high, low], axis=1), pool)


def swapped(value):
    first = (lanes(value.shape) & 8) == 0
    return jnp.where(first, pltpu.roll(value, 120, 1), pltpu.roll(value, 8, 1))


def normed_rows(values, scale):
    inverse = lax.rsqrt(jnp.mean(values * values, axis=-1, keepdims=True) + NORM_EPS)
    return values * scale * inverse, inverse


def build_turns(crow, srow, ccol, scol, cos_s, sin_s):
    rows, width = crow.shape[0], ccol.shape[0]
    cos_s[...] = (crow[...][:, None, :] * ccol[...][None]).reshape(rows * width, 128)
    sin_s[...] = (srow[...][:, None, :] + scol[...][None]).reshape(rows * width, 128)


def build_key_features(first_row, height, width, feat_s):
    groups, keys, _ = feat_s.shape
    lane = lanes((keys, 128))
    index = lax.broadcasted_iota(jnp.int32, (keys, 128), 0)
    row = index // width
    col = index - row * width
    far = jnp.where(jnp.abs(col - lane) <= RADIUS, 0.0, MASKED)
    base = jnp.where(lane < width, far, 0.0)
    base = jnp.where((lane == width) & (row > 2 * RADIUS), MASKED, base)
    base = jnp.where((lane == width + 1) & (row < 1), MASKED, base)
    base = jnp.where((lane >= 96) & (lane < 96 + 3 * 8), 1.0, base)
    row_lane = (lane >= width) & (lane < width + 2)
    for group in range(groups):
        place = first_row + 2 * group - RADIUS + row
        outside = (place < 0) | (place >= height)
        feat_s[group] = jnp.where(row_lane & outside, MASKED, base).astype(BF16)


def query_features(width):
    shape = (2 * width, 128)
    lane = lanes(shape)
    index = lax.broadcasted_iota(jnp.int32, shape, 0)
    row = index // width
    col = index - row * width
    hit = ((lane < width) & (lane == col)) | ((lane >= width) & (lane - width == row))
    return jnp.where(hit, 1.0, 0.0)


def block_diagonal(tile):
    low = lanes(tile.shape) < 64
    zero = jnp.zeros_like(tile)
    return jnp.concatenate([jnp.where(low, tile, zero), jnp.where(low, zero, tile)], axis=0)


MESH = pl.DeviceIdType.MESH


def flip(index, bit):
    return index + bit * (1 - 2 * ((index // bit) % 2))


def relatives(index, bits):
    found = [index]
    for bit in bits:
        found = found + [flip(i, bit) for i in found]
    return found


class Copies:
    def __init__(self, send, recv):
        self.send, self.recv, self.count = send, recv, 0

    def __call__(self, source, target, peer):
        slot = self.count
        self.count += 1
        return pltpu.make_async_remote_copy(
            src_ref=source,
            dst_ref=target,
            send_sem=self.send.at[slot],
            recv_sem=self.recv.at[slot],
            device_id=peer,
            device_id_type=MESH,
        )


def start(copies):
    for copy in copies:
        copy.start()


def arrive(copies):
    for copy in copies:
        copy.wait_recv()


def depart(copies):
    for copy in copies:
        copy.wait_send()


def greet(peers):
    barrier = pltpu.get_barrier_semaphore()
    for peer in peers:
        pl.semaphore_signal(barrier, inc=1, device_id=peer, device_id_type=MESH)
    pl.semaphore_wait(barrier, len(peers))


def place(devices):
    dp, band = lax.axis_index("dp"), lax.axis_index("band")
    bits = [1 << i for i in range(devices.bit_length() - 1)]
    return dp, band, bits


def ways(bits):
    far = bits[1:]
    return (far[::-1], far)


def gather_steps(devices, copy, local, shards, pairs, blocks, outs, splits):
    dp, band, bits = place(devices)
    high = band // 2
    core = (flip(dp, 1), band)
    n = len(shards)
    done = {"sent": []}

    def begin():
        done["near"] = [copy(shards[a], pairs[a], (dp, flip(band, 1))) for a in range(n)]
        start(done["near"])

    def pair():
        arrive(done["near"])
        odd = (band % 2) == 1
        for a in range(n):
            own, other = shards[a][...], pairs[a][...]
            rows = own.shape[0]
            blocks[a][:rows] = jnp.where(odd, other, own)
            blocks[a][rows:] = jnp.where(odd, own, other)
        done["own"] = [
            pltpu.make_async_copy(blocks[a], outs[a].at[dp, high], local.at[a]) for a in range(n)
        ]
        done["far"] = [
            copy(blocks[a], outs[a].at[dp, high], (dp, flip(band, 2))) for a in range(n)
        ]
        done["core"] = [copy(blocks[a], outs[a].at[dp, high], core) for a in range(n)]
        start(done["own"] + done["far"] + done["core"])
        done["sent"] += done["near"] + done["far"]

    def spread(k):
        def step():
            if k == 0:
                for own in done["own"]:
                    own.wait()
                arrive(done["far"])
                fresh = [copy(outs[a].at[dp, 1 - high], outs[a].at[dp, 1 - high], core) for a in range(n)]
            else:
                fresh = []
                arrive(done["ring"])
                for way, bit_order in enumerate(ways(bits)):
                    for index in relatives(flip(dp, bit_order[k - 1]), bit_order[: k - 1]):
                        for a in range(n):
                            cut = outs[a].at[index, :, :, pl.ds(*splits[a][way])]
                            fresh.append(copy(cut, cut, core))
            start(fresh)
            done["core"] += fresh
            if k == len(bits) - 1:
                return
            done["ring"] = []
            for way, bit_order in enumerate(ways(bits)):
                peer = (flip(dp, bit_order[k]), band)
                for index in relatives(dp, bit_order[:k]):
                    for a in range(n):
                        cut = outs[a].at[index, :, :, pl.ds(*splits[a][way])]
                        done["ring"].append(copy(cut, cut, peer))
            start(done["ring"])
            done["sent"] += done["ring"]

        return step

    def finish():
        arrive(done["core"])
        depart(done["sent"] + done["core"])

    return [begin, pair] + [spread(k) for k in range(len(bits))] + [finish]


def gather_copies(devices, n):
    count = n * 3
    bits = devices.bit_length() - 1
    for k in range(bits):
        count += n if k == 0 else 2 * n * (1 << (k - 1))
        if k < bits - 1:
            count += 2 * n * (1 << k)
    return count


def exchange_peers(devices):
    dp, band, bits = place(devices)
    return [(dp, flip(band, 1)), (dp, flip(band, 2))] + [(flip(dp, bit), band) for bit in bits]


def column_split(columns, first):
    return ((0, first), (first, columns - first))


def fetch_kernel(devices, splits, *refs):
    n = len(splits)
    shards, outs = refs[:n], refs[n : 2 * n]
    pairs, blocks = refs[2 * n : 3 * n], refs[3 * n : 4 * n]
    send, recv, local = refs[4 * n :]
    greet(exchange_peers(devices))
    for step in gather_steps(devices, Copies(send, recv), local, shards, pairs, blocks, outs, splits):
        step()


def fetch(devices, shards, firsts, collective):
    splits = [column_split(s.shape[1], first) for s, first in zip(shards, firsts)]
    count = gather_copies(devices, len(shards))
    outs = pl.pallas_call(
        functools.partial(fetch_kernel, devices, splits),
        out_shape=[
            jax.ShapeDtypeStruct((devices, 2, 2 * s.shape[0], s.shape[1]), s.dtype) for s in shards
        ],
        in_specs=[pl.BlockSpec(memory_space=pltpu.VMEM)] * len(shards),
        out_specs=[pl.BlockSpec(memory_space=pl.ANY)] * len(shards),
        scratch_shapes=[
            *[pltpu.VMEM(s.shape, s.dtype) for s in shards],
            *[pltpu.VMEM((2 * s.shape[0], s.shape[1]), s.dtype) for s in shards],
            pltpu.SemaphoreType.DMA((count,)),
            pltpu.SemaphoreType.DMA((count,)),
            pltpu.SemaphoreType.DMA((len(shards),)),
        ],
        compiler_params=pltpu.CompilerParams(
            collective_id=collective, has_side_effects=True, vmem_limit_bytes=VMEM_LIMIT
        ),
        name="fetch",
    )(*shards)
    return [o.reshape(-1, o.shape[-1]) for o in outs]


def add_into(target, index, cut, addend):
    start_col, width = cut
    columns = pl.ds(start_col, width)
    for half in range(2):
        total = target[index, half, :, columns].astype(F32) + addend(half)
        target[index, half, :, columns] = total.astype(BF16)


def scatter_steps(devices, copy, grads, inbox, near, far, outs, splits):
    dp, band, bits = place(devices)
    high = band // 2
    n = len(grads)
    done = {"sent": []}

    def send_core():
        done["in"] = []
        peer = flip(dp, 1)
        for k, index in enumerate(relatives(peer, bits[1:])):
            for a in range(n):
                done["in"].append(copy(grads[a].at[index], inbox[a].at[k], (peer, band)))
        start(done["in"])
        done["sent"] += done["in"]

    def add_core():
        arrive(done["in"])
        for k, index in enumerate(relatives(dp, bits[1:])):
            for a in range(n):
                whole = (0, splits[a][0][1] + splits[a][1][1])
                add_into(grads[a], index, whole, lambda half: inbox[a][k, half].astype(F32))

    base = 1 << (len(bits) - 1)

    def spot(k):
        return base + sum(1 << (len(bits) - 2 - j) for j in range(k))

    def send_far(k):
        done["in"] = []
        for way, order in enumerate(ways(bits)):
            bit = order[k]
            peer = flip(dp, bit)
            for j, index in enumerate(relatives(peer, order[k + 1 :])):
                for a in range(n):
                    cols = pl.ds(*splits[a][way])
                    done["in"].append(
                        copy(grads[a].at[index, :, :, cols], inbox[a].at[spot(k) + j, :, :, cols], (peer, band))
                    )
        start(done["in"])
        done["sent"] += done["in"]

    def add_far(k):
        arrive(done["in"])
        for way, order in enumerate(ways(bits)):
            for j, index in enumerate(relatives(dp, order[k + 1 :])):
                for a in range(n):
                    cols = pl.ds(*splits[a][way])
                    add_into(
                        grads[a], index, splits[a][way],
                        lambda half: inbox[a][spot(k) + j, half, :, cols].astype(F32),
                    )

    def send_band():
        done["in"] = [
            copy(grads[a].at[dp, 1 - high], far[a], (dp, flip(band, 2))) for a in range(n)
        ]
        start(done["in"])
        done["sent"] += done["in"]

    def send_near():
        arrive(done["in"])
        odd = (band % 2) == 1
        done["in"] = []
        for a in range(n):
            total = grads[a][dp, high].astype(F32) + far[a][...].astype(F32)
            rows = total.shape[0] // 2
            low, top = total[:rows], total[rows:]
            outs[a][...] = jnp.where(odd, top, low)
            near[a][0] = jnp.where(odd, low, top).astype(BF16)
            done["in"].append(copy(near[a].at[0], near[a].at[1], (dp, flip(band, 1))))
        start(done["in"])
        done["sent"] += done["in"]

    def finish():
        arrive(done["in"])
        for a in range(n):
            outs[a][...] += near[a][1].astype(F32)
        depart(done["sent"])

    def chain(*steps):
        def run():
            for step in steps:
                step()

        return run

    steps = [send_core, chain(add_core, functools.partial(send_far, 0))]
    for k in range(len(bits) - 1):
        following = functools.partial(send_far, k + 1) if k + 1 < len(bits) - 1 else send_band
        steps.append(chain(functools.partial(add_far, k), following))
    return steps + [send_near, finish]


def scatter_copies(devices, n):
    bits = devices.bit_length() - 1
    count = n * (1 << (bits - 1))
    for k in range(bits - 1):
        count += 2 * n * (1 << (bits - 2 - k))
    return count + 2 * n


def scatter_scratch(devices, shapes):
    slots = devices
    scratch = [pltpu.VMEM((slots, 2, s[2], s[3]), BF16) for s in shapes]
    scratch += [pltpu.VMEM((2, s[2] // 2, s[3]), BF16) for s in shapes]
    scratch += [pltpu.VMEM((s[2], s[3]), BF16) for s in shapes]
    return scratch


def settle_kernel(devices, splits, *refs):
    n = len(splits)
    grads_hbm, outs = refs[:n], refs[n : 2 * n]
    grads, inbox, near, far = (refs[(2 + i) * n : (3 + i) * n] for i in range(4))
    send, recv, local = refs[6 * n :]
    loads = [pltpu.make_async_copy(grads_hbm[a], grads[a], local.at[a]) for a in range(n)]
    start(loads)
    greet(exchange_peers(devices))
    for load in loads:
        load.wait()
    for step in scatter_steps(devices, Copies(send, recv), grads, inbox, near, far, outs, splits):
        step()


def settle(devices, grads, firsts, collective):
    splits = [column_split(g.shape[1], first) for g, first in zip(grads, firsts)]
    shapes = [(devices, 2, g.shape[0] // (2 * devices), g.shape[1]) for g in grads]
    count = scatter_copies(devices, len(grads))
    return pl.pallas_call(
        functools.partial(settle_kernel, devices, splits),
        out_shape=[jax.ShapeDtypeStruct((s[2] // 2, s[3]), F32) for s in shapes],
        in_specs=[pl.BlockSpec(memory_space=pl.ANY)] * len(grads),
        out_specs=[pl.BlockSpec(memory_space=pltpu.VMEM)] * len(grads),
        scratch_shapes=[
            *[pltpu.VMEM(s, BF16) for s in shapes],
            *scatter_scratch(devices, shapes),
            pltpu.SemaphoreType.DMA((count,)),
            pltpu.SemaphoreType.DMA((count,)),
            pltpu.SemaphoreType.DMA((len(grads),)),
        ],
        compiler_params=pltpu.CompilerParams(
            collective_id=collective, has_side_effects=True, vmem_limit_bytes=VMEM_LIMIT
        ),
        name="settle",
    )(*[g.reshape(s) for g, s in zip(grads, shapes)])


def open_kernel(
    devices, bands, splits, images,
    qkv, cond, maps, tokens,
    w_qkv, scales, chosen, top, bottom,
    pair, block, conds, padded, partial, part_in, band_in,
    send, recv, local, halo_send, halo_recv,
):
    dp, band, _ = place(devices)
    rows = maps.shape[0]
    copy = Copies(send, recv)
    around = [((dp + d) % devices, band) for d in range(1, devices)]
    along = [(dp, (band + d) % bands) for d in range(1, bands)]
    edge = top.shape[1]
    tall = tokens.shape[1]
    greet(around + along)
    steps = gather_steps(devices, copy, local, [qkv], [pair], [block], [w_qkv], splits)

    up = pltpu.make_async_remote_copy(
        src_ref=tokens.at[:, pl.ds(tall - edge, edge)], dst_ref=top,
        send_sem=halo_send.at[0], recv_sem=halo_recv.at[0],
        device_id=(dp, (band + 1) % bands), device_id_type=MESH,
    )
    down = pltpu.make_async_remote_copy(
        src_ref=tokens.at[:, pl.ds(0, edge)], dst_ref=bottom,
        send_sem=halo_send.at[1], recv_sem=halo_recv.at[1],
        device_id=(dp, (band + bands - 1) % bands), device_id_type=MESH,
    )
    fill_top = pltpu.make_async_copy(tokens.at[:, pl.ds(0, edge)], top, local.at[1])
    fill_bottom = pltpu.make_async_copy(tokens.at[:, pl.ds(0, edge)], bottom, local.at[1])

    steps[0]()
    conds[dp] = cond[...]
    first = [copy(cond, conds.at[dp], peer) for peer in around]
    start(first)
    padded[...] = jnp.zeros_like(padded)
    padded[:rows] = maps[...]
    steps[1]()

    arrive(first)
    offset = (dp * bands + band) * rows
    lane = lanes((conds.shape[2], 128))
    hit = (lax.broadcasted_iota(jnp.int32, lane.shape, 0) == lane + offset) & (lane < rows)
    picked = nn(conds[...].reshape(-1, conds.shape[2]), jnp.where(hit, 1.0, 0.0).astype(BF16)).astype(BF16)
    chosen[...] = picked
    partial[...] = nn(picked, padded[...]).reshape(partial.shape)
    second = [copy(partial.at[peer[0]], part_in.at[dp], peer) for peer in around]
    start(second)
    steps[2]()

    @pl.when(band < bands - 1)
    def _():
        up.start()

    @pl.when(band > 0)
    def _():
        down.start()

    @pl.when(band == 0)
    def _():
        fill_top.start()

    @pl.when(band == bands - 1)
    def _():
        fill_bottom.start()

    arrive(second)
    total = partial[dp]
    for peer in around:
        total = total + part_in[peer[0]]
    band_in[band] = total
    third = [copy(band_in.at[band], band_in.at[band], peer) for peer in along]
    start(third)
    for step in steps[3:-1]:
        step()
    arrive(third)
    total = band_in[0]
    for b in range(1, bands):
        total = total + band_in[b]
    scales[...] = 1.0 + total
    steps[-1]()
    depart(first + second + third)

    @pl.when(band < bands - 1)
    def _():
        up.wait_send()
        down.wait_recv()

    @pl.when(band > 0)
    def _():
        down.wait_send()
        up.wait_recv()

    @pl.when(band == 0)
    def _():
        fill_top.wait()

    @pl.when(band == bands - 1)
    def _():
        fill_bottom.wait()


def open_layer(devices, bands, qkv, cond, maps, tokens, first, collective):
    images = cond.shape[0]
    cond = jnp.pad(cond, ((0, 8 - images), (0, 0)))
    wide, both = cond.shape[1], maps.shape[1]
    count = gather_copies(devices, 1) + 2 * (devices - 1) + bands - 1
    rows, columns = qkv.shape
    halo = jax.ShapeDtypeStruct((images, RADIUS) + tokens.shape[2:], tokens.dtype)
    vmem, hbm = pl.BlockSpec(memory_space=pltpu.VMEM), pl.BlockSpec(memory_space=pl.ANY)
    w_qkv, scales, chosen, top, bottom = pl.pallas_call(
        functools.partial(open_kernel, devices, bands, [column_split(columns, first)], images),
        out_shape=[
            jax.ShapeDtypeStruct((devices, 2, 2 * rows, columns), BF16),
            jax.ShapeDtypeStruct((8, both), F32),
            jax.ShapeDtypeStruct((devices * 8, 128), BF16),
            halo, halo,
        ],
        in_specs=[vmem, vmem, vmem, hbm],
        out_specs=[hbm, vmem, vmem, hbm, hbm],
        scratch_shapes=[
            pltpu.VMEM((rows, columns), BF16),
            pltpu.VMEM((2 * rows, columns), BF16),
            pltpu.VMEM((devices, 8, wide), BF16),
            pltpu.VMEM((128, both), BF16),
            pltpu.VMEM((devices, 8, both), F32),
            pltpu.VMEM((devices, 8, both), F32),
            pltpu.VMEM((bands, 8, both), F32),
            pltpu.SemaphoreType.DMA((count,)),
            pltpu.SemaphoreType.DMA((count,)),
            pltpu.SemaphoreType.DMA((2,)),
            pltpu.SemaphoreType.DMA((2,)),
            pltpu.SemaphoreType.DMA((2,)),
        ],
        compiler_params=pltpu.CompilerParams(
            collective_id=collective, has_side_effects=True, vmem_limit_bytes=VMEM_LIMIT
        ),
        name="open_layer",
    )(qkv, cond, maps, tokens)
    return w_qkv.reshape(-1, columns), scales, chosen, top, bottom


def close_kernel(
    devices, bands, splits, images,
    grad, sums, chosen, maps,
    out, grad_maps, grad_cond, grad_heads,
    acc, inbox, near, far, band_in, all_in,
    send, recv, local,
):
    dp, band, _ = place(devices)
    copy = Copies(send, recv)
    around = [((dp + d) % devices, band) for d in range(1, devices)]
    along = [(dp, (band + d) % bands) for d in range(1, bands)]
    load = pltpu.make_async_copy(grad, acc, local.at[0])
    load.start()
    greet(around + along)
    first = [copy(sums, band_in.at[band], peer) for peer in along]
    start(first)
    band_in[band] = sums[...]
    load.wait()
    steps = scatter_steps(devices, copy, [acc], [inbox], [near], [far], [out], splits)
    steps[0]()
    arrive(first)
    total = band_in[0]
    for b in range(1, bands):
        total = total + band_in[b]
    all_in[dp] = total
    second = [copy(all_in.at[dp], all_in.at[dp], peer) for peer in around]
    start(second)
    steps[1]()
    parts = [part.astype(BF16) for part in thirds(total)]
    grad_cond[...] = sum(nt(part, maps[...]) for part in parts)
    steps[2]()
    arrive(second)
    whole = all_in[...]
    heads = whole[0]
    for d in range(1, devices):
        heads = heads + whole[d]
    grad_heads[...] = heads
    whole = whole.reshape(-1, whole.shape[-1])
    rows = grad_maps.shape[0]
    grad_maps[...] = sum(tn(chosen[...], part.astype(BF16)) for part in thirds(whole))[:rows]
    for step in steps[3:]:
        step()
    depart(first + second)


def close_layer(devices, bands, grad, sums, chosen, maps, images, first, collective):
    columns = grad.shape[1]
    shape = (devices, 2, grad.shape[0] // (2 * devices), columns)
    both = sums.shape[1]
    map_rows = maps.shape[0] // (devices * bands)
    count = scatter_copies(devices, 1) + devices - 1 + bands - 1
    vmem, hbm = pl.BlockSpec(memory_space=pltpu.VMEM), pl.BlockSpec(memory_space=pl.ANY)
    return pl.pallas_call(
        functools.partial(close_kernel, devices, bands, [column_split(columns, first)], images),
        out_shape=[
            jax.ShapeDtypeStruct((shape[2] // 2, columns), F32),
            jax.ShapeDtypeStruct((map_rows, both), F32),
            jax.ShapeDtypeStruct((8, maps.shape[0]), F32),
            jax.ShapeDtypeStruct((8, both), F32),
        ],
        in_specs=[hbm, vmem, vmem, vmem],
        out_specs=[vmem] * 4,
        scratch_shapes=[
            pltpu.VMEM(shape, BF16),
            *scatter_scratch(devices, [shape]),
            pltpu.VMEM((bands, 8, both), F32),
            pltpu.VMEM((devices, 8, both), F32),
            pltpu.SemaphoreType.DMA((count,)),
            pltpu.SemaphoreType.DMA((count,)),
            pltpu.SemaphoreType.DMA((1,)),
        ],
        compiler_params=pltpu.CompilerParams(
            collective_id=collective, has_side_effects=True, vmem_limit_bytes=VMEM_LIMIT
        ),
        name="close_layer",
    )(grad.reshape(shape), sums, chosen, maps)


def attend_kernel(
    height, width, first, x, top, bottom, scale, w_qkv, factor, pool, crow, srow, ccol, scol,
    att, q_out, k_out, v_out, inverse_out, log_out,
    cos_s, sin_s, feat_s,
):
    dim = x.shape[-1]
    pairs = dim // 128
    tokens = x.shape[1]
    border = top.shape[1]
    block = 2 * width
    keys = feat_s.shape[1]

    @pl.when(pl.program_id(0) == 0)
    def _():
        build_turns(crow, srow, ccol, scol, cos_s, sin_s)
        build_key_features(first[0], height, width, feat_s)

    row_scale = scale[0]
    part = (lanes((1, 128)) & 63).astype(F32)

    def shaped(raw, p, cos, sin):
        fr = factor[:, p * 128 : (p + 1) * 128] * lax.rsqrt(head_sums(raw * raw, pool[...]) + NORM_EPS)
        unit = raw * fr
        return unit * cos + swapped(unit) * sin, fr

    def halo(ref, start):
        normed, _ = normed_rows(ref[0].astype(F32), row_scale)
        mixed = nn(normed.astype(BF16), w_qkv[:, dim:])
        place = pl.ds(start, border)
        cos, sin = cos_s[place], sin_s[place]
        for p in range(pairs):
            cut = slice(p * 128, (p + 1) * 128)
            turned, _ = shaped(mixed[:, cut], p, cos, sin)
            k_out[0, place, cut] = turned.astype(BF16)
            v_out[0, place, cut] = mixed[:, dim + p * 128 : dim + (p + 1) * 128].astype(BF16)

    halo(top, 0)
    halo(bottom, border + tokens)

    chunk = 256

    def project(i, _):
        own = pl.ds(pl.multiple_of(i * chunk, chunk), chunk)
        place = pl.ds(pl.multiple_of(border + i * chunk, 64), chunk)
        normed, _ = normed_rows(x[0, own].astype(F32), row_scale)
        mixed = nn(normed.astype(BF16), w_qkv[...])
        cos, sin = cos_s[place], sin_s[place]
        kept = jnp.zeros((chunk, 128), F32)
        for p in range(pairs):
            cut = slice(p * 128, (p + 1) * 128)
            turned, fr = shaped(mixed[:, cut], p, cos, sin)
            q_out[0, own, cut] = turned.astype(BF16)
            kept = jnp.where(part == 2 * p, fr, kept)
            turned, fr = shaped(mixed[:, dim + p * 128 : dim + (p + 1) * 128], p, cos, sin)
            k_out[0, place, cut] = turned.astype(BF16)
            kept = jnp.where(part == 2 * p + 1, fr, kept)
            v_out[0, place, cut] = mixed[:, 2 * dim + p * 128 : 2 * dim + (p + 1) * 128].astype(BF16)
        inverse_out[0, own] = kept
        return 0

    lax.fori_loop(0, tokens // chunk, project, 0)

    ask = query_features(width).astype(BF16)
    ask = jnp.concatenate([ask, ask], axis=0)
    ones = jnp.ones((keys, 128), BF16)
    lane = lanes((block, 128))

    def attend(g, _):
        own = pl.ds(pl.multiple_of(g * block, block), block)
        window = pl.ds(pl.multiple_of(g * block, block), keys)
        feats = feat_s[g]
        logs = jnp.zeros((block, 128), F32)
        for p in range(pairs):
            cut = slice(p * 128, (p + 1) * 128)
            query = jnp.concatenate([block_diagonal(q_out[0, own, cut]), ask], axis=1)
            key = jnp.concatenate([k_out[0, window, cut], feats], axis=1)
            weight = jnp.exp(nt(query, key)).astype(BF16)
            value = jnp.concatenate([v_out[0, window, cut], ones], axis=1)
            both = nn(weight, value)
            total = both[:, 128:]
            mean = both[:, :128] / total
            att[0, own, cut] = jnp.where(lane < 64, mean[:block], mean[block:]).astype(BF16)
            for h in range(2):
                kept = thirds(-jnp.log(total[h * block : (h + 1) * block]))
                for t in range(3):
                    logs = jnp.where(lane == 96 + 3 * (2 * p + h) + t, kept[t], logs)
        log_out[0, own] = logs.astype(BF16)
        return 0

    lax.fori_loop(0, tokens // block, attend, 0)


def attend_forward(first, x, top, bottom, scale, w_qkv, factor, pool, turns, height, width):
    images, tokens, dim = x.shape
    border = top.shape[1]
    extended = tokens + 2 * border
    block = 2 * width
    keys = (2 * RADIUS + 2) * width
    image = lambda rows, cols: pl.BlockSpec((1, rows, cols), lambda i: (i, 0, 0))
    whole = lambda a: pl.BlockSpec(a.shape, lambda i: (0,) * a.ndim)
    return pl.pallas_call(
        functools.partial(attend_kernel, height, width),
        grid=(images,),
        in_specs=[
            pl.BlockSpec(memory_space=pltpu.SMEM),
            image(tokens, dim), image(border, dim), image(border, dim), image(1, dim),
            whole(w_qkv), whole(factor), whole(pool), *[whole(t) for t in turns],
        ],
        out_specs=[
            image(tokens, dim), image(tokens, dim), image(extended, dim), image(extended, dim),
            image(tokens, 128), image(tokens, 128),
        ],
        out_shape=[
            jax.ShapeDtypeStruct((images, tokens, dim), BF16),
            jax.ShapeDtypeStruct((images, tokens, dim), BF16),
            jax.ShapeDtypeStruct((images, extended, dim), BF16),
            jax.ShapeDtypeStruct((images, extended, dim), BF16),
            jax.ShapeDtypeStruct((images, tokens, 128), F32),
            jax.ShapeDtypeStruct((images, tokens, 128), BF16),
        ],
        scratch_shapes=[
            pltpu.VMEM((extended, 128), F32),
            pltpu.VMEM((extended, 128), F32),
            pltpu.VMEM((tokens // block, keys, 128), BF16),
        ],
        compiler_params=pltpu.CompilerParams(vmem_limit_bytes=VMEM_LIMIT),
        name="attend_forward",
    )(first, x, top, bottom, scale, w_qkv, factor, pool, *turns)


def gaussian_parts(gate):
    z = jnp.abs(gate) * math.sqrt(0.5)
    bell = jnp.exp(-z * z)
    t = 1.0 / (1.0 + 0.3275911 * z)
    tail = (((1.061405429 * t - 1.453152027) * t + 1.421413741) * t - 0.284496736) * t + 0.254829592
    tail = 0.5 * tail * t * bell
    return jnp.where(gate < 0, tail, 1.0 - tail), bell * (1.0 / math.sqrt(2.0 * math.pi))


def feed_kernel(
    x, att, cot, weight, scale, w_out, w_up, w_down, spread,
    result, d_residual, d_att, delta_out, grad_up_out, grad_down_out, d_scale,
    grad_up, grad_down_t, grad_out,
):
    step = pl.program_id(0) * pl.num_programs(1) + pl.program_id(1)
    last = pl.num_programs(0) * pl.num_programs(1) - 1
    hidden_units = w_down.shape[0]
    chunk = 512

    @pl.when(step == 0)
    def _():
        grad_up[...] = jnp.zeros_like(grad_up)
        grad_down_t[...] = jnp.zeros_like(grad_down_t)
        grad_out[...] = jnp.zeros_like(grad_out)

    @pl.when(pl.program_id(1) == 0)
    def _():
        d_scale[...] = jnp.zeros_like(d_scale)

    row_scale = scale[0]
    att_low = att[0]
    residual = x[0].astype(F32) + nn(att_low, w_out[...])
    normed, inverse = normed_rows(residual, row_scale)
    normed_low = normed.astype(BF16)
    seed = cot[0].astype(F32) * weight[0]
    seed_low = seed.astype(BF16)
    total = residual
    d_normed = jnp.zeros_like(residual)
    for c in range(hidden_units // chunk):
        low = slice(c * chunk, (c + 1) * chunk)
        high = slice(hidden_units + c * chunk, hidden_units + (c + 1) * chunk)
        value = nn(normed_low, w_up[:, low])
        gate = nn(normed_low, w_up[:, high])
        area, bell = gaussian_parts(gate)
        gelu = gate * area
        hidden = (value * gelu).astype(BF16)
        total = total + nn(hidden, w_down[low])
        d_hidden = nt(seed_low, w_down[low])
        d_value = (d_hidden * gelu).astype(BF16)
        d_gate = (d_hidden * value * (area + gate * bell)).astype(BF16)
        grad_down_t[:, low] += tn(seed_low, hidden)
        grad_up[:, low] += tn(normed_low, d_value)
        grad_up[:, high] += tn(normed_low, d_gate)
        d_normed = d_normed + nt(d_value, w_up[:, low]) + nt(d_gate, w_up[:, high])
    result[0] = total.astype(BF16)
    pull = d_normed * residual
    d_scale[0] += jnp.sum(pull * inverse, axis=0, keepdims=True)
    along = jnp.mean(pull * row_scale, axis=-1, keepdims=True)
    back = seed + row_scale * inverse * d_normed - residual * (inverse * inverse * inverse * along)
    d_residual[0] = back
    back_low = back.astype(BF16)
    grad_out[...] += tn(att_low, back_low)
    d_att_low = nt(back_low, w_out[...]).astype(BF16)
    d_att[0] = d_att_low
    delta = -head_sums(d_att_low.astype(F32) * att_low.astype(F32), spread[...])
    kept = thirds(delta)
    third = lax.rem(lanes(delta.shape), 3)
    delta_out[0] = jnp.where(third == 0, kept[0], jnp.where(third == 1, kept[1], kept[2])).astype(BF16)

    @pl.when(step == last)
    def _():
        grad_up_out[:, : 2 * hidden_units] = grad_up[...].astype(BF16)
        grad_up_out[:, 2 * hidden_units :] = grad_out[...].astype(BF16)
        grad_down_out[...] = grad_down_t[...].T.astype(BF16)


def feed(x, att, cot, weight, scale, w_up_out, w_down, spread):
    images, tokens, dim = x.shape
    tile = min(512, tokens)
    hidden_units = w_down.shape[0]
    block = lambda cols: pl.BlockSpec((1, tile, cols), lambda i, j: (i, j, 0))
    row = lambda cols: pl.BlockSpec((1, 1, cols), lambda i, j: (i, 0, 0))
    whole = lambda a: pl.BlockSpec(a.shape, lambda i, j: (0,) * len(a.shape))
    shapes = [
        jax.ShapeDtypeStruct((images, tokens, dim), BF16),
        jax.ShapeDtypeStruct((images, tokens, dim), F32),
        jax.ShapeDtypeStruct((images, tokens, dim), BF16),
        jax.ShapeDtypeStruct((images, tokens, 128), BF16),
        jax.ShapeDtypeStruct(w_up_out.shape, BF16),
        jax.ShapeDtypeStruct((hidden_units, dim), BF16),
        jax.ShapeDtypeStruct((images, 1, dim), F32),
    ]
    last = 2 * hidden_units // dim
    return pl.pallas_call(
        feed_kernel,
        grid=(images, tokens // tile),
        in_specs=[
            block(dim), block(dim), block(dim), row(dim), row(dim),
            pl.BlockSpec((dim, dim), lambda i, j: (0, last)),
            pl.BlockSpec((dim, 2 * hidden_units), lambda i, j: (0, 0)),
            whole(w_down), whole(spread),
        ],
        out_specs=[
            block(dim), block(dim), block(dim), block(128),
            whole(shapes[4]), whole(shapes[5]), row(dim),
        ],
        out_shape=shapes,
        scratch_shapes=[
            pltpu.VMEM((dim, 2 * hidden_units), F32),
            pltpu.VMEM((dim, hidden_units), F32),
            pltpu.VMEM((dim, dim), F32),
        ],
        compiler_params=pltpu.CompilerParams(vmem_limit_bytes=VMEM_LIMIT),
        name="feed",
    )(x, att, cot, weight, scale, w_up_out, w_up_out, w_down, spread)


def attend_back_kernel(
    height, width, first, q, k, v, d_att, logs, deltas,
    d_q, d_k, d_v, d_top, d_bottom,
    feat_s, dk_s, dv_s,
):
    dim = q.shape[-1]
    pairs = dim // 128
    tokens = q.shape[1]
    border = d_top.shape[1]
    block = 2 * width
    keys = feat_s.shape[1]

    @pl.when(pl.program_id(0) == 0)
    def _():
        build_key_features(first[0], height, width, feat_s)

    dk_s[...] = jnp.zeros_like(dk_s)
    dv_s[...] = jnp.zeros_like(dv_s)
    lane = lanes((block, 128))
    ask = query_features(width)
    one_lanes = jnp.where(lanes((keys, 128)) < 3 * 2 * pairs, 1.0, 0.0).astype(BF16)

    def back(g, _):
        own = pl.ds(pl.multiple_of(g * block, block), block)
        window = pl.ds(pl.multiple_of(g * block, block), keys)
        feats = feat_s[g]
        log_tile = logs[0, own].astype(F32)
        delta_tile = deltas[0, own].astype(F32)
        for p in range(pairs):
            cut = slice(p * 128, (p + 1) * 128)
            asks, pulls = [], []
            for h in range(2):
                start = 3 * (2 * p + h)
                asks.append(jnp.where((lane >= 96 + start) & (lane < 99 + start), log_tile, ask))
                pulls.append(jnp.where((lane >= start) & (lane < start + 3), delta_tile, 0.0))
            query = block_diagonal(q[0, own, cut])
            pull = block_diagonal(d_att[0, own, cut])
            query_wide = jnp.concatenate([query, jnp.concatenate(asks, 0).astype(BF16)], axis=1)
            pull_wide = jnp.concatenate([pull, jnp.concatenate(pulls, 0).astype(BF16)], axis=1)
            key = k[0, window, cut]
            value = v[0, window, cut]
            probs = jnp.exp(nt(jnp.concatenate([key, feats], axis=1), query_wide))
            d_probs = nt(jnp.concatenate([value, one_lanes], axis=1), pull_wide)
            d_scores = (probs * d_probs).astype(BF16)
            dv_s[window, cut] += nn(probs.astype(BF16), pull)
            dk_s[window, cut] += nn(d_scores, query)
            turned = tn(key, d_scores)
            turned = jnp.concatenate([turned[:64, :block], turned[64:, block:]], axis=0)
            d_q[0, own, cut] = turned.T
        return 0

    lax.fori_loop(0, tokens // block, back, 0)
    d_k[0] = dk_s[border : border + tokens]
    d_v[0] = dv_s[border : border + tokens]
    d_top[0, :, :dim] = dk_s[:border].astype(BF16)
    d_top[0, :, dim:] = dv_s[:border].astype(BF16)
    d_bottom[0, :, :dim] = dk_s[border + tokens :].astype(BF16)
    d_bottom[0, :, dim:] = dv_s[border + tokens :].astype(BF16)


def attend_backward(first, q, k, v, d_att, logs, deltas, height, width):
    images, tokens, dim = q.shape
    extended = k.shape[1]
    border = (extended - tokens) // 2
    block = 2 * width
    keys = (2 * RADIUS + 2) * width
    image = lambda rows, cols: pl.BlockSpec((1, rows, cols), lambda i: (i, 0, 0))
    return pl.pallas_call(
        functools.partial(attend_back_kernel, height, width),
        grid=(images,),
        in_specs=[
            pl.BlockSpec(memory_space=pltpu.SMEM),
            image(tokens, dim), image(extended, dim), image(extended, dim), image(tokens, dim),
            image(tokens, 128), image(tokens, 128),
        ],
        out_specs=[
            image(tokens, dim), image(tokens, dim), image(tokens, dim),
            image(border, 2 * dim), image(border, 2 * dim),
        ],
        out_shape=[
            jax.ShapeDtypeStruct((images, tokens, dim), F32),
            jax.ShapeDtypeStruct((images, tokens, dim), F32),
            jax.ShapeDtypeStruct((images, tokens, dim), F32),
            jax.ShapeDtypeStruct((images, border, 2 * dim), BF16),
            jax.ShapeDtypeStruct((images, border, 2 * dim), BF16),
        ],
        scratch_shapes=[
            pltpu.VMEM((tokens // block, keys, 128), BF16),
            pltpu.VMEM((extended, dim), F32),
            pltpu.VMEM((extended, dim), F32),
        ],
        compiler_params=pltpu.CompilerParams(vmem_limit_bytes=VMEM_LIMIT),
        name="attend_backward",
    )(first, q, k, v, d_att, logs, deltas)


def project_back_kernel(
    x, scale, q, k, d_q, d_k, d_v, above, below, inverse_in, d_residual, w_qkv, inverse_scale,
    pool, expand, crow, srow, ccol, scol,
    grad_input, grad_qkv_out, d_scale, d_attn,
    cos_s, sin_s, grad_qkv,
):
    dim = x.shape[-1]
    pairs = dim // 128
    tokens = x.shape[1]
    border = above.shape[1]
    step = pl.program_id(0)
    chunk = 256
    parts = tokens // chunk

    @pl.when(step == 0)
    def _():
        build_turns(crow, srow, ccol, scol, cos_s, sin_s)
        grad_qkv[...] = jnp.zeros_like(grad_qkv)
        d_attn[...] = jnp.zeros_like(d_attn)

    d_scale[...] = jnp.zeros_like(d_scale)
    row_scale = scale[0]

    def with_borders(ref, c, cols, offset):
        own = slice(c * chunk, (c + 1) * chunk)
        values = ref[0, own, cols]
        wide = slice(cols.start + offset, cols.stop + offset)
        pieces = [values]
        if c == 0:
            extra = above[0, :, wide].astype(F32)
            pieces = [pieces[0][:border] + extra, pieces[0][border:]]
        if c == parts - 1:
            extra = below[0, :, wide].astype(F32)
            head = pieces[:-1]
            tail = pieces[-1]
            cut = tail.shape[0] - border
            pieces = head + [tail[:cut], tail[cut:] + extra]
        return jnp.concatenate(pieces, axis=0) if len(pieces) > 1 else values

    for c in range(parts):
        own = slice(c * chunk, (c + 1) * chunk)
        place = slice(border + c * chunk, border + (c + 1) * chunk)
        values = x[0, own].astype(F32)
        normed, inverse = normed_rows(values, row_scale)
        normed_low = normed.astype(BF16)
        high, low = halves(inverse_in[0, own])
        fr = nn(jnp.concatenate([high, low], axis=1), expand[...])
        cos, sin = cos_s[place], sin_s[place]
        columns = {}
        for p in range(pairs):
            cut = slice(p * 128, (p + 1) * 128)
            for kind in range(2):
                unit = (q[0, own, cut] if kind == 0 else k[0, place, cut]).astype(F32)
                grad = d_q[0, own, cut] if kind == 0 else with_borders(d_k, c, cut, 0)
                along = head_sums(unit * grad, pool[...]) * inverse_scale[:, cut]
                d_attn[:, cut] += jnp.sum(along, axis=0, keepdims=True)
                grad = grad - unit * along
                grad = grad * cos - swapped(grad) * sin
                spot = (2 * p + kind) * 128
                columns[kind * pairs + p] = (grad * fr[:, spot : spot + 128]).astype(BF16)
            columns[2 * pairs + p] = with_borders(d_v, c, cut, dim).astype(BF16)
        d_mixed = jnp.concatenate([columns[i] for i in range(3 * pairs)], axis=1)
        grad_qkv[...] += tn(normed_low, d_mixed)
        d_normed = nt(d_mixed, w_qkv[...])
        pull = d_normed * values
        d_scale[0] += jnp.sum(pull * inverse, axis=0, keepdims=True)
        along = jnp.mean(pull * row_scale, axis=-1, keepdims=True)
        back = row_scale * inverse * d_normed - values * (inverse * inverse * inverse * along)
        grad_input[0, own] = d_residual[0, own] + back

    @pl.when(step == pl.num_programs(0) - 1)
    def _():
        grad_qkv_out[...] = grad_qkv[...].astype(BF16)


def project_backward(
    x, scale, q, k, d_q, d_k, d_v, above, below, inverse, d_residual, w_qkv, inverse_scale,
    pool, expand, turns,
):
    images, tokens, dim = x.shape
    border = above.shape[1]
    extended = tokens + 2 * border
    image = lambda rows, cols: pl.BlockSpec((1, rows, cols), lambda i: (i, 0, 0))
    whole = lambda a: pl.BlockSpec(a.shape, lambda i: (0,) * len(a.shape))
    grad = jax.ShapeDtypeStruct(w_qkv.shape, BF16)
    attn = jax.ShapeDtypeStruct((1, dim), F32)
    return pl.pallas_call(
        project_back_kernel,
        grid=(images,),
        in_specs=[
            image(tokens, dim), image(1, dim), image(tokens, dim), image(extended, dim),
            image(tokens, dim), image(tokens, dim), image(tokens, dim),
            image(border, 2 * dim), image(border, 2 * dim), image(tokens, 128), image(tokens, dim),
            whole(w_qkv), whole(inverse_scale), whole(pool), whole(expand), *[whole(t) for t in turns],
        ],
        out_specs=[image(tokens, dim), whole(grad), image(1, dim), whole(attn)],
        out_shape=[
            jax.ShapeDtypeStruct((images, tokens, dim), F32),
            grad,
            jax.ShapeDtypeStruct((images, 1, dim), F32),
            attn,
        ],
        scratch_shapes=[
            pltpu.VMEM((extended, 128), F32),
            pltpu.VMEM((extended, 128), F32),
            pltpu.VMEM(w_qkv.shape, F32),
        ],
        compiler_params=pltpu.CompilerParams(vmem_limit_bytes=VMEM_LIMIT),
        name="project_backward",
    )(x, scale, q, k, d_q, d_k, d_v, above, below, inverse, d_residual, w_qkv, inverse_scale,
      pool, expand, *turns)


def turn_tables(height, width):
    freqs = math.pi * 10.0 ** (np.arange(8) / 7.0)

    def angles(count, extent):
        places = np.arange(count) - (RADIUS if count != extent else 0)
        return ((2.0 * places + 1.0) / extent - 1.0)[:, None] * freqs[None, :]

    def table(angle, start):
        cos = np.ones((angle.shape[0], 64))
        sin = np.zeros((angle.shape[0], 64))
        cos[:, start : start + 8] = np.cos(angle)
        cos[:, start + 8 : start + 16] = np.cos(angle)
        sin[:, start : start + 8] = -np.sin(angle)
        sin[:, start + 8 : start + 16] = np.sin(angle)
        return [np.tile(t, (1, 2)).astype(np.float32) for t in (cos, sin)]

    return table(angles(height + 2 * RADIUS, height), 0), table(angles(width, width), 16)


def constants(head_count):
    index = np.arange(256)
    pool = ((index[:, None] % 128) // 64 == np.arange(128)[None, :] // 64).astype(np.float32)
    dim = head_count * 64
    rows = np.arange(2 * dim)
    spread = ((rows[:, None] % dim) // 64 == np.arange(128)[None, :] // 3).astype(np.float32)
    pieces = np.arange(dim * 2)
    source = pieces // 128 + 64 * ((pieces % 128) // 64)
    expand = (index[:, None] % 128 == source[None, :]).astype(np.float32)
    return [jnp.asarray(t, BF16) for t in (pool, spread, expand)]


def shifted(x, by):
    devices = lax.axis_size("band")
    pairs = [(i, i + by) for i in range(devices) if 0 <= i + by < devices]
    return lax.ppermute(x, "band", pairs)


def shards(
    tokens_in, cond, loss_weight, cotangent, norm1_map, qkv_weight, attn_scale, out_weight,
    norm2_map, up_weight, down_weight,
):
    images, band_rows, width, dim = tokens_in.shape
    head_count = attn_scale.shape[0]
    head_size = dim // head_count
    tokens = band_rows * width
    band = lax.axis_index("band")
    height = band_rows * lax.axis_size("band")
    first = (band * band_rows).astype(jnp.int32).reshape(1)
    (row_cos, row_sin), (col_cos, col_sin) = turn_tables(height, width)
    extended_rows = band_rows + 2 * RADIUS
    turns = (
        lax.dynamic_slice_in_dim(jnp.asarray(row_cos), first[0], extended_rows, 0),
        lax.dynamic_slice_in_dim(jnp.asarray(row_sin), first[0], extended_rows, 0),
        jnp.asarray(col_cos),
        jnp.asarray(col_sin),
    )
    pool, spread, expand = constants(head_count)

    devices, bands = lax.axis_size("dp"), lax.axis_size("band")
    hidden_units = down_weight.shape[0] * devices * bands
    maps = jnp.concatenate([norm1_map, norm2_map], axis=1)
    w_qkv, scales, chosen, top, bottom = open_layer(
        devices, bands, qkv_weight, cond, maps, tokens_in, 640, 0
    )
    top = top.reshape(images, RADIUS * width, dim)
    bottom = bottom.reshape(images, RADIUS * width, dim)
    x = tokens_in.reshape(images, tokens, dim)
    scale_one = scales[:images, None, :dim]
    scale_two = scales[:images, None, dim:]
    w_up_out, w_down, map_rows = fetch(
        devices, [jnp.concatenate([up_weight, out_weight], axis=1), down_weight, maps], [1920, 128, 384], 1
    )
    factor = jnp.repeat(jnp.sqrt(attn_scale), head_size)[None, :]
    inverse_scale = jnp.repeat(1.0 / attn_scale, head_size)[None, :]

    att, q, k, v, inverse, logs = attend_forward(
        first, x, top, bottom, scale_one, w_qkv, factor, pool, turns, height, width
    )
    weight_rows = jnp.broadcast_to(loss_weight[:, None, None], (images, 1, dim))
    result, d_residual, d_att, deltas, grad_up_out, grad_down, d_scale_two = feed(
        x, att, cotangent.reshape(images, tokens, dim), weight_rows, scale_two, w_up_out, w_down, spread
    )
    grad_up_out, grad_down = settle(devices, [grad_up_out, grad_down], [1920, 128], 2)
    d_q, d_k, d_v, d_top, d_bottom = attend_backward(first, q, k, v, d_att, logs, deltas, height, width)
    below = shifted(d_top, -1)
    above = shifted(d_bottom, 1)
    grad_input, grad_qkv, d_scale_one, d_attn = project_backward(
        x, scale_one, q, k, d_q, d_k, d_v, above, below, inverse, d_residual, w_qkv, inverse_scale,
        pool, expand, turns,
    )
    sums = jnp.concatenate([d_scale_one[:, 0], d_scale_two[:, 0]], axis=1)
    sums = jnp.concatenate([sums, jnp.pad(d_attn, ((0, 7 - images), (0, dim)))], axis=0)
    grad_qkv, grad_maps, grad_cond, d_attn = close_layer(
        devices, bands, grad_qkv, sums, chosen, map_rows, images, 640, 3
    )
    d_heads = 0.5 * d_attn[images, :dim].reshape(head_count, head_size)[:, 0]
    return (
        result.reshape(tokens_in.shape),
        grad_input.reshape(tokens_in.shape),
        grad_cond[:images],
        grad_maps[:, :dim],
        grad_qkv,
        d_heads,
        grad_up_out[:, 2 * hidden_units :],
        grad_maps[:, dim:],
        grad_up_out[:, : 2 * hidden_units],
        grad_down,
    )


def solution(mesh):
    tokens = P("dp", "band", None, None)
    weights = P(("dp", "band"), None)
    return jax.shard_map(
        shards,
        mesh=mesh,
        in_specs=(tokens, P("dp", None), P("dp"), tokens, weights, weights, P(), *[weights] * 4),
        out_specs=(tokens, tokens, P("dp", None), weights, weights, P(), *[weights] * 4),
        check_vma=False,
    )
```

time: 1510 us -> 352 us (0.23)
  blocking collectives: 583 us -> 0 us
  Pallas kernels: 0 us -> 326 us
  matrix products: 287 us -> 0 us
  local copies, waits for them, and re-layouts: 302 us -> 19.4 us
  other arithmetic: 218 us -> 1.96 us
  starting transfers between devices: 82.6 us -> 2.64 us
    pallas_call x0 -> x8, Pallas kernels: none -> 326 us  [the longest x1 74.1 us: feed(): pl.pallas_call(feed_kernel, grid=(images, tokens // tile), in_specs=[bloc...]
    all_gather x4 -> x0, blocking collectives: 294 us -> none  [the longest x1 79.9 us: shards(): lax.all_gather(qkv_weight, ('dp', 'band'), axis=0, tiled=True)]
    dot_general x39 -> x0, matrix products: 287 us -> none  [the longest x1 52.4 us: shards(): jnp.einsum('itd,fd->itf', loss_seed_low, w_down, preferred_element_type=j...]
    unnamed x1 -> x0, blocking collectives: 232 us -> none
    slice x16 -> x6, local copies, waits for them, and re-layouts: 95.8 us -> 7.17 us  [the longest x1 1.62 us: shards(): grad_up_out[:, :2 * hidden_units]]
    dynamic_update_slice x12 -> x0, local copies, waits for them, and re-layouts: 79.8 us -> none  [the longest x9 75.6 us: shards(): lax.map(attend_back, (query_blocks, keys_win, values_win, d_attended_bloc...]
    unnamed x25 -> x0, starting transfers between devices: 72.3 us -> none
    psum x2 -> x0, blocking collectives: 56.1 us -> none  [the longest x1 37.9 us: shards(): grad_scale = lax.psum(d_scale_heads, ('dp', 'band'))]
  transfers between devices with their start and end apart: 32 -> 2, of which waited for: 2 -> 0; matrix products, arithmetic and copies ran while one was open for 38% -> 1% of each run, Pallas kernels for 0% -> 13%
where the time goes in v1:
time: 352 us; the launch traced here: 351 us
  Pallas kernels  326 us (93%)
  local copies, waits for them, and re-layouts  19.4 us (6%)
    pallas_call x1, Pallas kernels, feed(): pl.pallas_call(feed_kernel, grid=(images, tokens // tile), in_specs=[bloc...  74.1 us
    pallas_call x1, Pallas kernels, fetch(): pl.pallas_call(functools.partial(fetch_kernel, devices, splits), out_shap...  50.3 us
    pallas_call x1, Pallas kernels, settle(): pl.pallas_call(functools.partial(settle_kernel, devices, splits), out_sha...  44.3 us
    pallas_call x1, Pallas kernels, attend_backward(): pl.pallas_call(functools.partial(attend_back_kernel, height, width), grid...  39.3 us
    pallas_call x1, Pallas kernels, attend_forward(): pl.pallas_call(functools.partial(attend_kernel, height, width), grid=(ima...  38.2 us
    pallas_call x1, Pallas kernels, open_layer(): pl.pallas_call(functools.partial(open_kernel, devices, bands, [column_spl...  29.9 us
    pallas_call x1, Pallas kernels, close_layer(): pl.pallas_call(functools.partial(close_kernel, devices, bands, [column_sp...  25.4 us
    pallas_call x1, Pallas kernels, project_backward(): pl.pallas_call(project_back_kernel, grid=(images,), in_specs=[image(token...  24.5 us
  transfers between devices with their start and end apart: 2, of which 0 were waited for; matrix products, arithmetic and copies ran while one was open for 1% of the time, Pallas kernels for 13%

profile of v1, /device:TPU:0, one launch (start us, length us, event | category | flops | bytes accessed | tf_op | source)
XLA Modules:
  0.0 350.9 jit_solution(7144181832565530220)
XLA Ops:
  0.7 0.8 constant_dynamic-update-slice_fusion.1
  1.4 0.7 constant_dynamic-update-slice_fusion.maps.refs_2_
  2.2 1.3 pad.8.cond
  3.5 29.9 %open_layer.1 = (bf16[8,2,24,1152]{3,2,1,0:T(8,128)(2,1)}, f32[8,768]{1,0:T(8,128)}, bf16[64,128]{1,0:T(8,128)(2,1)}, bf16[3,3,64,384]{3,2,1,0:T(8,128)(2,1)}, bf16[3,3,64,384]{3,2,1,0:T(8,128)(2,1)}) custom-call(bf16[12,1152]{1,0:T(8,128)(2,1)} %qkv.1, bf16[8,768]{1,0:T(8,128)(2,1)} %pad.8.cond, bf16[24,768]{1,0:T(8,128)(2,1)} %copy-done.2, ...), custom_call_target="tpu_custom_call" | custom-call | tf_op jit(solution)/shard_map/open_layer/pallas_call | solution.py:553
  33.4 0.7 fusion.1
  36.7 50.3 %fetch.1 = (bf16[8,2,24,3456]{3,2,1,0:T(8,128)(2,1)}, bf16[8,2,96,384]{3,2,1,0:T(8,128)(2,1)}, bf16[8,2,48,768]{3,2,1,0:T(8,128)(2,1)}) custom-call(bf16[12,3456]{1,0:T(8,128)(2,1)} %pad_maximum_fusion.refs_0_, bf16[48,384]{1,0:T(8,128)(2,1)} %refs_1_.1, bf16[24,768]{1,0:T(8,128)(2,1)} %copy-done.2), custom_call_target="tpu_custom_call" | custom-call | tf_op jit(solution)/shard_map/fetch/pallas_call | solution.py:268
  87.1 1.4 constant_dynamic-slice_fusion
  88.4 38.2 %attend_forward.1 = (bf16[3,1024,384]{2,1,0:T(8,128)(2,1)}, bf16[3,1024,384]{2,1,0:T(8,128)(2,1)}, bf16[3,1408,384]{2,1,0:T(8,128)(2,1)}, bf16[3,1408,384]{2,1,0...) custom-call(s32[1]{0:T(128)} %bitcast.1.first, bf16[3,1024,384]{2,1,0:T(8,128)(2,1)} %bitcast.21, ...), custom_call_target="tpu_custom_call" | custom-call | tf_op jit(solution)/shard_map/attend_forward/pallas_call | solution.py:763
  127.3 74.1 %feed.1 = (bf16[3,1024,384]{2,1,0:T(8,128)(2,1)}, f32[3,1024,384]{2,1,0:T(8,128)}, bf16[3,1024,384]{2,1,0:T(8,128)(2,1)}, bf16[3,1024,128]{2,1,0:T(8,128)(2,1)},...) custom-call(bf16[3,1024,384]{2,1,0:T(8,128)(2,1)} %bitcast.22, ...), custom_call_target="tpu_custom_call" | custom-call | tf_op jit(solution)/shard_map/feed/pallas_call | solution.py:886
  201.5 39.3 %attend_backward.1 = (f32[3,1024,384]{2,1,0:T(8,128)}, f32[3,1024,384]{2,1,0:T(8,128)}, f32[3,1024,384]{2,1,0:T(8,128)}, bf16[3,192,768]{2,1,0:T(8,128)(2,1)}, bf16[3,192,768]{2,1,0:T(8,128)(2,1)}) custom-call(s32[1]{0:T(128)} %bitcast.1.first, bf16[3,1024,384]{2,1,0:T(8,128)(2,1)} %get-tuple-element.54.q, bf16[3,1408,384]{2,1,0:T(8,128)(2,1)} %get-tuple-element.55.k, ...), custom_call_target="tpu_custom_call" | custom-call | tf_op jit(solution)/shard_map/attend_backward/pallas_call | solution.py:977
  240.8 1.3 collective-permute-start
  242.1 1.3 collective-permute-start.1
  243.4 44.3 %settle.1 = (f32[12,3456]{1,0:T(8,128)}, f32[48,384]{1,0:T(8,128)}) custom-call(bf16[8,2,24,3456]{3,2,1,0:T(8,128)(2,1)} %bitcast.28, bf16[8,2,96,384]{3,2,1,0:T(8,128)(2,1)} %bitcast.32), custom_call_target="tpu_custom_call" | custom-call | tf_op jit(solution)/shard_map/settle/pallas_call | solution.py:425
  287.8 1.6 slice.35
  289.4 1.3 slice.33
  291.5 0.9 copy-done
  292.7 24.5 %project_backward.1 = (f32[3,1024,384]{2,1,0:T(8,128)}, bf16[384,1152]{1,0:T(8,128)(2,1)}, f32[3,1,384]{2,1,0:T(1,128)}, f32[1,384]{1,0:T(1,128)}) custom-call(bf16[3,1024,384]{2,1,0:T(8,128)(2,1)} %bitcast.23, f32[3,1,384]{2,1,0:T(1,128)} %broadcast_in_dim.18.scale, bf16[3,1024,384]{2,1,0:T(8,128)(2,1)} %get-tuple-element.54.q, ...), custom_call_target="tpu_custom_call" | custom-call | tf_op jit(solution)/shard_map/project_backward/pallas_call | solution.py:1092
  317.2 0.7 copy.36
  317.9 1.3 select_maximum_fusion.sums
  319.2 25.4 %close_layer.1 = (f32[12,1152]{1,0:T(8,128)}, f32[24,768]{1,0:T(8,128)}, f32[8,768]{1,0:T(8,128)}, f32[8,768]{1,0:T(8,128)}) custom-call(bf16[8,2,24,1152]{3,2,1,0:T(8,128)(2,1)} %bitcast.33, f32[8,768]{1,0:T(8,128)} %select_maximum_fusion.sums, bf16[64,128]{1,0:T(8,128)(2,1)} %get-tuple-element.72.chosen, bf16[768,768]{1,0:T(8,128)(2,1)} %bitcast.31), custom_call_target="tpu_custom_call" | custom-call | tf_op jit(solution)/shard_map/close_layer/pallas_call | solution.py:637
  344.6 1.4 fusion
  346.0 1.3 slice.29
  347.4 0.7 slice_reduce_fusion
  348.8 1.5 copy.40
  (33 shorter events, 5.6 us)
Async XLA Ops:
  0.6 34.1 %copy-start.8 = (f32[6]{0:T(128)S(1)}, f32[6]{0:T(128)}, u32[]{:S(2)}) copy-start(f32[6]{0:T(128)} %param.24) | copy-start | bytes 76
  0.7 35.4 %copy-start.5 = (bf16[12,384]{1,0:T(8,128)(2,1)S(1)}, bf16[12,384]{1,0:T(8,128)(2,1)}, u32[]{:S(2)}) copy-start(bf16[12,384]{1,0:T(8,128)(2,1)} %param.25) | copy-start | bytes 27652
  0.7 35.4 %copy-start.3 = (bf16[12,3072]{1,0:T(8,128)(2,1)S(1)}, bf16[12,3072]{1,0:T(8,128)(2,1)}, u32[]{:S(2)}) copy-start(bf16[12,3072]{1,0:T(8,128)(2,1)} %param.27) | copy-start | bytes 221188
  2.2 1.3 copy-start.2
  36.0 90.6 %copy-start.7 = (f32[3]{0:T(128)S(1)}, f32[3]{0:T(128)}, u32[]{:S(2)}) copy-start(f32[3]{0:T(128)} %param.20) | copy-start | bytes 40
  240.8 50.7 %copy-start.6 = (f32[3,1,384]{2,1,0:T(1,128)S(1)}, f32[3,1,384]{2,1,0:T(1,128)}, u32[]{:S(2)}) copy-start(f32[3,1,384]{2,1,0:T(1,128)} %get-tuple-element.70) | copy-start | bytes 13828
  240.8 50.7 %collective-permute-start = (bf16[3,192,768]{2,1,0:T(8,128)(2,1)}, bf16[3,192,768]{2,1,0:T(8,128)(2,1)S(1)}, u32[]{:S(2)}, u32[]{:S(2)}) collective-permute-start(bf16[3,192,768]{2,1,0:T(8,128)(2,1)} %get-tuple-element.63), channel_id=1, source_target_pairs={{0,1},{1,2},{2,3},{4,5},{5,6},{6,7},{8,9},{9,10},{10,11},{12,13},{... | collective-permute-start | bytes 2654216 | tf_op jit(solution)/shard_map/ppermute | solution.py:1153
  242.1 49.4 %collective-permute-start.1 = (bf16[3,192,768]{2,1,0:T(8,128)(2,1)}, bf16[3,192,768]{2,1,0:T(8,128)(2,1)S(1)}, u32[]{:S(2)}, u32[]{:S(2)}) collective-permute-start(bf16[3,192,768]{2,1,0:T(8,128)(2,1)} %get-tuple-element.64), channel_id=1, source_target_pairs={{1,0},{2,1},{3,2},{5,4},{6,5},{7,6},{9,8},{10,9},{11,10},{13,12},{... | collective-permute-start | bytes 2654216 | tf_op jit(solution)/shard_map/ppermute | solution.py:1153
  291.5 0.9 copy-start
  291.5 1.2 copy-start.1
  317.1 33.2 %copy-start.4 = (f32[48,384]{1,0:T(8,128)S(1)}, f32[48,384]{1,0:T(8,128)}, u32[]{:S(2)}) copy-start(f32[48,384]{1,0:T(8,128)} %get-tuple-element.109) | copy-start | bytes 221188

commit v2 on v1

--- a/solution.py
+++ b/solution.py
@@ -120,9 +120,21 @@
     def __init__(self, send, recv):
         self.send, self.recv, self.count = send, recv, 0
 
-    def __call__(self, source, target, peer):
-        slot = self.count
-        self.count += 1
+    def reserve(self, count):
+        self.count += count
+        return self.count - count
+
+    def batch(self, count, build):
+        first = self.reserve(count)
+
+        def made():
+            entries = build()
+            assert len(entries) == count
+            return [self.one(first + i, *entry) for i, entry in enumerate(entries)]
+
+        return made
+
+    def one(self, slot, source, target, peer):
         return pltpu.make_async_remote_copy(
             src_ref=source,
             dst_ref=target,
@@ -133,19 +145,30 @@
         )
 
 
-def start(copies):
-    for copy in copies:
-        copy.start()
-
-
-def arrive(copies):
-    for copy in copies:
-        copy.wait_recv()
-
-
-def depart(copies):
-    for copy in copies:
-        copy.wait_send()
+def start(*batches):
+    for batch in batches:
+        for copy in batch():
+            copy.start()
+
+
+def arrive(*batches):
+    for batch in batches:
+        for copy in batch():
+            copy.wait_recv()
+
+
+def depart(*batches):
+    for batch in batches:
+        for copy in batch():
+            copy.wait_send()
+
+
+def run(*steps):
+    def step():
+        for inner in steps:
+            inner()
+
+    return step
 
 
 def greet(peers):
@@ -155,10 +178,12 @@
     pl.semaphore_wait(barrier, len(peers))
 
 
-def place(devices):
-    dp, band = lax.axis_index("dp"), lax.axis_index("band")
-    bits = [1 << i for i in range(devices.bit_length() - 1)]
-    return dp, band, bits
+def here():
+    return lax.axis_index("dp"), lax.axis_index("band")
+
+
+def mesh_bits(devices):
+    return [1 << i for i in range(devices.bit_length() - 1)]
 
 
 def ways(bits):
@@ -166,279 +191,239 @@
     return (far[::-1], far)
 
 
-def gather_steps(devices, copy, local, shards, pairs, blocks, outs, splits):
-    dp, band, bits = place(devices)
-    high = band // 2
-    core = (flip(dp, 1), band)
+def exchange_peers(devices, bands):
+    dp, band = here()
+    return [(dp, (band + d) % bands) for d in range(1, bands)] + [
+        (flip(dp, bit), band) for bit in mesh_bits(devices)
+    ]
+
+
+def column_split(columns, first):
+    return ((0, first), (first, columns - first))
+
+
+def gather_steps(devices, copies, local, shards, pairs, blocks, outs, splits):
+    bits = mesh_bits(devices)
     n = len(shards)
-    done = {"sent": []}
-
-    def begin():
-        done["near"] = [copy(shards[a], pairs[a], (dp, flip(band, 1))) for a in range(n)]
-        start(done["near"])
+    stages = len(bits) - 1
+    each = range(n)
+
+    def near_entries():
+        dp, band = here()
+        return [(shards[a], pairs[a], (dp, flip(band, 1))) for a in each]
+
+    def far_entries():
+        dp, band = here()
+        return [(blocks[a], outs[a].at[dp, band // 2], (dp, flip(band, 2))) for a in each]
+
+    def core_entries():
+        dp, band = here()
+        return [(blocks[a], outs[a].at[dp, band // 2], (flip(dp, 1), band)) for a in each]
+
+    def other_entries():
+        dp, band = here()
+        spots = [outs[a].at[dp, 1 - band // 2] for a in each]
+        return [(spot, spot, (flip(dp, 1), band)) for spot in spots]
+
+    def ring_entries(k, forward):
+        dp, band = here()
+        entries = []
+        for way, order in enumerate(ways(bits)):
+            source = flip(dp, order[k]) if forward else dp
+            peer = flip(dp, 1) if forward else flip(dp, order[k])
+            for index in relatives(source, order[:k]):
+                for a in each:
+                    cut = outs[a].at[index, :, :, pl.ds(*splits[a][way])]
+                    entries.append((cut, cut, (peer, band)))
+        return entries
+
+    near = copies.batch(n, near_entries)
+    far = copies.batch(n, far_entries)
+    core = copies.batch(n, core_entries)
+    other = copies.batch(n, other_entries)
+    rings = [copies.batch(2 * n << k, functools.partial(ring_entries, k, False)) for k in range(stages)]
+    fresh = [copies.batch(2 * n << k, functools.partial(ring_entries, k, True)) for k in range(stages)]
+
+    def own():
+        dp, band = here()
+        return [
+            pltpu.make_async_copy(blocks[a], outs[a].at[dp, band // 2], local.at[a]) for a in each
+        ]
 
     def pair():
-        arrive(done["near"])
-        odd = (band % 2) == 1
-        for a in range(n):
-            own, other = shards[a][...], pairs[a][...]
-            rows = own.shape[0]
-            blocks[a][:rows] = jnp.where(odd, other, own)
-            blocks[a][rows:] = jnp.where(odd, own, other)
-        done["own"] = [
-            pltpu.make_async_copy(blocks[a], outs[a].at[dp, high], local.at[a]) for a in range(n)
-        ]
-        done["far"] = [
-            copy(blocks[a], outs[a].at[dp, high], (dp, flip(band, 2))) for a in range(n)
-        ]
-        done["core"] = [copy(blocks[a], outs[a].at[dp, high], core) for a in range(n)]
-        start(done["own"] + done["far"] + done["core"])
-        done["sent"] += done["near"] + done["far"]
+        arrive(near)
+        odd = (lax.axis_index("band") % 2) == 1
+        for a in each:
+            mine, theirs = shards[a][...], pairs[a][...]
+            rows = mine.shape[0]
+            blocks[a][:rows] = jnp.where(odd, theirs, mine)
+            blocks[a][rows:] = jnp.where(odd, mine, theirs)
+        start(own, far, core)
 
     def spread(k):
         def step():
             if k == 0:
-                for own in done["own"]:
-                    own.wait()
-                arrive(done["far"])
-                fresh = [copy(outs[a].at[dp, 1 - high], outs[a].at[dp, 1 - high], core) for a in range(n)]
+                for copy in own():
+                    copy.wait()
+                arrive(far)
+                start(other)
             else:
-                fresh = []
-                arrive(done["ring"])
-                for way, bit_order in enumerate(ways(bits)):
-                    for index in relatives(flip(dp, bit_order[k - 1]), bit_order[: k - 1]):
-                        for a in range(n):
-                            cut = outs[a].at[index, :, :, pl.ds(*splits[a][way])]
-                            fresh.append(copy(cut, cut, core))
-            start(fresh)
-            done["core"] += fresh
-            if k == len(bits) - 1:
-                return
-            done["ring"] = []
-            for way, bit_order in enumerate(ways(bits)):
-                peer = (flip(dp, bit_order[k]), band)
-                for index in relatives(dp, bit_order[:k]):
-                    for a in range(n):
-                        cut = outs[a].at[index, :, :, pl.ds(*splits[a][way])]
-                        done["ring"].append(copy(cut, cut, peer))
-            start(done["ring"])
-            done["sent"] += done["ring"]
+                arrive(rings[k - 1])
+                start(fresh[k - 1])
+            if k < stages:
+                start(rings[k])
 
         return step
 
     def finish():
-        arrive(done["core"])
-        depart(done["sent"] + done["core"])
-
-    return [begin, pair] + [spread(k) for k in range(len(bits))] + [finish]
+        arrive(core, other, *fresh)
+        depart(near, far, core, other, *rings, *fresh)
+
+    return [functools.partial(start, near), pair, *[spread(k) for k in range(stages + 1)], finish]
 
 
 def gather_copies(devices, n):
-    count = n * 3
-    bits = devices.bit_length() - 1
-    for k in range(bits):
-        count += n if k == 0 else 2 * n * (1 << (k - 1))
-        if k < bits - 1:
-            count += 2 * n * (1 << k)
-    return count
-
-
-def exchange_peers(devices):
-    dp, band, bits = place(devices)
-    return [(dp, flip(band, 1)), (dp, flip(band, 2))] + [(flip(dp, bit), band) for bit in bits]
-
-
-def column_split(columns, first):
-    return ((0, first), (first, columns - first))
-
-
-def fetch_kernel(devices, splits, *refs):
-    n = len(splits)
-    shards, outs = refs[:n], refs[n : 2 * n]
-    pairs, blocks = refs[2 * n : 3 * n], refs[3 * n : 4 * n]
-    send, recv, local = refs[4 * n :]
-    greet(exchange_peers(devices))
-    for step in gather_steps(devices, Copies(send, recv), local, shards, pairs, blocks, outs, splits):
-        step()
-
-
-def fetch(devices, shards, firsts, collective):
-    splits = [column_split(s.shape[1], first) for s, first in zip(shards, firsts)]
+    stages = devices.bit_length() - 2
+    return 4 * n + sum(4 * n << k for k in range(stages))
+
+
+def gather_outputs(devices, shards):
+    return [jax.ShapeDtypeStruct((devices, 2, 2 * s.shape[0], s.shape[1]), s.dtype) for s in shards]
+
+
+def gather_scratch(devices, shards):
     count = gather_copies(devices, len(shards))
-    outs = pl.pallas_call(
-        functools.partial(fetch_kernel, devices, splits),
-        out_shape=[
-            jax.ShapeDtypeStruct((devices, 2, 2 * s.shape[0], s.shape[1]), s.dtype) for s in shards
-        ],
-        in_specs=[pl.BlockSpec(memory_space=pltpu.VMEM)] * len(shards),
-        out_specs=[pl.BlockSpec(memory_space=pl.ANY)] * len(shards),
-        scratch_shapes=[
-            *[pltpu.VMEM(s.shape, s.dtype) for s in shards],
-            *[pltpu.VMEM((2 * s.shape[0], s.shape[1]), s.dtype) for s in shards],
-            pltpu.SemaphoreType.DMA((count,)),
-            pltpu.SemaphoreType.DMA((count,)),
-            pltpu.SemaphoreType.DMA((len(shards),)),
-        ],
-        compiler_params=pltpu.CompilerParams(
-            collective_id=collective, has_side_effects=True, vmem_limit_bytes=VMEM_LIMIT
-        ),
-        name="fetch",
-    )(*shards)
-    return [o.reshape(-1, o.shape[-1]) for o in outs]
+    return [
+        *[pltpu.VMEM(s.shape, s.dtype) for s in shards],
+        *[pltpu.VMEM((2 * s.shape[0], s.shape[1]), s.dtype) for s in shards],
+        pltpu.SemaphoreType.DMA((count,)),
+        pltpu.SemaphoreType.DMA((count,)),
+        pltpu.SemaphoreType.DMA((len(shards),)),
+    ]
 
 
 def add_into(target, index, cut, addend):
-    start_col, width = cut
-    columns = pl.ds(start_col, width)
+    columns = pl.ds(*cut)
     for half in range(2):
-        total = target[index, half, :, columns].astype(F32) + addend(half)
+        total = target[index, half, :, columns].astype(F32) + addend(half, columns).astype(F32)
         target[index, half, :, columns] = total.astype(BF16)
 
 
-def scatter_steps(devices, copy, grads, inbox, near, far, outs, splits):
-    dp, band, bits = place(devices)
-    high = band // 2
+def scatter_steps(devices, copies, grads, inbox, near, far, outs, splits):
+    bits = mesh_bits(devices)
     n = len(grads)
-    done = {"sent": []}
-
-    def send_core():
-        done["in"] = []
+    stages = len(bits) - 1
+    each = range(n)
+    base = 1 << stages
+    spots = [base + sum(1 << (stages - 1 - j) for j in range(k)) for k in range(stages)]
+
+    def core_entries():
+        dp, band = here()
         peer = flip(dp, 1)
-        for k, index in enumerate(relatives(peer, bits[1:])):
-            for a in range(n):
-                done["in"].append(copy(grads[a].at[index], inbox[a].at[k], (peer, band)))
-        start(done["in"])
-        done["sent"] += done["in"]
+        return [
+            (grads[a].at[index], inbox[a].at[k], (peer, band))
+            for k, index in enumerate(relatives(peer, bits[1:]))
+            for a in each
+        ]
+
+    def ring_entries(k):
+        dp, band = here()
+        entries = []
+        for way, order in enumerate(ways(bits)):
+            peer = flip(dp, order[k])
+            for j, index in enumerate(relatives(peer, order[k + 1 :])):
+                for a in each:
+                    columns = pl.ds(*splits[a][way])
+                    source = grads[a].at[index, :, :, columns]
+                    entries.append((source, inbox[a].at[spots[k] + j, :, :, columns], (peer, band)))
+        return entries
+
+    def far_entries():
+        dp, band = here()
+        return [(grads[a].at[dp, 1 - band // 2], far[a], (dp, flip(band, 2))) for a in each]
+
+    def near_entries():
+        dp, band = here()
+        return [(near[a].at[0], near[a].at[1], (dp, flip(band, 1))) for a in each]
+
+    core = copies.batch(n << stages, core_entries)
+    rings = [
+        copies.batch(2 * n << (stages - 1 - k), functools.partial(ring_entries, k)) for k in range(stages)
+    ]
+    bands_far = copies.batch(n, far_entries)
+    bands_near = copies.batch(n, near_entries)
 
     def add_core():
-        arrive(done["in"])
+        arrive(core)
+        dp, _ = here()
         for k, index in enumerate(relatives(dp, bits[1:])):
-            for a in range(n):
-                whole = (0, splits[a][0][1] + splits[a][1][1])
-                add_into(grads[a], index, whole, lambda half: inbox[a][k, half].astype(F32))
-
-    base = 1 << (len(bits) - 1)
-
-    def spot(k):
-        return base + sum(1 << (len(bits) - 2 - j) for j in range(k))
-
-    def send_far(k):
-        done["in"] = []
-        for way, order in enumerate(ways(bits)):
-            bit = order[k]
-            peer = flip(dp, bit)
-            for j, index in enumerate(relatives(peer, order[k + 1 :])):
-                for a in range(n):
-                    cols = pl.ds(*splits[a][way])
-                    done["in"].append(
-                        copy(grads[a].at[index, :, :, cols], inbox[a].at[spot(k) + j, :, :, cols], (peer, band))
-                    )
-        start(done["in"])
-        done["sent"] += done["in"]
-
-    def add_far(k):
-        arrive(done["in"])
+            for a in each:
+                whole = (0, sum(width for _, width in splits[a]))
+                add_into(grads[a], index, whole, lambda half, columns: inbox[a][k, half])
+
+    def add_ring(k):
+        arrive(rings[k])
+        dp, _ = here()
         for way, order in enumerate(ways(bits)):
             for j, index in enumerate(relatives(dp, order[k + 1 :])):
-                for a in range(n):
-                    cols = pl.ds(*splits[a][way])
+                for a in each:
                     add_into(
                         grads[a], index, splits[a][way],
-                        lambda half: inbox[a][spot(k) + j, half, :, cols].astype(F32),
+                        lambda half, columns: inbox[a][spots[k] + j, half, :, columns],
                     )
 
-    def send_band():
-        done["in"] = [
-            copy(grads[a].at[dp, 1 - high], far[a], (dp, flip(band, 2))) for a in range(n)
-        ]
-        start(done["in"])
-        done["sent"] += done["in"]
-
-    def send_near():
-        arrive(done["in"])
+    def add_far():
+        arrive(bands_far)
+        dp, band = here()
         odd = (band % 2) == 1
-        done["in"] = []
-        for a in range(n):
-            total = grads[a][dp, high].astype(F32) + far[a][...].astype(F32)
+        for a in each:
+            total = grads[a][dp, band // 2].astype(F32) + far[a][...].astype(F32)
             rows = total.shape[0] // 2
             low, top = total[:rows], total[rows:]
             outs[a][...] = jnp.where(odd, top, low)
             near[a][0] = jnp.where(odd, low, top).astype(BF16)
-            done["in"].append(copy(near[a].at[0], near[a].at[1], (dp, flip(band, 1))))
-        start(done["in"])
-        done["sent"] += done["in"]
 
     def finish():
-        arrive(done["in"])
-        for a in range(n):
+        arrive(bands_near)
+        for a in each:
             outs[a][...] += near[a][1].astype(F32)
-        depart(done["sent"])
-
-    def chain(*steps):
-        def run():
-            for step in steps:
-                step()
-
-        return run
-
-    steps = [send_core, chain(add_core, functools.partial(send_far, 0))]
-    for k in range(len(bits) - 1):
-        following = functools.partial(send_far, k + 1) if k + 1 < len(bits) - 1 else send_band
-        steps.append(chain(functools.partial(add_far, k), following))
-    return steps + [send_near, finish]
+        depart(core, *rings, bands_far, bands_near)
+
+    sends = [*rings, bands_far, bands_near]
+    adds = [add_core, *[functools.partial(add_ring, k) for k in range(stages)], add_far]
+    steps = [run(add, functools.partial(start, send)) for add, send in zip(adds, sends)]
+    return [functools.partial(start, core), *steps, finish]
 
 
 def scatter_copies(devices, n):
-    bits = devices.bit_length() - 1
-    count = n * (1 << (bits - 1))
-    for k in range(bits - 1):
-        count += 2 * n * (1 << (bits - 2 - k))
-    return count + 2 * n
+    stages = devices.bit_length() - 2
+    return (n << stages) + sum(2 * n << k for k in range(stages)) + 2 * n
 
 
 def scatter_scratch(devices, shapes):
-    slots = devices
-    scratch = [pltpu.VMEM((slots, 2, s[2], s[3]), BF16) for s in shapes]
-    scratch += [pltpu.VMEM((2, s[2] // 2, s[3]), BF16) for s in shapes]
-    scratch += [pltpu.VMEM((s[2], s[3]), BF16) for s in shapes]
-    return scratch
-
-
-def settle_kernel(devices, splits, *refs):
-    n = len(splits)
-    grads_hbm, outs = refs[:n], refs[n : 2 * n]
-    grads, inbox, near, far = (refs[(2 + i) * n : (3 + i) * n] for i in range(4))
-    send, recv, local = refs[6 * n :]
-    loads = [pltpu.make_async_copy(grads_hbm[a], grads[a], local.at[a]) for a in range(n)]
-    start(loads)
-    greet(exchange_peers(devices))
-    for load in loads:
-        load.wait()
-    for step in scatter_steps(devices, Copies(send, recv), grads, inbox, near, far, outs, splits):
-        step()
-
-
-def settle(devices, grads, firsts, collective):
-    splits = [column_split(g.shape[1], first) for g, first in zip(grads, firsts)]
-    shapes = [(devices, 2, g.shape[0] // (2 * devices), g.shape[1]) for g in grads]
-    count = scatter_copies(devices, len(grads))
-    return pl.pallas_call(
-        functools.partial(settle_kernel, devices, splits),
-        out_shape=[jax.ShapeDtypeStruct((s[2] // 2, s[3]), F32) for s in shapes],
-        in_specs=[pl.BlockSpec(memory_space=pl.ANY)] * len(grads),
-        out_specs=[pl.BlockSpec(memory_space=pltpu.VMEM)] * len(grads),
-        scratch_shapes=[
-            *[pltpu.VMEM(s, BF16) for s in shapes],
-            *scatter_scratch(devices, shapes),
-            pltpu.SemaphoreType.DMA((count,)),
-            pltpu.SemaphoreType.DMA((count,)),
-            pltpu.SemaphoreType.DMA((len(grads),)),
-        ],
-        compiler_params=pltpu.CompilerParams(
-            collective_id=collective, has_side_effects=True, vmem_limit_bytes=VMEM_LIMIT
-        ),
-        name="settle",
-    )(*[g.reshape(s) for g, s in zip(grads, shapes)])
+    count = scatter_copies(devices, len(shapes))
+    return [
+        *[pltpu.VMEM(s, BF16) for s in shapes],
+        *[pltpu.VMEM(s, BF16) for s in shapes],
+        *[pltpu.VMEM((2, s[2] // 2, s[3]), BF16) for s in shapes],
+        *[pltpu.VMEM((s[2], s[3]), BF16) for s in shapes],
+        pltpu.SemaphoreType.DMA((count,)),
+        pltpu.SemaphoreType.DMA((count,)),
+        pltpu.SemaphoreType.DMA((len(shapes),)),
+    ]
+
+
+def grad_shapes(devices, grads):
+    return [(devices, 2, g.shape[0] // (2 * devices), g.shape[1]) for g in grads]
+
+
+def spaced(first, span, steps):
+    return [(first + span * k // len(steps), step) for k, step in enumerate(steps)]
+
+
+def hooked(moment, hooks):
+    for when, hook in hooks:
+        pl.when(moment == when)(hook)
 
 
 def open_kernel(
@@ -448,15 +433,20 @@
     pair, block, conds, padded, partial, part_in, band_in,
     send, recv, local, halo_send, halo_recv,
 ):
-    dp, band, _ = place(devices)
+    dp, band = here()
     rows = maps.shape[0]
-    copy = Copies(send, recv)
+    copies = Copies(send, recv)
     around = [((dp + d) % devices, band) for d in range(1, devices)]
     along = [(dp, (band + d) % bands) for d in range(1, bands)]
     edge = top.shape[1]
     tall = tokens.shape[1]
     greet(around + along)
-    steps = gather_steps(devices, copy, local, [qkv], [pair], [block], [w_qkv], splits)
+    steps = gather_steps(devices, copies, local, [qkv], [pair], [block], [w_qkv], splits)
+    first = copies.batch(devices - 1, lambda: [(cond, conds.at[dp], peer) for peer in around])
+    second = copies.batch(
+        devices - 1, lambda: [(partial.at[peer[0]], part_in.at[dp], peer) for peer in around]
+    )
+    third = copies.batch(bands - 1, lambda: [(band_in.at[band], band_in.at[band], peer) for peer in along])
 
     up = pltpu.make_async_remote_copy(
         src_ref=tokens.at[:, pl.ds(tall - edge, edge)], dst_ref=top,
@@ -473,7 +463,6 @@
 
     steps[0]()
     conds[dp] = cond[...]
-    first = [copy(cond, conds.at[dp], peer) for peer in around]
     start(first)
     padded[...] = jnp.zeros_like(padded)
     padded[:rows] = maps[...]
@@ -486,7 +475,6 @@
     picked = nn(conds[...].reshape(-1, conds.shape[2]), jnp.where(hit, 1.0, 0.0).astype(BF16)).astype(BF16)
     chosen[...] = picked
     partial[...] = nn(picked, padded[...]).reshape(partial.shape)
-    second = [copy(partial.at[peer[0]], part_in.at[dp], peer) for peer in around]
     start(second)
     steps[2]()
 
@@ -511,7 +499,6 @@
     for peer in around:
         total = total + part_in[peer[0]]
     band_in[band] = total
-    third = [copy(band_in.at[band], band_in.at[band], peer) for peer in along]
     start(third)
     for step in steps[3:-1]:
         step()
@@ -521,7 +508,7 @@
         total = total + band_in[b]
     scales[...] = 1.0 + total
     steps[-1]()
-    depart(first + second + third)
+    depart(first, second, third)
 
     @pl.when(band < bands - 1)
     def _():
@@ -586,28 +573,28 @@
     devices, bands, splits, images,
     grad, sums, chosen, maps,
     out, grad_maps, grad_cond, grad_heads,
-    acc, inbox, near, far, band_in, all_in,
-    send, recv, local,
+    acc, inbox, near, far, send, recv, local, band_in, all_in, sum_send, sum_recv,
 ):
-    dp, band, _ = place(devices)
-    copy = Copies(send, recv)
+    dp, band = here()
+    copies = Copies(send, recv)
+    small = Copies(sum_send, sum_recv)
     around = [((dp + d) % devices, band) for d in range(1, devices)]
     along = [(dp, (band + d) % bands) for d in range(1, bands)]
     load = pltpu.make_async_copy(grad, acc, local.at[0])
     load.start()
     greet(around + along)
-    first = [copy(sums, band_in.at[band], peer) for peer in along]
+    first = small.batch(bands - 1, lambda: [(sums, band_in.at[band], peer) for peer in along])
+    second = small.batch(devices - 1, lambda: [(all_in.at[dp], all_in.at[dp], peer) for peer in around])
     start(first)
     band_in[band] = sums[...]
     load.wait()
-    steps = scatter_steps(devices, copy, [acc], [inbox], [near], [far], [out], splits)
+    steps = scatter_steps(devices, copies, [acc], [inbox], [near], [far], [out], splits)
     steps[0]()
     arrive(first)
     total = band_in[0]
     for b in range(1, bands):
         total = total + band_in[b]
     all_in[dp] = total
-    second = [copy(all_in.at[dp], all_in.at[dp], peer) for peer in around]
     start(second)
     steps[1]()
     parts = [part.astype(BF16) for part in thirds(total)]
@@ -624,7 +611,7 @@
     grad_maps[...] = sum(tn(chosen[...], part.astype(BF16)) for part in thirds(whole))[:rows]
     for step in steps[3:]:
         step()
-    depart(first + second)
+    depart(first, second)
 
 
 def close_layer(devices, bands, grad, sums, chosen, maps, images, first, collective):
@@ -632,7 +619,7 @@
     shape = (devices, 2, grad.shape[0] // (2 * devices), columns)
     both = sums.shape[1]
     map_rows = maps.shape[0] // (devices * bands)
-    count = scatter_copies(devices, 1) + devices - 1 + bands - 1
+    count = devices - 1 + bands - 1
     vmem, hbm = pl.BlockSpec(memory_space=pltpu.VMEM), pl.BlockSpec(memory_space=pl.ANY)
     return pl.pallas_call(
         functools.partial(close_kernel, devices, bands, [column_split(columns, first)], images),
@@ -645,13 +632,11 @@
         in_specs=[hbm, vmem, vmem, vmem],
         out_specs=[vmem] * 4,
         scratch_shapes=[
-            pltpu.VMEM(shape, BF16),
             *scatter_scratch(devices, [shape]),
             pltpu.VMEM((bands, 8, both), F32),
             pltpu.VMEM((devices, 8, both), F32),
             pltpu.SemaphoreType.DMA((count,)),
             pltpu.SemaphoreType.DMA((count,)),
-            pltpu.SemaphoreType.DMA((1,)),
         ],
         compiler_params=pltpu.CompilerParams(
             collective_id=collective, has_side_effects=True, vmem_limit_bytes=VMEM_LIMIT
@@ -661,10 +646,26 @@
 
 
 def attend_kernel(
-    height, width, first, x, top, bottom, scale, w_qkv, factor, pool, crow, srow, ccol, scol,
-    att, q_out, k_out, v_out, inverse_out, log_out,
-    cos_s, sin_s, feat_s,
+    height, width, images, devices, bands, splits, *refs,
 ):
+    n = len(splits)
+    first, x, top, bottom, scale, w_qkv, factor, pool, crow, srow, ccol, scol = refs[:12]
+    shards, rest = refs[12 : 12 + n], refs[12 + n :]
+    att, q_out, k_out, v_out, inverse_out, log_out = rest[:6]
+    outs, rest = rest[6 : 6 + n], rest[6 + n :]
+    cos_s, sin_s, feat_s = rest[:3]
+    pairs_s, blocks_s = rest[3 : 3 + n], rest[3 + n : 3 + 2 * n]
+    send, recv, local = rest[3 + 2 * n :]
+    steps = gather_steps(devices, Copies(send, recv), local, shards, pairs_s, blocks_s, outs, splits)
+    groups = x.shape[1] // (2 * width)
+    final = images * groups
+    hooks = spaced(2, final - 4, steps[1:-1])
+
+    @pl.when(pl.program_id(0) == 0)
+    def _():
+        greet(exchange_peers(devices, bands))
+        steps[0]()
+
     dim = x.shape[-1]
     pairs = dim // 128
     tokens = x.shape[1]
@@ -747,12 +748,21 @@
                 for t in range(3):
                     logs = jnp.where(lane == 96 + 3 * (2 * p + h) + t, kept[t], logs)
         log_out[0, own] = logs.astype(BF16)
+        hooked(pl.program_id(0) * groups + g, hooks)
         return 0
 
     lax.fori_loop(0, tokens // block, attend, 0)
 
-
-def attend_forward(first, x, top, bottom, scale, w_qkv, factor, pool, turns, height, width):
+    @pl.when(pl.program_id(0) == pl.num_programs(0) - 1)
+    def _():
+        steps[-1]()
+
+
+def attend_forward(
+    first, x, top, bottom, scale, w_qkv, factor, pool, turns, height, width,
+    devices, bands, shards, firsts, collective,
+):
+    splits = [column_split(s.shape[1], start_col) for s, start_col in zip(shards, firsts)]
     images, tokens, dim = x.shape
     border = top.shape[1]
     extended = tokens + 2 * border
@@ -760,17 +770,18 @@
     keys = (2 * RADIUS + 2) * width
     image = lambda rows, cols: pl.BlockSpec((1, rows, cols), lambda i: (i, 0, 0))
     whole = lambda a: pl.BlockSpec(a.shape, lambda i: (0,) * a.ndim)
-    return pl.pallas_call(
-        functools.partial(attend_kernel, height, width),
+    outs = pl.pallas_call(
+        functools.partial(attend_kernel, height, width, images, devices, bands, splits),
         grid=(images,),
         in_specs=[
             pl.BlockSpec(memory_space=pltpu.SMEM),
             image(tokens, dim), image(border, dim), image(border, dim), image(1, dim),
-            whole(w_qkv), whole(factor), whole(pool), *[whole(t) for t in turns],
+            whole(w_qkv), whole(factor), whole(pool), *[whole(t) for t in turns], *[whole(t) for t in shards],
         ],
         out_specs=[
             image(tokens, dim), image(tokens, dim), image(extended, dim), image(extended, dim),
             image(tokens, 128), image(tokens, 128),
+            *[pl.BlockSpec(memory_space=pl.ANY) for _ in shards],
         ],
         out_shape=[
             jax.ShapeDtypeStruct((images, tokens, dim), BF16),
@@ -779,15 +790,20 @@
             jax.ShapeDtypeStruct((images, extended, dim), BF16),
             jax.ShapeDtypeStruct((images, tokens, 128), F32),
             jax.ShapeDtypeStruct((images, tokens, 128), BF16),
+            *gather_outputs(devices, shards),
         ],
         scratch_shapes=[
             pltpu.VMEM((extended, 128), F32),
             pltpu.VMEM((extended, 128), F32),
             pltpu.VMEM((tokens // block, keys, 128), BF16),
-        ],
-        compiler_params=pltpu.CompilerParams(vmem_limit_bytes=VMEM_LIMIT),
+            *gather_scratch(devices, shards),
+        ],
+        compiler_params=pltpu.CompilerParams(
+            collective_id=collective, has_side_effects=True, vmem_limit_bytes=VMEM_LIMIT
+        ),
         name="attend_forward",
-    )(first, x, top, bottom, scale, w_qkv, factor, pool, *turns)
+    )(first, x, top, bottom, scale, w_qkv, factor, pool, *turns, *shards)
+    return outs[:6], [o.reshape(-1, o.shape[-1]) for o in outs[6:]]
 
 
 def gaussian_parts(gate):
@@ -907,21 +923,74 @@
     )(x, att, cot, weight, scale, w_up_out, w_up_out, w_down, spread)
 
 
-def attend_back_kernel(
-    height, width, first, q, k, v, d_att, logs, deltas,
-    d_q, d_k, d_v, d_top, d_bottom,
-    feat_s, dk_s, dv_s,
-):
+def attend_back_kernel(height, width, q_images, devices, bands, splits, *refs):
+    n = len(splits)
+    first, q, k, v, d_att, logs, deltas = refs[:7]
+    grads_hbm, rest = refs[7 : 7 + n], refs[7 + n :]
+    d_q, d_k, d_v, above, below = rest[:5]
+    outs, rest = rest[5 : 5 + n], rest[5 + n :]
+    feat_s, dk_s, dv_s, d_top, d_bottom, halo_send, halo_recv, fill = rest[:8]
+    rest = rest[8:]
+    grads, inbox, near, far = (rest[i * n : (i + 1) * n] for i in range(4))
+    send, recv, local = rest[4 * n :]
     dim = q.shape[-1]
     pairs = dim // 128
     tokens = q.shape[1]
     border = d_top.shape[1]
     block = 2 * width
+    groups = tokens // block
     keys = feat_s.shape[1]
-
-    @pl.when(pl.program_id(0) == 0)
-    def _():
+    image = pl.program_id(0)
+    images = q_images
+    steps = scatter_steps(devices, Copies(send, recv), grads, inbox, near, far, outs, splits)
+    hooks = spaced(3, images * groups - 4, steps[1:-1])
+
+    def loads():
+        return [pltpu.make_async_copy(grads_hbm[a], grads[a], local.at[a]) for a in range(n)]
+
+    def to_above(at):
+        dp, band = here()
+        return pltpu.make_async_remote_copy(
+            src_ref=d_top.at[at], dst_ref=below.at[at],
+            send_sem=halo_send.at[0, at], recv_sem=halo_recv.at[0, at],
+            device_id=(dp, (band + bands - 1) % bands), device_id_type=MESH,
+        )
+
+    def to_below(at):
+        dp, band = here()
+        return pltpu.make_async_remote_copy(
+            src_ref=d_bottom.at[at], dst_ref=above.at[at],
+            send_sem=halo_send.at[1, at], recv_sem=halo_recv.at[1, at],
+            device_id=(dp, (band + 1) % bands), device_id_type=MESH,
+        )
+
+    def empty(side, target):
+        return pltpu.make_async_copy(side, target, fill.at[0])
+
+    @pl.when(image == 0)
+    def _():
+        for load in loads():
+            load.start()
         build_key_features(first[0], height, width, feat_s)
+        greet(exchange_peers(devices, bands))
+        for load in loads():
+            load.wait()
+        steps[0]()
+
+    def send_borders():
+        band = lax.axis_index("band")
+        d_top[image, :, :dim] = dk_s[:border].astype(BF16)
+        d_top[image, :, dim:] = dv_s[:border].astype(BF16)
+        d_bottom[image, :, :dim] = dk_s[border + tokens :].astype(BF16)
+        d_bottom[image, :, dim:] = dv_s[border + tokens :].astype(BF16)
+
+        @pl.when(band > 0)
+        def _():
+            to_above(image).start()
+
+        @pl.when(band < bands - 1)
+        def _():
+            to_below(image).start()
 
     dk_s[...] = jnp.zeros_like(dk_s)
     dv_s[...] = jnp.zeros_like(dv_s)
@@ -929,7 +998,12 @@
     ask = query_features(width)
     one_lanes = jnp.where(lanes((keys, 128)) < 3 * 2 * pairs, 1.0, 0.0).astype(BF16)
 
-    def back(g, _):
+    def back(i, _):
+        pl.when(i == groups // 2)(send_borders)
+        hooked(image * groups + i, hooks)
+        quarter = groups // 4
+        half = i // (2 * quarter)
+        g = i + 2 * quarter * ((i // quarter) % 2) * (1 - half) - quarter * half
         own = pl.ds(pl.multiple_of(g * block, block), block)
         window = pl.ds(pl.multiple_of(g * block, block), keys)
         feats = feat_s[g]
@@ -961,30 +1035,66 @@
     lax.fori_loop(0, tokens // block, back, 0)
     d_k[0] = dk_s[border : border + tokens]
     d_v[0] = dv_s[border : border + tokens]
-    d_top[0, :, :dim] = dk_s[:border].astype(BF16)
-    d_top[0, :, dim:] = dv_s[:border].astype(BF16)
-    d_bottom[0, :, :dim] = dk_s[border + tokens :].astype(BF16)
-    d_bottom[0, :, dim:] = dv_s[border + tokens :].astype(BF16)
-
-
-def attend_backward(first, q, k, v, d_att, logs, deltas, height, width):
+
+    @pl.when(image == images - 1)
+    def _():
+        band = lax.axis_index("band")
+        count = above.shape[0]
+
+        @pl.when(band > 0)
+        def _():
+            for at in range(count):
+                to_above(at).wait_send()
+                to_below(at).wait_recv()
+
+        @pl.when(band < bands - 1)
+        def _():
+            for at in range(count):
+                to_below(at).wait_send()
+                to_above(at).wait_recv()
+
+        @pl.when(band == 0)
+        def _():
+            d_top[...] = jnp.zeros_like(d_top)
+            copy = empty(d_top, above)
+            copy.start()
+            copy.wait()
+
+        @pl.when(band == bands - 1)
+        def _():
+            d_bottom[...] = jnp.zeros_like(d_bottom)
+            copy = empty(d_bottom, below)
+            copy.start()
+            copy.wait()
+
+        steps[-1]()
+
+
+def attend_backward(
+    first, q, k, v, d_att, logs, deltas, height, width, devices, bands, grads, firsts, collective
+):
+    splits = [column_split(g.shape[1], start_col) for g, start_col in zip(grads, firsts)]
+    shapes = grad_shapes(devices, grads)
     images, tokens, dim = q.shape
     extended = k.shape[1]
     border = (extended - tokens) // 2
     block = 2 * width
     keys = (2 * RADIUS + 2) * width
     image = lambda rows, cols: pl.BlockSpec((1, rows, cols), lambda i: (i, 0, 0))
-    return pl.pallas_call(
-        functools.partial(attend_back_kernel, height, width),
+    whole = lambda shape: pl.BlockSpec(shape, lambda i: (0,) * len(shape))
+    hbm = pl.BlockSpec(memory_space=pl.ANY)
+    slices = [(s[2] // 2, s[3]) for s in shapes]
+    outs = pl.pallas_call(
+        functools.partial(attend_back_kernel, height, width, images, devices, bands, splits),
         grid=(images,),
         in_specs=[
             pl.BlockSpec(memory_space=pltpu.SMEM),
             image(tokens, dim), image(extended, dim), image(extended, dim), image(tokens, dim),
-            image(tokens, 128), image(tokens, 128),
+            image(tokens, 128), image(tokens, 128), *[hbm for _ in grads],
         ],
         out_specs=[
-            image(tokens, dim), image(tokens, dim), image(tokens, dim),
-            image(border, 2 * dim), image(border, 2 * dim),
+            image(tokens, dim), image(tokens, dim), image(tokens, dim), hbm, hbm,
+            *[whole(s) for s in slices],
         ],
         out_shape=[
             jax.ShapeDtypeStruct((images, tokens, dim), F32),
@@ -992,15 +1102,25 @@
             jax.ShapeDtypeStruct((images, tokens, dim), F32),
             jax.ShapeDtypeStruct((images, border, 2 * dim), BF16),
             jax.ShapeDtypeStruct((images, border, 2 * dim), BF16),
+            *[jax.ShapeDtypeStruct(s, F32) for s in slices],
         ],
         scratch_shapes=[
             pltpu.VMEM((tokens // block, keys, 128), BF16),
             pltpu.VMEM((extended, dim), F32),
             pltpu.VMEM((extended, dim), F32),
-        ],
-        compiler_params=pltpu.CompilerParams(vmem_limit_bytes=VMEM_LIMIT),
+            pltpu.VMEM((images, border, 2 * dim), BF16),
+            pltpu.VMEM((images, border, 2 * dim), BF16),
+            pltpu.SemaphoreType.DMA((2, images)),
+            pltpu.SemaphoreType.DMA((2, images)),
+            pltpu.SemaphoreType.DMA((1,)),
+            *scatter_scratch(devices, shapes),
+        ],
+        compiler_params=pltpu.CompilerParams(
+            collective_id=collective, has_side_effects=True, vmem_limit_bytes=VMEM_LIMIT
+        ),
         name="attend_backward",
-    )(first, q, k, v, d_att, logs, deltas)
+    )(first, q, k, v, d_att, logs, deltas, *[g.reshape(s) for g, s in zip(grads, shapes)])
+    return outs[:5], outs[5:]
 
 
 def project_back_kernel(
@@ -1147,12 +1267,6 @@
     return [jnp.asarray(t, BF16) for t in (pool, spread, expand)]
 
 
-def shifted(x, by):
-    devices = lax.axis_size("band")
-    pairs = [(i, i + by) for i in range(devices) if 0 <= i + by < devices]
-    return lax.ppermute(x, "band", pairs)
-
-
 def shards(
     tokens_in, cond, loss_weight, cotangent, norm1_map, qkv_weight, attn_scale, out_weight,
     norm2_map, up_weight, down_weight,
@@ -1185,23 +1299,22 @@
     x = tokens_in.reshape(images, tokens, dim)
     scale_one = scales[:images, None, :dim]
     scale_two = scales[:images, None, dim:]
-    w_up_out, w_down, map_rows = fetch(
-        devices, [jnp.concatenate([up_weight, out_weight], axis=1), down_weight, maps], [1920, 128, 384], 1
-    )
     factor = jnp.repeat(jnp.sqrt(attn_scale), head_size)[None, :]
     inverse_scale = jnp.repeat(1.0 / attn_scale, head_size)[None, :]
 
-    att, q, k, v, inverse, logs = attend_forward(
-        first, x, top, bottom, scale_one, w_qkv, factor, pool, turns, height, width
+    up_out = jnp.concatenate([up_weight, out_weight], axis=1)
+    (att, q, k, v, inverse, logs), (w_up_out, w_down, map_rows) = attend_forward(
+        first, x, top, bottom, scale_one, w_qkv, factor, pool, turns, height, width,
+        devices, bands, [up_out, down_weight, maps], [1920, 128, 384], 1,
     )
     weight_rows = jnp.broadcast_to(loss_weight[:, None, None], (images, 1, dim))
     result, d_residual, d_att, deltas, grad_up_out, grad_down, d_scale_two = feed(
         x, att, cotangent.reshape(images, tokens, dim), weight_rows, scale_two, w_up_out, w_down, spread
     )
-    grad_up_out, grad_down = settle(devices, [grad_up_out, grad_down], [1920, 128], 2)
-    d_q, d_k, d_v, d_top, d_bottom = attend_backward(first, q, k, v, d_att, logs, deltas, height, width)
-    below = shifted(d_top, -1)
-    above = shifted(d_bottom, 1)
+    (d_q, d_k, d_v, above, below), (grad_up_out, grad_down) = attend_backward(
+        first, q, k, v, d_att, logs, deltas, height, width,
+        devices, bands, [grad_up_out, grad_down], [1920, 128], 2,
+    )
     grad_input, grad_qkv, d_scale_one, d_attn = project_backward(
         x, scale_one, q, k, d_q, d_k, d_v, above, below, inverse, d_residual, w_qkv, inverse_scale,
         pool, expand, turns,

time: 352 us -> 288 us (0.82)
  Pallas kernels: 326 us -> 268 us
    pallas_call x4 -> x2, Pallas kernels: 172 us -> 115 us  [the longest x1 59.3 us: attend_backward(): pl.pallas_call(functools.partial(attend_back_kernel, height, width, image...]
  transfers between devices with their start and end apart: 2 -> 0, of which waited for: 0 -> 0; matrix products, arithmetic and copies ran while one was open for 1% -> 0% of each run, Pallas kernels for 13% -> 0%
where the time goes in v2:
time: 288 us
  Pallas kernels  268 us (93%)
  local copies, waits for them, and re-layouts  16.5 us (6%)
    pallas_call x1, Pallas kernels, feed(): pl.pallas_call(feed_kernel, grid=(images, tokens // tile), in_specs=[bloc...  74.2 us
    pallas_call x1, Pallas kernels, attend_backward(): pl.pallas_call(functools.partial(attend_back_kernel, height, width, image...  59.3 us
    pallas_call x1, Pallas kernels, attend_forward(): pl.pallas_call(functools.partial(attend_kernel, height, width, images, de...  55.7 us
    pallas_call x1, Pallas kernels, open_layer(): pl.pallas_call(functools.partial(open_kernel, devices, bands, [column_spl...  29.9 us
    pallas_call x1, Pallas kernels, close_layer(): pl.pallas_call(functools.partial(close_kernel, devices, bands, [column_sp...  24.8 us
    pallas_call x1, Pallas kernels, project_backward(): pl.pallas_call(project_back_kernel, grid=(images,), in_specs=[image(token...  24.5 us

profile of v2, /device:TPU:0, one launch (start us, length us, event | category | flops | bytes accessed | tf_op | source)
XLA Modules:
  0.0 287.6 jit_solution(134858843625178812)
XLA Ops:
  0.7 1.4 constant_dynamic-slice_fusion
  2.1 0.7 constant_dynamic-update-slice_fusion.1
  2.8 0.7 constant_dynamic-update-slice_fusion.maps.refs_14_
  3.5 1.3 pad.8.cond
  4.8 29.9 %open_layer.1 = (bf16[8,2,24,1152]{3,2,1,0:T(8,128)(2,1)}, f32[8,768]{1,0:T(8,128)}, bf16[64,128]{1,0:T(8,128)(2,1)}, bf16[3,3,64,384]{3,2,1,0:T(8,128)(2,1)}, bf16[3,3,64,384]{3,2,1,0:T(8,128)(2,1)}) custom-call(bf16[12,1152]{1,0:T(8,128)(2,1)} %qkv.1, bf16[8,768]{1,0:T(8,128)(2,1)} %pad.8.cond, bf16[24,768]{1,0:T(8,128)(2,1)} %copy-done, ...), custom_call_target="tpu_custom_call" | custom-call | tf_op jit(solution)/shard_map/open_layer/pallas_call | solution.py:540
  34.7 0.7 fusion.1
  36.1 0.6 broadcast_in_dim_reshape.6.refs_6_
  36.8 0.7 pad_maximum_fusion.refs_12_
  37.4 55.7 %attend_forward.1 = (bf16[3,1024,384]{2,1,0:T(8,128)(2,1)}, bf16[3,1024,384]{2,1,0:T(8,128)(2,1)}, bf16[3,1408,384]{2,1,0:T(8,128)(2,1)}, bf16[3,1408,384]{2,1,0...) custom-call(s32[1]{0:T(128)} %bitcast.1.refs_0_, ...), custom_call_target="tpu_custom_call" | custom-call | tf_op jit(solution)/shard_map/attend_forward/pallas_call | solution.py:773
  93.7 0.7 broadcast_in_dim.20.weight
  94.4 74.2 %feed.1 = (bf16[3,1024,384]{2,1,0:T(8,128)(2,1)}, f32[3,1024,384]{2,1,0:T(8,128)}, bf16[3,1024,384]{2,1,0:T(8,128)(2,1)}, bf16[3,1024,128]{2,1,0:T(8,128)(2,1)},...) custom-call(bf16[3,1024,384]{2,1,0:T(8,128)(2,1)} %bitcast.22, ...), custom_call_target="tpu_custom_call" | custom-call | tf_op jit(solution)/shard_map/feed/pallas_call | solution.py:902
  168.6 59.3 %attend_backward.1 = (f32[3,1024,384]{2,1,0:T(8,128)}, f32[3,1024,384]{2,1,0:T(8,128)}, f32[3,1024,384]{2,1,0:T(8,128)}, bf16[3,192,768]{2,1,0:T(8,128)(2,1)}, b...) custom-call(s32[1]{0:T(128)} %bitcast.1.refs_0_, ...), custom_call_target="tpu_custom_call" | custom-call | tf_op jit(solution)/shard_map/attend_backward/pallas_call | solution.py:1087
  227.9 0.6 broadcast_in_dim_reshape.7.inverse_scale
  228.6 24.5 %project_backward.1 = (f32[3,1024,384]{2,1,0:T(8,128)}, bf16[384,1152]{1,0:T(8,128)(2,1)}, f32[3,1,384]{2,1,0:T(1,128)}, f32[1,384]{1,0:T(1,128)}) custom-call(bf16[3,1024,384]{2,1,0:T(8,128)(2,1)} %bitcast.23, f32[3,1,384]{2,1,0:T(1,128)} %broadcast_in_dim.18.refs_4_.scale, bf16[3,1024,384]{2,1,0:T(8,128)(2,1)} %get-tuple-element.54.refs_1_.q, ...), custom_call_target="tpu_custom_call" | custom-call | tf_op jit(solution)/shard_map/project_backward/pallas_call | solution.py:1212
  253.1 0.7 copy.36
  253.8 1.3 select_maximum_fusion.sums
  255.1 24.8 %close_layer.1 = (f32[12,1152]{1,0:T(8,128)}, f32[24,768]{1,0:T(8,128)}, f32[8,768]{1,0:T(8,128)}, f32[8,768]{1,0:T(8,128)}) custom-call(bf16[8,2,24,1152]{3,2,1,0:T(8,128)(2,1)} %bitcast.33, f32[8,768]{1,0:T(8,128)} %select_maximum_fusion.sums, bf16[64,128]{1,0:T(8,128)(2,1)} %get-tuple-element.74.chosen, bf16[768,768]{1,0:T(8,128)(2,1)} %bitcast.32), custom_call_target="tpu_custom_call" | custom-call | tf_op jit(solution)/shard_map/close_layer/pallas_call | solution.py:624
  279.9 1.4 fusion
  281.4 1.3 slice.29
  282.7 0.7 slice_reduce_fusion
  284.1 0.7 slice.35
  284.8 0.6 slice.33
  285.4 1.5 copy.40
  286.9 0.6 copy.41
  (25 shorter events, 2.1 us)
Async XLA Ops:
  0.6 35.4 %copy-start.7 = (f32[6]{0:T(128)S(1)}, f32[6]{0:T(128)}, u32[]{:S(2)}) copy-start(f32[6]{0:T(128)} %param.24) | copy-start | bytes 76
  0.7 36.1 %copy-start.4 = (bf16[12,384]{1,0:T(8,128)(2,1)S(1)}, bf16[12,384]{1,0:T(8,128)(2,1)}, u32[]{:S(2)}) copy-start(bf16[12,384]{1,0:T(8,128)(2,1)} %param.25) | copy-start | bytes 27652
  0.7 36.1 %copy-start.2 = (bf16[12,3072]{1,0:T(8,128)(2,1)S(1)}, bf16[12,3072]{1,0:T(8,128)(2,1)}, u32[]{:S(2)}) copy-start(bf16[12,3072]{1,0:T(8,128)(2,1)} %param.27) | copy-start | bytes 221188
  3.5 1.3 copy-start
  36.8 56.9 %copy-start.6 = (f32[3]{0:T(128)S(1)}, f32[3]{0:T(128)}, u32[]{:S(2)}) copy-start(f32[3]{0:T(128)} %param.20) | copy-start | bytes 40
  228.6 25.2 %copy-start.5 = (f32[3,1,384]{2,1,0:T(1,128)S(1)}, f32[3,1,384]{2,1,0:T(1,128)}, u32[]{:S(2)}) copy-start(f32[3,1,384]{2,1,0:T(1,128)} %get-tuple-element.72) | copy-start | bytes 13828
  253.1 31.0 %copy-start.1 = (f32[12,3456]{1,0:T(8,128)S(1)}, f32[12,3456]{1,0:T(8,128)}, u32[]{:S(2)}) copy-start(f32[12,3456]{1,0:T(8,128)} %get-tuple-element.80) | copy-start | bytes 497668
  253.1 33.9 %copy-start.3 = (f32[48,384]{1,0:T(8,128)S(1)}, f32[48,384]{1,0:T(8,128)}, u32[]{:S(2)}) copy-start(f32[48,384]{1,0:T(8,128)} %get-tuple-element.109) | copy-start | bytes 221188

commit v3 on v0

v3 whole, which is shorter than its diff:
```python
import functools
import math

import jax
import jax.numpy as jnp
import numpy as np
from jax import lax
from jax.experimental import pallas as pl
from jax.experimental.pallas import tpu as pltpu
from jax.sharding import PartitionSpec as P

KERNEL = 7
RADIUS = KERNEL // 2
NORM_EPS = 1e-06
MASKED = -10000.0
F32 = jnp.float32
BF16 = jnp.bfloat16
VMEM_LIMIT = 61900 << 10


def nn(a, b):
    return lax.dot_general(a, b, (((1,), (0,)), ((), ())), preferred_element_type=F32)


def nt(a, b):
    return lax.dot_general(a, b, (((1,), (1,)), ((), ())), preferred_element_type=F32)


def tn(a, b):
    return lax.dot_general(a, b, (((0,), (0,)), ((), ())), preferred_element_type=F32)


def lanes(shape):
    return lax.broadcasted_iota(jnp.int32, shape, len(shape) - 1)


def halves(value):
    high = value.astype(BF16)
    low = (value - high.astype(F32)).astype(BF16)
    return high, low


def thirds(value):
    high = value.astype(BF16)
    rest = value - high.astype(F32)
    middle = rest.astype(BF16)
    return high.astype(F32), middle.astype(F32), rest - middle.astype(F32)


def head_sums(value, pool):
    high, low = halves(value)
    return nn(jnp.concatenate([high, low], axis=1), pool)


def swapped(value):
    first = (lanes(value.shape) & 8) == 0
    return jnp.where(first, pltpu.roll(value, 120, 1), pltpu.roll(value, 8, 1))


def normed_rows(values, scale):
    inverse = lax.rsqrt(jnp.mean(values * values, axis=-1, keepdims=True) + NORM_EPS)
    return values * scale * inverse, inverse


def build_turns(first_row, crow, srow, ccol, scol, cos_s, sin_s):
    for row in range(cos_s.shape[0]):
        cos_s[row] = crow[pl.ds(first_row + row, 1)] * ccol[...]
        sin_s[row] = srow[pl.ds(first_row + row, 1)] + scol[...]


QUERY_ROWS = 4


def tile_columns(width):
    half = width // 2
    wide = half + 8
    return half, wide, (0, width - wide)


def build_key_features(first_row, height, width, feat_s):
    half, wide, starts = tile_columns(width)
    keys = feat_s.shape[1]
    lane = lanes((keys, 128))
    index = lax.broadcasted_iota(jnp.int32, (keys, 128), 0)
    row = index // wide
    step = row - (lane - half)
    row_lane = (lane >= half) & (lane < half + QUERY_ROWS)
    for tile in range(feat_s.shape[0]):
        group, side = tile // 2, tile % 2
        col = index - row * wide + starts[side] - side * half
        place = first_row + QUERY_ROWS * group - RADIUS + row
        near_col = jnp.abs(col - lane) <= RADIUS
        near_row = (step >= 0) & (step <= 2 * RADIUS) & (place >= 0) & (place < height)
        seen = jnp.where(lane < half, jnp.where(near_col, 0.0, MASKED), 0.0)
        seen = jnp.where(row_lane, jnp.where(near_row, 0.0, MASKED), seen)
        feat_s[tile] = seen.astype(BF16)


def query_features(width):
    half = width // 2
    shape = (QUERY_ROWS * half, 128)
    lane = lanes(shape)
    index = lax.broadcasted_iota(jnp.int32, shape, 0)
    row = index // half
    col = index - row * half
    hit = ((lane < half) & (lane == col)) | ((lane >= half) & (lane - half == row))
    return jnp.where(hit, 1.0, 0.0).astype(BF16)


def block_diagonal(tile):
    low = lanes(tile.shape) < 64
    zero = jnp.zeros_like(tile)
    return jnp.concatenate([jnp.where(low, tile, zero), jnp.where(low, zero, tile)], axis=0)


MESH = pl.DeviceIdType.MESH


def flip(index, bit):
    return index + bit * (1 - 2 * ((index // bit) % 2))


def relatives(index, bits):
    found = [index]
    for bit in bits:
        found = found + [flip(i, bit) for i in found]
    return found


class Copies:
    def __init__(self, send, recv):
        self.send, self.recv, self.count = send, recv, 0

    def reserve(self, count):
        self.count += count
        return self.count - count

    def batch(self, count, build):
        first = self.reserve(count)

        def made():
            entries = build()
            assert len(entries) == count
            return [self.one(first + i, *entry) for i, entry in enumerate(entries)]

        return made

    def one(self, slot, source, target, peer):
        return pltpu.make_async_remote_copy(
            src_ref=source,
            dst_ref=target,
            send_sem=self.send.at[slot],
            recv_sem=self.recv.at[slot],
            device_id=peer,
            device_id_type=MESH,
        )


def start(*batches):
    for batch in batches:
        for copy in batch():
            copy.start()


def arrive(*batches):
    for batch in batches:
        for copy in batch():
            copy.wait_recv()


def depart(*batches):
    for batch in batches:
        for copy in batch():
            copy.wait_send()


def run(*steps):
    def step():
        for inner in steps:
            inner()

    return step


def here():
    return lax.axis_index("dp"), lax.axis_index("band")


def mesh_bits(devices):
    return [1 << i for i in range(devices.bit_length() - 1)]


def ways(bits):
    far = bits[1:]
    return (far[::-1], far)


def exchange_peers(devices, bands):
    dp, band = here()
    return [(dp, (band + d) % bands) for d in range(1, bands)] + [
        (flip(dp, bit), band) for bit in mesh_bits(devices)
    ]


def column_split(columns, first):
    return ((0, first), (first, columns - first))


def gather_steps(devices, bands, copies, local, shards, boxes, blocks, outs, splits, waited=False):
    bits = mesh_bits(devices)
    n = len(shards)
    stages = len(bits) - 1
    each = range(n)

    def band_entries():
        dp, band = here()
        return [
            (boxes[a].at[band], boxes[a].at[band], (dp, (band + d) % bands))
            for d in range(1, bands)
            for a in each
        ]

    def core_entries():
        dp, band = here()
        return [(blocks[a], outs[a].at[dp], (flip(dp, 1), band)) for a in each]

    def ring_entries(k, forward):
        dp, band = here()
        entries = []
        for way, order in enumerate(ways(bits)):
            source = flip(dp, order[k]) if forward else dp
            peer = flip(dp, 1) if forward else flip(dp, order[k])
            for index in relatives(source, order[:k]):
                for a in each:
                    columns = pl.ds(*splits[a][way])
                    cut = outs[a].at[index, :, columns]
                    held = blocks[a].at[:, columns] if k == 0 and not forward else cut
                    entries.append((held, cut, (peer, band)))
        return entries

    along = copies.batch(n * (bands - 1), band_entries)
    core = copies.batch(n, core_entries)
    rings = [copies.batch(2 * n << k, functools.partial(ring_entries, k, False)) for k in range(stages)]
    fresh = [copies.batch(2 * n << k, functools.partial(ring_entries, k, True)) for k in range(stages)]

    def own():
        dp, _ = here()
        return [pltpu.make_async_copy(blocks[a], outs[a].at[dp], local.at[a]) for a in each]

    def begin():
        _, band = here()
        for a in each:
            at = 0
            for part in shards[a]:
                boxes[a][band, :, at : at + part.shape[1]] = part[...]
                at += part.shape[1]
        start(along)

    def assemble():
        if not waited:
            arrive(along)
        for a in each:
            rows = boxes[a].shape[1]
            for b in range(bands):
                blocks[a][b * rows : (b + 1) * rows] = boxes[a][b]
        start(rings[0], own, core)

    def spread(k):
        def step():
            if k == 1:
                for copy in own():
                    copy.wait()
            arrive(rings[k - 1])
            if k < stages:
                start(rings[k])
            start(fresh[k - 1])

        return step

    def finish():
        arrive(core, *fresh)
        depart(along, core, *rings, *fresh)

    if waited:
        begin = (begin, functools.partial(arrive, along))
    return [begin, assemble, *[spread(k) for k in range(1, stages + 1)], finish]


def gather_copies(devices, bands, n):
    stages = devices.bit_length() - 2
    return n * bands + sum(4 * n << k for k in range(stages))


def gather_shape(devices, bands, shard):
    return (devices, bands * shard.shape[0], shard.shape[1])


def gather_scratch(devices, bands, shards):
    count = gather_copies(devices, bands, len(shards))
    return [
        *[pltpu.VMEM((bands,) + s.shape, s.dtype) for s in shards],
        *[pltpu.VMEM(gather_shape(devices, bands, s)[1:], s.dtype) for s in shards],
        pltpu.SemaphoreType.DMA((count,)),
        pltpu.SemaphoreType.DMA((count,)),
        pltpu.SemaphoreType.DMA((len(shards),)),
    ]


def add_into(target, index, cut, addend):
    columns = pl.ds(*cut)
    total = target[index, :, columns].astype(F32) + addend(columns).astype(F32)
    target[index, :, columns] = total.astype(BF16)


def scatter_steps(devices, bands, copies, grads, inbox, pieces, arrivals, outs, splits):
    bits = mesh_bits(devices)
    n = len(grads)
    stages = len(bits) - 1
    each = range(n)
    base = 1 << stages
    spots = [base + sum(1 << (stages - 1 - j) for j in range(k)) for k in range(stages)]

    def core_entries():
        dp, band = here()
        peer = flip(dp, 1)
        return [
            (grads[a].at[index], inbox[a].at[k], (peer, band))
            for k, index in enumerate(relatives(peer, bits[1:]))
            for a in each
        ]

    def ring_entries(k):
        dp, band = here()
        entries = []
        for way, order in enumerate(ways(bits)):
            peer = flip(dp, order[k])
            for j, index in enumerate(relatives(peer, order[k + 1 :])):
                for a in each:
                    columns = pl.ds(*splits[a][way])
                    source = grads[a].at[index, :, columns]
                    entries.append((source, inbox[a].at[spots[k] + j, :, columns], (peer, band)))
        return entries

    def band_entries():
        dp, band = here()
        peers = [(band + d) % bands for d in range(1, bands)]
        return [(pieces[a].at[peer], arrivals[a].at[band], (dp, peer)) for peer in peers for a in each]

    core = copies.batch(n << stages, core_entries)
    rings = [
        copies.batch(2 * n << (stages - 1 - k), functools.partial(ring_entries, k)) for k in range(stages)
    ]
    along = copies.batch(n * (bands - 1), band_entries)

    def add_core():
        arrive(core)
        dp, _ = here()
        for k, index in enumerate(relatives(dp, bits[1:])):
            for a in each:
                whole = (0, sum(width for _, width in splits[a]))
                add_into(grads[a], index, whole, lambda columns: inbox[a][k])

    def add_ring(k):
        arrive(rings[k])
        dp, _ = here()
        for way, order in enumerate(ways(bits)):
            for j, index in enumerate(relatives(dp, order[k + 1 :])):
                for a in each:
                    add_into(
                        grads[a], index, splits[a][way],
                        lambda columns: inbox[a][spots[k] + j, :, columns],
                    )

    def cut():
        dp, _ = here()
        for a in each:
            rows = pieces[a].shape[1]
            for b in range(bands):
                pieces[a][b] = grads[a][dp, b * rows : (b + 1) * rows]

    def finish():
        arrive(along)
        _, band = here()
        for a in each:
            total = pieces[a][band].astype(F32)
            for d in range(1, bands):
                total = total + arrivals[a][(band + d) % bands].astype(F32)
            at = 0
            for part in outs[a]:
                part[...] = total[:, at : at + part.shape[1]]
                at += part.shape[1]
        depart(core, *rings, along)

    adds = [add_core, *[functools.partial(add_ring, k) for k in range(stages)]]
    adds[-1] = run(adds[-1], cut)
    steps = [run(add, functools.partial(start, send)) for add, send in zip(adds, [*rings, along])]
    return [functools.partial(start, core), *steps, finish]


def scatter_copies(devices, bands, n):
    stages = devices.bit_length() - 2
    return (n << stages) + sum(2 * n << k for k in range(stages)) + n * (bands - 1)


def scatter_scratch(devices, bands, shapes):
    count = scatter_copies(devices, bands, len(shapes))
    return [
        *[pltpu.VMEM(s, BF16) for s in shapes],
        *[pltpu.VMEM((devices - 1,) + s[1:], BF16) for s in shapes],
        *[pltpu.VMEM((bands, s[1] // bands, s[2]), BF16) for s in shapes],
        *[pltpu.VMEM((bands, s[1] // bands, s[2]), BF16) for s in shapes],
        pltpu.SemaphoreType.DMA((count,)),
        pltpu.SemaphoreType.DMA((count,)),
    ]


def grad_shape(devices, bands, rows, columns):
    return (devices, rows // devices, columns)


def spaced(moments, steps):
    first, reach, count = moments[0], moments[-1] - moments[0], len(steps) - 1
    if count + 1 != len(moments):
        moments = [first + reach * k // count for k in range(count + 1)]
    return list(zip(moments, steps))


def hooked(moment, hooks):
    for when, hook in hooks:
        pl.when(moment == when)(hook)


def hail(peers):
    barrier = pltpu.get_barrier_semaphore()
    for peer in peers:
        pl.semaphore_signal(barrier, inc=1, device_id=peer, device_id_type=MESH)
    return lambda: pl.semaphore_wait(barrier, len(peers))


def every_peer(devices, bands):
    dp, band = here()
    return [(dp, (band + d) % bands) for d in range(1, bands)] + [
        ((dp + d) % devices, band) for d in range(1, devices)
    ]


def head_row(attn, columns):
    head = lanes((1, columns)) // 64
    row = jnp.zeros((1, columns), F32)
    for h in range(attn.shape[0]):
        row = jnp.where(head == h, attn[h], row)
    return row


def split_refs(refs, *counts):
    parts, at = [], 0
    for count in counts:
        parts.append(refs[at] if count is None else refs[at : at + count])
        at += 1 if count is None else count
    assert at == len(refs)
    return parts


def attend_kernel(height, images, devices, bands, splits, qkv_split, map_split, *refs):
    n = len(splits)
    (
        x, tokens, attn, cond, map_one, map_two, pool, crow, srow, ccol, scol, qkv, up, out, down,
        att, q_out, k_out, v_out, inverse_out, log_out, w_qkv, scales, chosen, map_rows, outs,
        cos_s, sin_s, feat_s, kf_s, vf_s, top, bottom, conds, padded, partial, part_in, qkv_all,
        small_send, small_recv, halo_send, halo_recv,
        qkv_box, qkv_block, qkv_send, qkv_recv, qkv_local,
        map_box, map_block, map_send, map_recv, map_local,
        boxes, blocks, send, recv, local,
    ) = split_refs(
        refs, *[None] * 15, *[None] * 10, n, *[None] * 16, *[None] * 10, n, n, *[None] * 3
    )
    image = pl.program_id(0)
    _, band_rows, width, dim = x.shape
    pairs = dim // 128
    border = top.shape[1]
    groups = band_rows // QUERY_ROWS
    half, wide, starts = tile_columns(width)
    window = QUERY_ROWS + 2 * RADIUS
    queries = QUERY_ROWS * half
    dp, band = here()
    around = [((dp + d) % devices, band) for d in range(1, devices)]
    shards = [[up, out], [down]]
    steps = gather_steps(devices, bands, Copies(send, recv), local, shards, boxes, blocks, outs, splits)
    map_steps = gather_steps(
        devices, bands, Copies(map_send, map_recv), map_local, [[map_one, map_two]], [map_box], [map_block],
        [map_rows], [map_split], waited=True,
    )
    both_steps = [run(one, two) for one, two in zip(steps[1:], map_steps[1:])]
    hooks = spaced((0, 4, 10), both_steps[:-1])

    def upward(at):
        dp, band = here()
        return pltpu.make_async_remote_copy(
            src_ref=tokens.at[at, pl.ds(band_rows - border, border)], dst_ref=top.at[at],
            send_sem=halo_send.at[0, at], recv_sem=halo_recv.at[0, at],
            device_id=(dp, (band + 1) % bands), device_id_type=MESH,
        )

    def downward(at):
        dp, band = here()
        return pltpu.make_async_remote_copy(
            src_ref=tokens.at[at, pl.ds(0, border)], dst_ref=bottom.at[at],
            send_sem=halo_send.at[1, at], recv_sem=halo_recv.at[1, at],
            device_id=(dp, (band + bands - 1) % bands), device_id_type=MESH,
        )

    def send_halos(which):
        _, band = here()

        @pl.when(band < bands - 1)
        def _():
            for at in which:
                upward(at).start()

        @pl.when(band > 0)
        def _():
            for at in which:
                downward(at).start()

    @pl.when(image == 0)
    def _():
        conds[...] = jnp.zeros_like(conds)
        wait = hail(every_peer(devices, bands))
        conds[dp, : cond.shape[0]] = cond[...]
        padded[...] = jnp.zeros_like(padded)
        own = gather_steps(
            devices, bands, Copies(qkv_send, qkv_recv), qkv_local, [[qkv]], [qkv_box], [qkv_block],
            [qkv_all], [qkv_split],
        )
        small = Copies(small_send, small_recv)
        first = small.batch(devices - 1, lambda: [(conds.at[dp], conds.at[dp], peer) for peer in around])
        second = small.batch(
            devices - 1, lambda: [(partial.at[peer[0]], part_in.at[dp], peer) for peer in around]
        )
        wait()
        own[0]()
        map_steps[0][0]()
        start(first)
        first_row = band * band_rows
        build_turns(first_row, crow, srow, ccol, scol, cos_s, sin_s)
        build_key_features(first_row, height, width, feat_s)
        own[1]()
        send_halos([0])
        steps[0]()
        rows = map_box.shape[1]
        map_steps[0][1]()
        for b in range(bands):
            padded[b * rows : (b + 1) * rows] = map_box[b]
        arrive(first)
        offset = dp * bands * rows
        lane = lanes((conds.shape[2], 128))
        hit = (lax.broadcasted_iota(jnp.int32, lane.shape, 0) == lane + offset) & (lane < bands * rows)
        picked = nn(conds[...].reshape(-1, conds.shape[2]), jnp.where(hit, 1.0, 0.0).astype(BF16))
        chosen[...] = picked.astype(BF16)
        partial[...] = nn(picked.astype(BF16), padded[...]).reshape(partial.shape)
        start(second)
        for step in own[2:-1]:
            step()
        send_halos(range(1, images))

        @pl.when(band == 0)
        def _():
            top[...] = jnp.zeros_like(top)

        @pl.when(band == bands - 1)
        def _():
            bottom[...] = jnp.zeros_like(bottom)

        arrive(second)
        total = partial[dp]
        for peer in around:
            total = total + part_in[peer[0]]
        scales[...] = 1.0 + total
        own[-1]()
        depart(first, second)
        tall = qkv_all.shape[1]
        for d in range(devices):
            w_qkv[d * tall : (d + 1) * tall] = qkv_all[d]

    row_scale = scales[pl.ds(image, 1), :dim]
    factor = jnp.sqrt(head_row(attn, dim))
    part = (lanes((1, 128)) & 63).astype(F32)

    def shaped(raw, p, cos, sin):
        fr = factor[:, p * 128 : (p + 1) * 128] * lax.rsqrt(head_sums(raw * raw, pool[...]) + NORM_EPS)
        unit = raw * fr
        return unit * cos + swapped(unit) * sin, fr

    def keep(spot, cut, key, value):
        shape = (spot.size, width, 128)
        key_low, value_low = key.astype(BF16), value.astype(BF16)
        k_out[0, spot, :, cut] = key_low.reshape(shape)
        v_out[0, spot, :, cut] = value_low.reshape(shape)
        kf_s[spot, :, cut] = key_low.astype(F32).reshape(shape)
        vf_s[spot, :, cut] = value_low.astype(F32).reshape(shape)

    def turns_at(spot):
        return [t[spot].reshape(spot.size * width, 128) for t in (cos_s, sin_s)]

    def halo(ref, at):
        values = ref[image].reshape(border * width, dim)
        normed, _ = normed_rows(values.astype(F32), row_scale)
        mixed = nn(normed.astype(BF16), w_qkv[:, dim:])
        spot = pl.ds(at, border)
        cos, sin = turns_at(spot)
        for p in range(pairs):
            cut = slice(p * 128, (p + 1) * 128)
            turned, _ = shaped(mixed[:, cut], p, cos, sin)
            keep(spot, cut, turned, mixed[:, dim + p * 128 : dim + (p + 1) * 128])

    chunk = QUERY_ROWS * width

    def lift(i):
        own = pl.ds(i * QUERY_ROWS, QUERY_ROWS)
        normed, _ = normed_rows(x[0, own].reshape(chunk, dim).astype(F32), row_scale)
        return nn(normed.astype(BF16), w_qkv[...])

    def shape_rows(i, mixed):
        own = pl.ds(i * QUERY_ROWS, QUERY_ROWS)
        spot = pl.ds(border + i * QUERY_ROWS, QUERY_ROWS)
        cos, sin = turns_at(spot)
        kept = jnp.zeros((chunk, 128), F32)
        raws = [mixed[:, c * 128 : (c + 1) * 128] for c in range(3 * pairs)]
        totals = [head_sums(raw * raw, pool[...]) for raw in raws[: 2 * pairs]]
        for p in range(pairs):
            cut = slice(p * 128, (p + 1) * 128)
            turned = []
            for kind in range(2):
                fr = factor[:, cut] * lax.rsqrt(totals[kind * pairs + p] + NORM_EPS)
                unit = raws[kind * pairs + p] * fr
                turned.append(unit * cos + swapped(unit) * sin)
                kept = jnp.where(part == 2 * p + kind, fr, kept)
            q_out[0, own, :, cut] = turned[0].astype(BF16).reshape(QUERY_ROWS, width, 128)
            keep(spot, cut, turned[1], raws[2 * pairs + p])
        inverse_out[0, own] = kept.reshape(QUERY_ROWS, width, 128)

    ready = lift(0)
    for i in range(groups):
        mixed = ready
        if i + 1 < groups:
            ready = lift(i + 1)
        shape_rows(i, mixed)

    @pl.when(band > 0)
    def _():
        downward(image).wait_send()
        upward(image).wait_recv()

    @pl.when(band < bands - 1)
    def _():
        upward(image).wait_send()
        downward(image).wait_recv()

    halo(top, 0)
    halo(bottom, border + band_rows)

    ask = query_features(width)
    ask = jnp.concatenate([ask, ask], axis=0)

    def attend(g, _):
        own = pl.ds(g * QUERY_ROWS, QUERY_ROWS)
        seen = pl.ds(g * QUERY_ROWS, window)

        def score(side, p):
            mine = slice(side * half, (side + 1) * half)
            theirs = slice(starts[side], starts[side] + wide)
            cut = slice(p * 128, (p + 1) * 128)
            query = block_diagonal(q_out[0, own, mine, cut].reshape(queries, 128))
            key = kf_s[seen, theirs, cut].reshape(window * wide, 128).astype(BF16)
            wide_key = jnp.concatenate([key, feat_s[2 * g + side]], axis=1)
            return nt(wide_key, jnp.concatenate([query, ask], axis=1))

        def gather(side, p, weight, total):
            mine = slice(side * half, (side + 1) * half)
            theirs = slice(starts[side], starts[side] + wide)
            cut = slice(p * 128, (p + 1) * 128)
            value = vf_s[seen, theirs, cut].reshape(window * wide, 128).astype(BF16)
            mean = tn(value, weight) / total
            mean = jnp.concatenate([mean[:64, :queries], mean[64:, queries:]], axis=0)
            att[0, own, mine, cut] = mean.T.astype(BF16).reshape(QUERY_ROWS, half, 128)
            log_out[0, 2 * g + side, p : p + 1] = jnp.log(total)

        tiles = [(side, p) for side in range(2) for p in range(pairs)]
        ready, past = score(*tiles[0]), None
        for at, tile in enumerate(tiles):
            scores = ready
            if at + 1 < len(tiles):
                ready = score(*tiles[at + 1])
            if past is not None:
                gather(*past)
            weight = jnp.exp(scores)
            past = (*tile, weight.astype(BF16), jnp.sum(weight, axis=0, keepdims=True))
        gather(*past)
        hooked(image * groups + g, hooks)
        return 0

    lax.fori_loop(0, groups, attend, 0)

    @pl.when(image == images - 1)
    def _():
        both_steps[-1]()


def attend_forward(
    x, attn, cond, map_one, map_two, pool, turns, height, devices, bands, qkv, up, out, down, collective
):
    images, band_rows, width, dim = x.shape
    extended = band_rows + 2 * RADIUS
    groups = band_rows // QUERY_ROWS
    half, wide_columns, _ = tile_columns(width)
    keys = (QUERY_ROWS + 2 * RADIUS) * wide_columns
    wide, both = cond.shape[1], 2 * map_one.shape[1]
    kinds = [
        jax.ShapeDtypeStruct((up.shape[0], up.shape[1] + out.shape[1]), BF16),
        jax.ShapeDtypeStruct(down.shape, BF16),
    ]
    maps = jax.ShapeDtypeStruct((map_one.shape[0], both), BF16)
    splits = [column_split(kinds[0].shape[1], 1920), column_split(kinds[1].shape[1], 128)]
    small = 2 * (devices - 1)
    image = lambda *shape: pl.BlockSpec((1,) + shape, lambda i: (i,) + (0,) * len(shape))
    whole = lambda shape: pl.BlockSpec(shape, lambda i: (0,) * len(shape))
    hbm = pl.BlockSpec(memory_space=pl.ANY)
    inputs = [cond, map_one, map_two, pool, *turns, qkv, up, out, down]
    qkv_whole = (qkv.shape[0] * devices * bands, qkv.shape[1])
    outs = pl.pallas_call(
        functools.partial(
            attend_kernel, height, images, devices, bands, splits, column_split(qkv.shape[1], 640),
            column_split(both, 384),
        ),
        grid=(images,),
        in_specs=[
            image(band_rows, width, dim), hbm, pl.BlockSpec(memory_space=pltpu.SMEM),
            *[whole(a.shape) for a in inputs],
        ],
        out_specs=[
            image(band_rows, width, dim), image(band_rows, width, dim),
            image(extended, width, dim), image(extended, width, dim),
            image(band_rows, width, 128), image(2 * groups, 8, 2 * QUERY_ROWS * half),
            whole(qkv_whole), whole((8, both)), whole((devices * 8, 128)), hbm, *[hbm for _ in kinds],
        ],
        out_shape=[
            jax.ShapeDtypeStruct((images, band_rows, width, dim), BF16),
            jax.ShapeDtypeStruct((images, band_rows, width, dim), BF16),
            jax.ShapeDtypeStruct((images, extended, width, dim), BF16),
            jax.ShapeDtypeStruct((images, extended, width, dim), BF16),
            jax.ShapeDtypeStruct((images, band_rows, width, 128), F32),
            jax.ShapeDtypeStruct((images, 2 * groups, 8, 2 * QUERY_ROWS * half), F32),
            jax.ShapeDtypeStruct(qkv_whole, BF16),
            jax.ShapeDtypeStruct((8, both), F32),
            jax.ShapeDtypeStruct((devices * 8, 128), BF16),
            jax.ShapeDtypeStruct(gather_shape(devices, bands, maps), BF16),
            *[jax.ShapeDtypeStruct(gather_shape(devices, bands, s), BF16) for s in kinds],
        ],
        scratch_shapes=[
            pltpu.VMEM((extended, width, 128), F32),
            pltpu.VMEM((extended, width, 128), F32),
            pltpu.VMEM((2 * groups, keys, 128), BF16),
            pltpu.VMEM((extended, width, dim), F32),
            pltpu.VMEM((extended, width, dim), F32),
            pltpu.VMEM((images, RADIUS, width, dim), BF16),
            pltpu.VMEM((images, RADIUS, width, dim), BF16),
            pltpu.VMEM((devices, 8, wide), BF16),
            pltpu.VMEM((128, both), BF16),
            pltpu.VMEM((devices, 8, both), F32),
            pltpu.VMEM((devices, 8, both), F32),
            pltpu.VMEM(gather_shape(devices, bands, qkv), BF16),
            pltpu.SemaphoreType.DMA((small,)),
            pltpu.SemaphoreType.DMA((small,)),
            pltpu.SemaphoreType.DMA((2, images)),
            pltpu.SemaphoreType.DMA((2, images)),
            *gather_scratch(devices, bands, [qkv]),
            *gather_scratch(devices, bands, [maps]),
            *gather_scratch(devices, bands, kinds),
        ],
        compiler_params=pltpu.CompilerParams(
            collective_id=collective, has_side_effects=True, vmem_limit_bytes=VMEM_LIMIT
        ),
        name="attend_forward",
    )(x, x, attn, *inputs)
    return outs[:9], [o.reshape(-1, o.shape[-1]) for o in outs[9:]]


def gaussian_parts(gate):
    bell = jnp.exp2(gate * gate * (-0.5 * math.log2(math.e)))
    t = 1.0 / (1.0 + (0.3275911 * math.sqrt(0.5)) * jnp.abs(gate))
    tail = ((((0.5 * 1.061405429) * t - 0.5 * 1.453152027) * t + 0.5 * 1.421413741) * t - 0.5 * 0.284496736) * t
    tail = (tail + 0.5 * 0.254829592) * (t * bell)
    return jnp.where(gate < 0, tail, 1.0 - tail), bell


def feed_kernel(
    x, att, cot, weight, scales, w_out, w_up, w_down, spread,
    result, d_residual, d_att, delta_out, grad_up_out, grad_down_out, d_scale,
    grad_up, grad_down_t, grad_out, down_t,
):
    image = pl.program_id(0)
    step = image * pl.num_programs(1) + pl.program_id(1)
    last = pl.num_programs(0) * pl.num_programs(1) - 1
    hidden_units = w_down.shape[0]
    chunk = 256

    @pl.when(step == 0)
    def _():
        grad_up[...] = jnp.zeros_like(grad_up)
        down_t[...] = w_down[...].T
        grad_down_t[...] = jnp.zeros_like(grad_down_t)
        grad_out[...] = jnp.zeros_like(grad_out)

    @pl.when(pl.program_id(1) == 0)
    def _():
        d_scale[...] = jnp.zeros_like(d_scale)

    row_scale = scales[pl.ds(image, 1), x.shape[-1] :]
    att_low = att[0]
    residual = x[0].astype(F32) + nn(att_low, w_out[...])
    normed, inverse = normed_rows(residual, row_scale)
    normed_low = normed.astype(BF16)
    seed = cot[0].astype(F32) * weight[image]
    seed_low = seed.astype(BF16)
    total = residual
    seed_flip = seed_low.T
    normed_flip = normed_low.T
    d_normed = jnp.zeros_like(residual)
    total_t = jnp.zeros((x.shape[-1], x.shape[1]), F32)
    normed_t = total_t
    count = hidden_units // chunk
    spans = [
        (slice(c * chunk, (c + 1) * chunk), slice(hidden_units + c * chunk, hidden_units + (c + 1) * chunk))
        for c in range(count)
    ]
    lift = lambda c: (
        nn(normed_low, w_up[:, spans[c][0]]), nn(normed_low, w_up[:, spans[c][1]]), nt(seed_low, w_down[spans[c][0]])
    )
    def grads(c, hidden, d_value, d_gate):
        low, high = spans[c]
        grad_down_t[:, low] += nn(seed_flip, hidden)
        grad_up[:, low] += nn(normed_flip, d_value)
        grad_up[:, high] += nn(normed_flip, d_gate)
        return nt(down_t[:, low], hidden), nt(w_up[:, low], d_value) + nt(w_up[:, high], d_gate)

    ready = lift(0)
    past = None
    for c in range(count + 1):
        if c < count:
            value, gate, d_hidden = ready
        if c + 1 < count:
            ready = lift(c + 1)
        if past is not None:
            more, back = grads(c - 1, *past)
            total_t = total_t + more
            normed_t = normed_t + back
        if c < count:
            area, bell = gaussian_parts(gate)
            gelu = gate * area
            hidden = (value * gelu).astype(BF16)
            d_value = (d_hidden * gelu).astype(BF16)
            d_gate = (d_hidden * value * (area + (gate * (1.0 / math.sqrt(2.0 * math.pi))) * bell)).astype(BF16)
            past = (hidden, d_value, d_gate)
    total = total + total_t.T
    d_normed = normed_t.T
    result[0] = total.astype(BF16)
    pull = d_normed * residual
    d_scale[0] += jnp.sum(pull * inverse, axis=0, keepdims=True)
    along = jnp.mean(pull * row_scale, axis=-1, keepdims=True)
    back = seed + row_scale * inverse * d_normed - residual * (inverse * inverse * inverse * along)
    d_residual[0] = back
    back_low = back.astype(BF16)
    grad_out[...] += tn(att_low, back_low)
    d_att_low = nt(back_low, w_out[...]).astype(BF16)
    d_att[0] = d_att_low
    delta = -head_sums(d_att_low.astype(F32) * att_low.astype(F32), spread[...])
    kept = thirds(delta)
    third = lax.rem(lanes(delta.shape), 3)
    delta_out[0] = jnp.where(third == 0, kept[0], jnp.where(third == 1, kept[1], kept[2])).astype(BF16)

    @pl.when(step == last)
    def _():
        grad_up_out[:, : 2 * hidden_units] = grad_up[...].astype(BF16)
        grad_up_out[:, 2 * hidden_units :] = grad_out[...].astype(BF16)
        grad_down_out[...] = grad_down_t[...].T.astype(BF16)


def feed(x, att, cot, weight, scales, w_up_out, w_down, spread):
    images, tokens, dim = x.shape
    tile = min(512, tokens)
    hidden_units = w_down.shape[0]
    block = lambda cols: pl.BlockSpec((1, tile, cols), lambda i, j: (i, j, 0))
    row = lambda cols: pl.BlockSpec((1, 1, cols), lambda i, j: (i, 0, 0))
    whole = lambda a: pl.BlockSpec(a.shape, lambda i, j: (0,) * len(a.shape))
    shapes = [
        jax.ShapeDtypeStruct((images, tokens, dim), BF16),
        jax.ShapeDtypeStruct((images, tokens, dim), F32),
        jax.ShapeDtypeStruct((images, tokens, dim), BF16),
        jax.ShapeDtypeStruct((images, tokens, 128), BF16),
        jax.ShapeDtypeStruct(w_up_out.shape, BF16),
        jax.ShapeDtypeStruct((hidden_units, dim), BF16),
        jax.ShapeDtypeStruct((images, 1, dim), F32),
    ]
    last = 2 * hidden_units // dim
    return pl.pallas_call(
        feed_kernel,
        grid=(images, tokens // tile),
        in_specs=[
            block(dim), block(dim), block(dim), pl.BlockSpec(memory_space=pltpu.SMEM), whole(scales),
            pl.BlockSpec((dim, dim), lambda i, j: (0, last)),
            pl.BlockSpec((dim, 2 * hidden_units), lambda i, j: (0, 0)),
            whole(w_down), whole(spread),
        ],
        out_specs=[
            block(dim), block(dim), block(dim), block(128),
            whole(shapes[4]), whole(shapes[5]), row(dim),
        ],
        out_shape=shapes,
        scratch_shapes=[
            pltpu.VMEM((dim, 2 * hidden_units), F32),
            pltpu.VMEM((dim, hidden_units), F32),
            pltpu.VMEM((dim, dim), F32),
            pltpu.VMEM((dim, hidden_units), BF16),
        ],
        compiler_params=pltpu.CompilerParams(vmem_limit_bytes=VMEM_LIMIT),
        name="feed",
    )(x, att, cot, weight, scales, w_up_out, w_up_out, w_down, spread)


def backward_kernel(height, images, devices, bands, splits, qkv_split, *refs):
    n = len(splits)
    (
        q, k, v, d_att, logs, deltas,
        x_mix, q_past, inverse_in, x_norm, d_residual, attn,
        w_qkv, scales, d_scale_two, pool, expand, crow, srow, ccol, scol, chosen, maps,
        grads_hbm,
        grad_input, up_out, out_out, down_out, qkv_out, map_one_out, map_two_out, grad_cond, grad_heads,
        cos_s, sin_s, feat_s, kf_s, vf_s, dq_s, dk_s, dv_s, mixed_s, unit_s, grad_qkv, sums,
        d_top, d_bottom, above, below, halo_send, halo_recv, local,
        band_in, all_in, small_send, small_recv,
        grads, inbox, pieces, arrivals, send, recv,
        qkv_acc, qkv_inbox, qkv_pieces, qkv_arrivals, qkv_send, qkv_recv,
    ) = split_refs(
        refs, *[None] * 23, n, *[None] * 9, *[None] * 12, *[None] * 7, *[None] * 4,
        n, n, n, n, None, None, *[None] * 6,
    )
    _, band_rows, width, dim = q.shape
    pairs = dim // 128
    edge = RADIUS
    border = edge * width
    groups = band_rows // QUERY_ROWS
    half, wide, starts = tile_columns(width)
    window = QUERY_ROWS + 2 * RADIUS
    queries = QUERY_ROWS * half
    chunk = QUERY_ROWS * width
    step = pl.program_id(0)
    dp, band = here()
    steps = scatter_steps(
        devices, bands, Copies(send, recv), grads, inbox, pieces, arrivals,
        [[up_out, out_out], [down_out]], splits,
    )
    hooks = spaced((3, 6, 8), steps[1:-1])
    around = [((dp + d) % devices, band) for d in range(1, devices)]
    beside = [(dp, (band + d) % bands) for d in range(1, bands)]
    small = Copies(small_send, small_recv)
    first = small.batch(bands - 1, lambda: [(sums, band_in.at[here()[1]], peer) for peer in beside])
    second = small.batch(
        devices - 1, lambda: [(all_in.at[here()[0]], all_in.at[here()[0]], peer) for peer in around]
    )
    last = scatter_steps(
        devices, bands, Copies(qkv_send, qkv_recv), [qkv_acc], [qkv_inbox], [qkv_pieces], [qkv_arrivals],
        [[qkv_out]], [qkv_split],
    )

    def loads():
        return [pltpu.make_async_copy(grads_hbm[a], grads[a], local.at[a]) for a in range(n)]

    def to_above(at):
        dp, band = here()
        return pltpu.make_async_remote_copy(
            src_ref=d_top, dst_ref=below.at[at % 2],
            send_sem=halo_send.at[0, at], recv_sem=halo_recv.at[0, at],
            device_id=(dp, (band + bands - 1) % bands), device_id_type=MESH,
        )

    def to_below(at):
        dp, band = here()
        return pltpu.make_async_remote_copy(
            src_ref=d_bottom, dst_ref=above.at[at % 2],
            send_sem=halo_send.at[1, at], recv_sem=halo_recv.at[1, at],
            device_id=(dp, (band + 1) % bands), device_id_type=MESH,
        )

    @pl.when(step == 0)
    def _():
        for load in loads():
            load.start()
        wait = hail(every_peer(devices, bands))
        first_row = band * band_rows
        build_turns(first_row + edge, crow, srow, ccol, scol, cos_s, sin_s)
        build_key_features(first_row, height, width, feat_s)
        grad_qkv[...] = jnp.zeros_like(grad_qkv)
        sums[...] = jnp.zeros_like(sums)
        for at in range(images):
            sums[at : at + 1, dim:] = d_scale_two[at]

        @pl.when(band == 0)
        def _():
            above[...] = jnp.zeros_like(above)

        @pl.when(band == bands - 1)
        def _():
            below[...] = jnp.zeros_like(below)

        for load in loads():
            load.wait()
        wait()
        steps[0]()

    def with_borders(ref, at, c, cols, offset):
        values = ref[edge + c * QUERY_ROWS : edge + (c + 1) * QUERY_ROWS, :, cols].reshape(chunk, 128)
        across = slice(cols.start + offset, cols.stop + offset)
        found = [values]
        if c == 0:
            extra = above[at % 2, :, across].astype(F32)
            found = [values[:border] + extra, values[border:]]
        if c == groups - 1:
            extra = below[at % 2, :, across].astype(F32)
            tail = found[-1]
            cut = tail.shape[0] - border
            found = found[:-1] + [tail[:cut], tail[cut:] + extra]
        return jnp.concatenate(found, axis=0) if len(found) > 1 else values

    def mix_front(at, c):
        own = slice(c * QUERY_ROWS, (c + 1) * QUERY_ROWS)
        spot = slice(edge + c * QUERY_ROWS, edge + (c + 1) * QUERY_ROWS)
        flat = slice(c * chunk, (c + 1) * chunk)
        values = x_mix[0, own].reshape(chunk, dim).astype(F32)
        inverse = lax.rsqrt(jnp.mean(values * values, axis=-1, keepdims=True) + NORM_EPS)
        unit_s[flat] = (values * inverse).astype(BF16)
        inverse_scale = 1.0 / head_row(attn, dim)
        high, low = halves(inverse_in[0, own].reshape(chunk, 128))
        fr = nn(jnp.concatenate([high, low], axis=1), expand[...])
        found = []
        for p in range(pairs):
            cut = slice(p * 128, (p + 1) * 128)
            for kind in range(2):
                if kind == 0:
                    unit = q_past[0, own, :, cut].reshape(chunk, 128).astype(F32)
                    grad = dq_s[own, :, cut].reshape(chunk, 128)
                else:
                    unit = kf_s[spot, :, cut].reshape(chunk, 128)
                    grad = with_borders(dk_s, at, c, cut, 0)
                found.append((unit, grad, head_sums(unit * grad, pool[...]) * inverse_scale[:, cut]))
        return fr, found

    def mix_rest(at, c, fr, found):
        own = slice(c * QUERY_ROWS, (c + 1) * QUERY_ROWS)
        flat = slice(c * chunk, (c + 1) * chunk)
        slot = at % 2
        cos, sin = cos_s[own].reshape(chunk, 128), sin_s[own].reshape(chunk, 128)
        for p in range(pairs):
            cut = slice(p * 128, (p + 1) * 128)
            for kind in range(2):
                unit, grad, along = found[2 * p + kind]
                sums[images : images + 1, cut] += jnp.sum(along, axis=0, keepdims=True)
                grad = grad - unit * along
                grad = grad * cos - swapped(grad) * sin
                lane = (2 * p + kind) * 128
                mixed_s[slot, flat, kind * dim + p * 128 : kind * dim + (p + 1) * 128] = (
                    grad * fr[:, lane : lane + 128]
                ).astype(BF16)
            mixed_s[slot, flat, 2 * dim + p * 128 : 2 * dim + (p + 1) * 128] = with_borders(
                dv_s, at, c, cut, dim
            ).astype(BF16)

    def mix_back(at, order):
        ready = mix_front(at, order[0])
        for spot, c in enumerate(order):
            current = ready
            if spot + 1 < len(order):
                ready = mix_front(at, order[spot + 1])
            mix_rest(at, c, *current)

    def weight_back(at):
        slot = at % 2
        column = jnp.broadcast_to(scales[pl.ds(at, 1), :dim], (8, dim)).T[:, :1]
        ones = jnp.ones((8, dim), BF16)
        row = jnp.zeros((8, dim), F32)
        flipped = unit_s[...].T
        for part in range(3):
            cut = slice(part * dim, (part + 1) * dim)
            product = nn(flipped, mixed_s[slot, :, cut])
            grad_qkv[:, cut] += product * column
            high, low = halves(product * w_qkv[:, cut].astype(F32))
            row = row + nt(ones, high) + nt(ones, low)
        sums[pl.ds(at, 1), :dim] = row[:1]

    def norm_back(at, c):
        own = slice(c * QUERY_ROWS, (c + 1) * QUERY_ROWS)
        flat = slice(c * chunk, (c + 1) * chunk)
        values = x_norm[0, own].reshape(chunk, dim).astype(F32)
        row_scale = scales[pl.ds(at, 1), :dim]
        inverse = lax.rsqrt(jnp.mean(values * values, axis=-1, keepdims=True) + NORM_EPS)
        d_normed = nt(mixed_s[at % 2, flat], w_qkv[...])
        pull = d_normed * values
        along = jnp.mean(pull * row_scale, axis=-1, keepdims=True)
        back = row_scale * inverse * d_normed - values * (inverse * inverse * inverse * along)
        grad_input[0, own] = d_residual[0, own] + back.reshape(QUERY_ROWS, width, dim)

    @pl.when((step > 0) & (step <= images))
    def _():
        at = step - 1
        mix_back(at, list(range(1, groups - 1)))

        @pl.when(step >= 2)
        def _():
            for c in range(groups):
                norm_back(step - 2, c)

        @pl.when(band > 0)
        def _():
            to_above(at).wait_send()
            to_below(at).wait_recv()

        @pl.when(band < bands - 1)
        def _():
            to_below(at).wait_send()
            to_above(at).wait_recv()

        mix_back(at, [0, groups - 1])
        weight_back(at)

    @pl.when(step == images)
    def _():
        tall = qkv_acc.shape[1]
        for d in range(devices):
            qkv_acc[d] = grad_qkv[d * tall : (d + 1) * tall].astype(BF16)
        last[0]()
        start(first)
        band_in[band] = sums[...]
        steps[-1]()

    @pl.when(step == images + 1)
    def _():
        for c in range(groups):
            norm_back(step - 2, c)

    ask = query_features(width)
    ask = jnp.concatenate([ask, ask], axis=0)
    lane = lanes((queries, 128))
    one_lanes = jnp.where(lanes((window * wide, 128)) < 3 * 2 * pairs, 1.0, 0.0).astype(BF16)

    def send_borders():
        _, band = here()
        low, high = slice(0, edge), slice(edge + band_rows, 2 * edge + band_rows)
        for spot, target in ((low, d_top), (high, d_bottom)):
            target[:, :dim] = dk_s[spot].reshape(border, dim).astype(BF16)
            target[:, dim:] = dv_s[spot].reshape(border, dim).astype(BF16)

        @pl.when(band > 0)
        def _():
            to_above(step).start()

        @pl.when(band < bands - 1)
        def _():
            to_below(step).start()

    def back(i, _):
        pl.when(i == 2)(send_borders)
        hooked(step * groups + i, hooks)
        later = (i + groups - 2) // groups
        g = i + ((i + groups - 1) // groups - later) * (groups - 2) - later
        own = pl.ds(g * QUERY_ROWS, QUERY_ROWS)
        seen = pl.ds(g * QUERY_ROWS, window)

        def begin(side, p):
            mine = slice(side * half, (side + 1) * half)
            theirs = slice(starts[side], starts[side] + wide)
            cut = slice(p * 128, (p + 1) * 128)
            delta_tile = deltas[0, own, mine].reshape(queries, 128)
            pulls = []
            for h in range(2):
                spot = 3 * (2 * p + h)
                hit = (lane >= spot) & (lane < spot + 3)
                pulls.append(jnp.where(hit, delta_tile, jnp.zeros_like(delta_tile)))
            query = block_diagonal(q[0, own, mine, cut].reshape(queries, 128))
            pull = block_diagonal(d_att[0, own, mine, cut].reshape(queries, 128))
            query_wide = jnp.concatenate([query, ask], axis=1)
            pull_wide = jnp.concatenate([pull, jnp.concatenate(pulls, axis=0)], axis=1)
            key = kf_s[seen, theirs, cut].reshape(window * wide, 128).astype(BF16)
            value = vf_s[seen, theirs, cut].reshape(window * wide, 128).astype(BF16)
            scores = nt(jnp.concatenate([key, feat_s[2 * g + side]], axis=1), query_wide)
            d_probs = nt(jnp.concatenate([value, one_lanes], axis=1), pull_wide)
            return scores, d_probs, key, query, pull

        def end(side, p, probs, d_scores, key, query, pull):
            mine = slice(side * half, (side + 1) * half)
            theirs = slice(starts[side], starts[side] + wide)
            cut = slice(p * 128, (p + 1) * 128)
            dv_s[seen, theirs, cut] += nn(probs, pull).reshape(window, wide, 128)
            dk_s[seen, theirs, cut] += nn(d_scores, query).reshape(window, wide, 128)
            turned = tn(key, d_scores)
            turned = jnp.concatenate([turned[:64, :queries], turned[64:, queries:]], axis=0)
            dq_s[own, mine, cut] = turned.T.reshape(QUERY_ROWS, half, 128)

        tiles = [(side, p) for side in range(2) for p in range(pairs)]
        ready, past = begin(*tiles[0]), None
        for at, (side, p) in enumerate(tiles):
            scores, d_probs, key, query, pull = ready
            if at + 1 < len(tiles):
                ready = begin(*tiles[at + 1])
            if past is not None:
                end(*past)
            probs = jnp.exp(scores - logs[0, 2 * g + side, p : p + 1])
            past = (side, p, probs.astype(BF16), (probs * d_probs).astype(BF16), key, query, pull)
        end(*past)
        return 0

    @pl.when(step < images)
    def _():
        dk_s[...] = jnp.zeros_like(dk_s)
        dv_s[...] = jnp.zeros_like(dv_s)
        kf_s[...] = k[0].astype(F32)
        vf_s[...] = v[0].astype(F32)
        lax.fori_loop(0, groups, back, 0)

    @pl.when(step == images)
    def _():
        last[1]()
        arrive(first)
        total = band_in[0]
        for b in range(1, bands):
            total = total + band_in[b]
        all_in[dp] = total
        start(second)
        grad_cond[...] = sum(nt(part.astype(BF16), maps[...]) for part in thirds(total))[: grad_cond.shape[0]]

    @pl.when(step == images + 1)
    def _():
        last[2]()
        arrive(second)
        everyone = all_in[...]
        heads = everyone[0]
        for d in range(1, devices):
            heads = heads + everyone[d]
        grad_heads[...] = heads
        everyone = everyone.reshape(-1, everyone.shape[-1])
        map_all = sum(tn(chosen[...], part.astype(BF16)) for part in thirds(everyone))
        rows = map_one_out.shape[0]
        mine = map_all[:rows]
        for b in range(1, bands):
            mine = jnp.where(band == b, map_all[b * rows : (b + 1) * rows], mine)
        map_one_out[...] = mine[:, :dim]
        map_two_out[...] = mine[:, dim:]
        for move in last[3:]:
            move()
        depart(first, second)


def backward(
    q, k, v, d_att, logs, deltas, x, inverse, d_residual, attn, w_qkv, scales, d_scale_two,
    pool, expand, turns, chosen, maps, height, devices, bands, grads, up_columns, cond_rows, collective,
):
    splits = [column_split(grads[0].shape[1], 1920), column_split(grads[1].shape[1], 128)]
    shapes = [grad_shape(devices, bands, *g.shape) for g in grads]
    qkv_shape = grad_shape(devices, bands, *w_qkv.shape)
    images, band_rows, width, dim = q.shape
    extended = k.shape[1]
    groups = band_rows // QUERY_ROWS
    _, wide_columns, _ = tile_columns(width)
    keys = (QUERY_ROWS + 2 * RADIUS) * wide_columns
    both = scales.shape[1]
    small = devices - 1 + bands - 1
    final = images - 1

    def block(low, *shape, buffers=2):
        place = lambda i: jnp.minimum(jnp.maximum(i - low, 0), final)
        return pl.BlockSpec(
            (1,) + shape, lambda i: (place(i),) + (0,) * len(shape), pipeline_mode=pl.Buffered(buffers)
        )

    whole = lambda shape: pl.BlockSpec(shape, lambda i: (0,) * len(shape))
    once = lambda shape: pl.BlockSpec(shape, lambda i: (0,) * len(shape), pipeline_mode=pl.Buffered(1))
    hbm = pl.BlockSpec(memory_space=pl.ANY)
    own = (band_rows, width)
    fixed = [w_qkv, scales, d_scale_two, pool, expand, *turns, chosen, maps]
    map_row = maps.shape[0] // (devices * bands)
    up_rows = shapes[0][1] // bands
    results = [
        jax.ShapeDtypeStruct((up_rows, up_columns), F32),
        jax.ShapeDtypeStruct((up_rows, shapes[0][2] - up_columns), F32),
        jax.ShapeDtypeStruct((shapes[1][1] // bands, shapes[1][2]), F32),
        jax.ShapeDtypeStruct((qkv_shape[1] // bands, qkv_shape[2]), F32),
        jax.ShapeDtypeStruct((map_row, dim), F32),
        jax.ShapeDtypeStruct((map_row, dim), F32),
        jax.ShapeDtypeStruct((cond_rows, maps.shape[0]), F32),
        jax.ShapeDtypeStruct((8, both), F32),
    ]
    halo = pltpu.VMEM((2, RADIUS * width, 2 * dim), BF16)
    field = pltpu.VMEM((extended, width, dim), F32)
    return pl.pallas_call(
        functools.partial(
            backward_kernel, height, images, devices, bands, splits, column_split(w_qkv.shape[1], 640)
        ),
        grid=(images + 2,),
        in_specs=[
            block(0, *own, dim), block(0, extended, width, dim), block(0, extended, width, dim),
            block(0, *own, dim), block(0, *logs.shape[1:]), block(0, *own, 128),
            block(1, *own, dim), block(1, *own, dim), block(1, *own, 128),
            block(2, *own, dim, buffers=1), block(2, *own, dim), pl.BlockSpec(memory_space=pltpu.SMEM),
            *[once(a.shape) for a in fixed], *[hbm for _ in grads],
        ],
        out_specs=[block(2, *own, dim), *[whole(r.shape) for r in results]],
        out_shape=[jax.ShapeDtypeStruct((images, *own, dim), F32), *results],
        scratch_shapes=[
            pltpu.VMEM((*own, 128), F32),
            pltpu.VMEM((*own, 128), F32),
            pltpu.VMEM((2 * groups, keys, 128), BF16),
            field, field,
            pltpu.VMEM((*own, dim), F32),
            field, field,
            pltpu.VMEM((2, band_rows * width, 3 * dim), BF16),
            pltpu.VMEM((band_rows * width, dim), BF16),
            pltpu.VMEM(w_qkv.shape, F32),
            pltpu.VMEM((8, both), F32),
            pltpu.VMEM((RADIUS * width, 2 * dim), BF16),
            pltpu.VMEM((RADIUS * width, 2 * dim), BF16),
            halo, halo,
            pltpu.SemaphoreType.DMA((2, images)),
            pltpu.SemaphoreType.DMA((2, images)),
            pltpu.SemaphoreType.DMA((len(grads),)),
            pltpu.VMEM((bands, 8, both), F32),
            pltpu.VMEM((devices, 8, both), F32),
            pltpu.SemaphoreType.DMA((small,)),
            pltpu.SemaphoreType.DMA((small,)),
            *scatter_scratch(devices, bands, shapes),
            *scatter_scratch(devices, bands, [qkv_shape]),
        ],
        compiler_params=pltpu.CompilerParams(
            collective_id=collective, has_side_effects=True, vmem_limit_bytes=VMEM_LIMIT
        ),
        name="backward",
    )(q, k, v, d_att, logs, deltas, x, q, inverse, x, d_residual, attn, *fixed,
      *[g.reshape(s) for g, s in zip(grads, shapes)])


def finish_kernel(image_count, *refs):
    count = len(refs) // 2
    sources, targets = refs[:count], refs[count:]
    targets[0][...] = sources[0][...]

    @pl.when(pl.program_id(0) == 0)
    def _():
        for source, target in zip(sources[1:-1], targets[1:-1]):
            target[...] = source[...]
        heads = targets[-1].shape[1]
        row = sources[-1][image_count : image_count + 1, : heads * 64]
        for h in range(heads):
            targets[-1][:, h : h + 1] = 0.5 * row[:, h * 64 : h * 64 + 1]


def finish(arrays, head_count):
    images, rows, width, dim = arrays[0].shape
    whole = lambda a: pl.BlockSpec(a.shape, lambda i: (0,) * len(a.shape))
    large = pl.BlockSpec((1, rows // 2, width, dim), lambda i: (i // 2, i % 2, 0, 0))
    shapes = [jax.ShapeDtypeStruct(a.shape, a.dtype) for a in arrays[:-1]]
    shapes.append(jax.ShapeDtypeStruct((1, head_count), F32))
    return pl.pallas_call(
        functools.partial(finish_kernel, images),
        grid=(2 * images,),
        in_specs=[large, *[whole(a) for a in arrays[1:]]],
        out_specs=[large, *[whole(a) for a in shapes[1:]]],
        out_shape=shapes,
        name="finish",
    )(*arrays)


def turn_tables(height, width):
    freqs = math.pi * 10.0 ** (np.arange(8) / 7.0)

    def angles(count, extent):
        places = np.arange(count) - (RADIUS if count != extent else 0)
        return ((2.0 * places + 1.0) / extent - 1.0)[:, None] * freqs[None, :]

    def table(angle, start):
        cos = np.ones((angle.shape[0], 64))
        sin = np.zeros((angle.shape[0], 64))
        cos[:, start : start + 8] = np.cos(angle)
        cos[:, start + 8 : start + 16] = np.cos(angle)
        sin[:, start : start + 8] = -np.sin(angle)
        sin[:, start + 8 : start + 16] = np.sin(angle)
        return [np.tile(t, (1, 2)).astype(np.float32) for t in (cos, sin)]

    return table(angles(height + 2 * RADIUS, height), 0), table(angles(width, width), 16)


def constants(head_count):
    index = np.arange(256)
    pool = ((index[:, None] % 128) // 64 == np.arange(128)[None, :] // 64).astype(np.float32)
    dim = head_count * 64
    rows = np.arange(2 * dim)
    spread = ((rows[:, None] % dim) // 64 == np.arange(128)[None, :] // 3).astype(np.float32)
    pieces = np.arange(dim * 2)
    source = pieces // 128 + 64 * ((pieces % 128) // 64)
    expand = (index[:, None] % 128 == source[None, :]).astype(np.float32)
    return [jnp.asarray(t, BF16) for t in (pool, spread, expand)]


def shards(
    tokens_in, cond, loss_weight, cotangent, norm1_map, qkv_weight, attn_scale, out_weight,
    norm2_map, up_weight, down_weight,
):
    images, band_rows, width, dim = tokens_in.shape
    head_count = attn_scale.shape[0]
    tokens = band_rows * width
    devices, bands = lax.axis_size("dp"), lax.axis_size("band")
    height = band_rows * bands
    (row_cos, row_sin), (col_cos, col_sin) = turn_tables(height, width)
    turns = [jnp.asarray(t) for t in (row_cos, row_sin, col_cos, col_sin)]
    pool, spread, expand = constants(head_count)
    (att, q, k, v, inverse, logs, w_qkv, scales, chosen), (maps, w_up_out, w_down) = attend_forward(
        tokens_in, attn_scale, cond, norm1_map, norm2_map, pool, turns, height, devices, bands,
        qkv_weight, up_weight, out_weight, down_weight, 0,
    )
    flat = lambda a: a.reshape(images, tokens, a.shape[-1])
    deep = lambda a: a.reshape(images, band_rows, width, a.shape[-1])
    result, d_residual, d_att, deltas, grad_up_out, grad_down, d_scale_two = feed(
        flat(tokens_in), flat(att), flat(cotangent), loss_weight, scales, w_up_out, w_down, spread
    )
    grads = backward(
        q, k, v, deep(d_att), logs, deep(deltas), tokens_in, inverse, deep(d_residual), attn_scale, w_qkv,
        scales, d_scale_two, pool, expand, turns, chosen, maps, height, devices, bands,
        [grad_up_out, grad_down], up_weight.shape[1], images, 1,
    )
    grad_input, grad_up, grad_out, grad_down, grad_qkv, grad_one, grad_two, grad_cond, grad_heads = finish(
        grads, head_count
    )
    return (
        deep(result), grad_input, grad_cond, grad_one, grad_qkv, grad_heads.reshape(head_count), grad_out,
        grad_two, grad_up, grad_down,
    )


def solution(mesh):
    tokens = P("dp", "band", None, None)
    weights = P(("dp", "band"), None)
    return jax.shard_map(
        shards,
        mesh=mesh,
        in_specs=(tokens, P("dp", None), P("dp"), tokens, weights, weights, P(), *[weights] * 4),
        out_specs=(tokens, tokens, P("dp", None), weights, weights, P(), *[weights] * 4),
        check_vma=False,
    )
```

time: 1510 us -> 212 us (0.14)
  blocking collectives: 583 us -> 0 us
  local copies, waits for them, and re-layouts: 302 us -> 0 us
  matrix products: 287 us -> 0 us
  other arithmetic: 218 us -> 0 us
  Pallas kernels: 0 us -> 210 us
  starting transfers between devices: 82.6 us -> 0 us
    all_gather x4 -> x0, blocking collectives: 294 us -> none  [the longest x1 79.9 us: shards(): lax.all_gather(qkv_weight, ('dp', 'band'), axis=0, tiled=True)]
    dot_general x39 -> x0, matrix products: 287 us -> none  [the longest x1 52.4 us: shards(): jnp.einsum('itd,fd->itf', loss_seed_low, w_down, preferred_element_type=j...]
    unnamed x1 -> x0, blocking collectives: 232 us -> none
    pallas_call x0 -> x4, Pallas kernels: none -> 210 us  [the longest x1 85.5 us: backward(): pl.pallas_call(functools.partial(backward_kernel, height, images, devices...]
    slice x16 -> x0, local copies, waits for them, and re-layouts: 95.8 us -> none  [the longest x2 27.8 us: shards(): windows[..., :model_dim]]
    dynamic_update_slice x12 -> x0, local copies, waits for them, and re-layouts: 79.8 us -> none  [the longest x9 75.6 us: shards(): lax.map(attend_back, (query_blocks, keys_win, values_win, d_attended_bloc...]
    unnamed x25 -> x0, starting transfers between devices: 72.3 us -> none
    psum x2 -> x0, blocking collectives: 56.1 us -> none  [the longest x1 37.9 us: shards(): grad_scale = lax.psum(d_scale_heads, ('dp', 'band'))]
  transfers between devices with their start and end apart: 32 -> 0, of which waited for: 2 -> 0; matrix products, arithmetic and copies ran while one was open for 38% -> 0% of each run, Pallas kernels for 0% -> 0%
where the time goes in v3:
time: 212 us; the launch traced here: 211 us
  Pallas kernels  210 us (99%)
    pallas_call x1, Pallas kernels, backward(): pl.pallas_call(functools.partial(backward_kernel, height, images, devices...  85.5 us
    pallas_call x1, Pallas kernels, feed(): pl.pallas_call(feed_kernel, grid=(images, tokens // tile), in_specs=[bloc...  61.3 us
    pallas_call x1, Pallas kernels, attend_forward(): pl.pallas_call(functools.partial(attend_kernel, height, images, devices,...  57.3 us
    pallas_call x1, Pallas kernels, finish(): pl.pallas_call(functools.partial(finish_kernel, images), grid=(2 * images...  6.39 us

profile of v3, /device:TPU:0, one launch (start us, length us, event | category | flops | bytes accessed | tf_op | source)
XLA Modules:
  0.0 211.3 jit_solution(4336651399818906172)
XLA Ops:
  0.6 57.3 %attend_forward.1 = (bf16[3,16,64,384]{3,2,1,0:T(8,128)(2,1)}, bf16[3,16,64,384]{3,2,1,0:T(8,128)(2,1)}, bf16[3,22,64,384]{3,2,1,0:T(8,128)(2,1)}, bf16[3,22,64,...) custom-call(bf16[3,16,64,384]{3,2,1,0:T(8,128)(2,1)} %refs_9_.2, ...), custom_call_target="tpu_custom_call" | custom-call | tf_op jit(solution)/shard_map/attend_forward/pallas_call | solution.py:730
  57.9 61.3 %feed.1 = (bf16[3,1024,384]{2,1,0:T(8,128)(2,1)}, f32[3,1024,384]{2,1,0:T(8,128)}, bf16[3,1024,384]{2,1,0:T(8,128)(2,1)}, bf16[3,1024,128]{2,1,0:T(8,128)(2,1)},...) custom-call(bf16[3,1024,384]{2,1,0:T(8,128)(2,1)} %bitcast.13, ...), custom_call_target="tpu_custom_call" | custom-call | tf_op jit(solution)/shard_map/feed/pallas_call | solution.py:905
  119.2 85.5 %backward.1 = (f32[3,16,64,384]{3,2,1,0:T(8,128)}, f32[12,3072]{1,0:T(8,128)}, f32[12,384]{1,0:T(8,128)}, f32[48,384]{1,0:T(8,128)}, f32[12,1152]{1,0:T(8,128)},...) custom-call(bf16[3,16,64,384]{3,2,1,0:T(8,128)(2,1)} %get-tuple-element.52.refs_0_.refs_7_, ...), custom_call_target="tpu_custom_call" | custom-call | tf_op jit(solution)/shard_map/backward/pallas_call | solution.py:1302
  204.7 6.4 %finish.1 = (f32[3,16,64,384]{3,2,1,0:T(8,128)}, f32[12,3072]{1,0:T(8,128)}, f32[12,384]{1,0:T(8,128)}, f32[48,384]{1,0:T(8,128)}, f32[12,1152]{1,0:T(8,128)}, /...) custom-call(f32[3,16,64,384]{3,2,1,0:T(8,128)} %get-tuple-element.66.refs_0_, ...), custom_call_target="tpu_custom_call" | custom-call | tf_op jit(solution)/shard_map/finish/pallas_call | solution.py:1369

commit v4 on v3

--- a/solution.py
+++ b/solution.py
@@ -491,7 +491,7 @@
         [map_rows], [map_split], waited=True,
     )
     both_steps = [run(one, two) for one, two in zip(steps[1:], map_steps[1:])]
-    hooks = spaced((0, 4, 10), both_steps[:-1])
+    hooks = spaced((1, 4, 9), both_steps[:-1])
 
     def upward(at):
         dp, band = here()
@@ -794,8 +794,8 @@
 
 
 def feed_kernel(
-    x, att, cot, weight, scales, w_out, w_up, w_down, spread,
-    result, d_residual, d_att, delta_out, grad_up_out, grad_down_out, d_scale,
+    x, att, cot, weight, scales, w_out, w_up, w_down,
+    result, d_residual, d_att, grad_up_out, grad_down_out, d_scale,
     grad_up, grad_down_t, grad_out, down_t,
 ):
     image = pl.program_id(0)
@@ -871,12 +871,7 @@
     d_residual[0] = back
     back_low = back.astype(BF16)
     grad_out[...] += tn(att_low, back_low)
-    d_att_low = nt(back_low, w_out[...]).astype(BF16)
-    d_att[0] = d_att_low
-    delta = -head_sums(d_att_low.astype(F32) * att_low.astype(F32), spread[...])
-    kept = thirds(delta)
-    third = lax.rem(lanes(delta.shape), 3)
-    delta_out[0] = jnp.where(third == 0, kept[0], jnp.where(third == 1, kept[1], kept[2])).astype(BF16)
+    d_att[0] = nt(back_low, w_out[...]).astype(BF16)
 
     @pl.when(step == last)
     def _():
@@ -885,7 +880,7 @@
         grad_down_out[...] = grad_down_t[...].T.astype(BF16)
 
 
-def feed(x, att, cot, weight, scales, w_up_out, w_down, spread):
+def feed(x, att, cot, weight, scales, w_up_out, w_down):
     images, tokens, dim = x.shape
     tile = min(512, tokens)
     hidden_units = w_down.shape[0]
@@ -896,7 +891,6 @@
         jax.ShapeDtypeStruct((images, tokens, dim), BF16),
         jax.ShapeDtypeStruct((images, tokens, dim), F32),
         jax.ShapeDtypeStruct((images, tokens, dim), BF16),
-        jax.ShapeDtypeStruct((images, tokens, 128), BF16),
         jax.ShapeDtypeStruct(w_up_out.shape, BF16),
         jax.ShapeDtypeStruct((hidden_units, dim), BF16),
         jax.ShapeDtypeStruct((images, 1, dim), F32),
@@ -909,11 +903,10 @@
             block(dim), block(dim), block(dim), pl.BlockSpec(memory_space=pltpu.SMEM), whole(scales),
             pl.BlockSpec((dim, dim), lambda i, j: (0, last)),
             pl.BlockSpec((dim, 2 * hidden_units), lambda i, j: (0, 0)),
-            whole(w_down), whole(spread),
+            whole(w_down),
         ],
         out_specs=[
-            block(dim), block(dim), block(dim), block(128),
-            whole(shapes[4]), whole(shapes[5]), row(dim),
+            block(dim), block(dim), block(dim), whole(shapes[3]), whole(shapes[4]), row(dim),
         ],
         out_shape=shapes,
         scratch_shapes=[
@@ -924,13 +917,13 @@
         ],
         compiler_params=pltpu.CompilerParams(vmem_limit_bytes=VMEM_LIMIT),
         name="feed",
-    )(x, att, cot, weight, scales, w_up_out, w_up_out, w_down, spread)
+    )(x, att, cot, weight, scales, w_up_out, w_up_out, w_down)
 
 
 def backward_kernel(height, images, devices, bands, splits, qkv_split, *refs):
     n = len(splits)
     (
-        q, k, v, d_att, logs, deltas,
+        q, k, v, d_att, logs,
         x_mix, q_past, inverse_in, x_norm, d_residual, attn,
         w_qkv, scales, d_scale_two, pool, expand, crow, srow, ccol, scol, chosen, maps,
         grads_hbm,
@@ -941,7 +934,7 @@
         grads, inbox, pieces, arrivals, send, recv,
         qkv_acc, qkv_inbox, qkv_pieces, qkv_arrivals, qkv_send, qkv_recv,
     ) = split_refs(
-        refs, *[None] * 23, n, *[None] * 9, *[None] * 12, *[None] * 7, *[None] * 4,
+        refs, *[None] * 22, n, *[None] * 9, *[None] * 12, *[None] * 7, *[None] * 4,
         n, n, n, n, None, None, *[None] * 6,
     )
     _, band_rows, width, dim = q.shape
@@ -959,7 +952,7 @@
         devices, bands, Copies(send, recv), grads, inbox, pieces, arrivals,
         [[up_out, out_out], [down_out]], splits,
     )
-    hooks = spaced((3, 6, 8), steps[1:-1])
+    hooks = spaced((2, 5, 7), steps[1:-1])
     around = [((dp + d) % devices, band) for d in range(1, devices)]
     beside = [(dp, (band + d) % bands) for d in range(1, bands)]
     small = Copies(small_send, small_recv)
@@ -1113,7 +1106,7 @@
         at = step - 1
         mix_back(at, list(range(1, groups - 1)))
 
-        @pl.when(step >= 2)
+        @pl.when((step >= 2) & (step < images))
         def _():
             for c in range(groups):
                 norm_back(step - 2, c)
@@ -1139,6 +1132,8 @@
         last[0]()
         start(first)
         band_in[band] = sums[...]
+        for c in range(groups):
+            norm_back(images - 2, c)
         steps[-1]()
 
     @pl.when(step == images + 1)
@@ -1148,8 +1143,6 @@
 
     ask = query_features(width)
     ask = jnp.concatenate([ask, ask], axis=0)
-    lane = lanes((queries, 128))
-    one_lanes = jnp.where(lanes((window * wide, 128)) < 3 * 2 * pairs, 1.0, 0.0).astype(BF16)
 
     def send_borders():
         _, band = here()
@@ -1178,20 +1171,13 @@
             mine = slice(side * half, (side + 1) * half)
             theirs = slice(starts[side], starts[side] + wide)
             cut = slice(p * 128, (p + 1) * 128)
-            delta_tile = deltas[0, own, mine].reshape(queries, 128)
-            pulls = []
-            for h in range(2):
-                spot = 3 * (2 * p + h)
-                hit = (lane >= spot) & (lane < spot + 3)
-                pulls.append(jnp.where(hit, delta_tile, jnp.zeros_like(delta_tile)))
             query = block_diagonal(q[0, own, mine, cut].reshape(queries, 128))
             pull = block_diagonal(d_att[0, own, mine, cut].reshape(queries, 128))
             query_wide = jnp.concatenate([query, ask], axis=1)
-            pull_wide = jnp.concatenate([pull, jnp.concatenate(pulls, axis=0)], axis=1)
             key = kf_s[seen, theirs, cut].reshape(window * wide, 128).astype(BF16)
             value = vf_s[seen, theirs, cut].reshape(window * wide, 128).astype(BF16)
             scores = nt(jnp.concatenate([key, feat_s[2 * g + side]], axis=1), query_wide)
-            d_probs = nt(jnp.concatenate([value, one_lanes], axis=1), pull_wide)
+            d_probs = nt(value, pull)
             return scores, d_probs, key, query, pull
 
         def end(side, p, probs, d_scores, key, query, pull):
@@ -1213,7 +1199,9 @@
             if past is not None:
                 end(*past)
             probs = jnp.exp(scores - logs[0, 2 * g + side, p : p + 1])
-            past = (side, p, probs.astype(BF16), (probs * d_probs).astype(BF16), key, query, pull)
+            shares = probs * d_probs
+            inner = jnp.sum(shares, axis=0, keepdims=True)
+            past = (side, p, probs.astype(BF16), (shares - probs * inner).astype(BF16), key, query, pull)
         end(*past)
         return 0
 
@@ -1259,7 +1247,7 @@
 
 
 def backward(
-    q, k, v, d_att, logs, deltas, x, inverse, d_residual, attn, w_qkv, scales, d_scale_two,
+    q, k, v, d_att, logs, x, inverse, d_residual, attn, w_qkv, scales, d_scale_two,
     pool, expand, turns, chosen, maps, height, devices, bands, grads, up_columns, cond_rows, collective,
 ):
     splits = [column_split(grads[0].shape[1], 1920), column_split(grads[1].shape[1], 128)]
@@ -1306,7 +1294,7 @@
         grid=(images + 2,),
         in_specs=[
             block(0, *own, dim), block(0, extended, width, dim), block(0, extended, width, dim),
-            block(0, *own, dim), block(0, *logs.shape[1:]), block(0, *own, 128),
+            block(0, *own, dim), block(0, *logs.shape[1:]),
             block(1, *own, dim), block(1, *own, dim), block(1, *own, 128),
             block(2, *own, dim, buffers=1), block(2, *own, dim), pl.BlockSpec(memory_space=pltpu.SMEM),
             *[once(a.shape) for a in fixed], *[hbm for _ in grads],
@@ -1341,7 +1329,7 @@
             collective_id=collective, has_side_effects=True, vmem_limit_bytes=VMEM_LIMIT
         ),
         name="backward",
-    )(q, k, v, d_att, logs, deltas, x, q, inverse, x, d_residual, attn, *fixed,
+    )(q, k, v, d_att, logs, x, q, inverse, x, d_residual, attn, *fixed,
       *[g.reshape(s) for g, s in zip(grads, shapes)])
 
 
@@ -1363,12 +1351,12 @@
 def finish(arrays, head_count):
     images, rows, width, dim = arrays[0].shape
     whole = lambda a: pl.BlockSpec(a.shape, lambda i: (0,) * len(a.shape))
-    large = pl.BlockSpec((1, rows // 2, width, dim), lambda i: (i // 2, i % 2, 0, 0))
+    large = pl.BlockSpec((1, rows, width, dim), lambda i: (i, 0, 0, 0))
     shapes = [jax.ShapeDtypeStruct(a.shape, a.dtype) for a in arrays[:-1]]
     shapes.append(jax.ShapeDtypeStruct((1, head_count), F32))
     return pl.pallas_call(
         functools.partial(finish_kernel, images),
-        grid=(2 * images,),
+        grid=(images,),
         in_specs=[large, *[whole(a) for a in arrays[1:]]],
         out_specs=[large, *[whole(a) for a in shapes[1:]]],
         out_shape=shapes,
@@ -1399,12 +1387,10 @@
     index = np.arange(256)
     pool = ((index[:, None] % 128) // 64 == np.arange(128)[None, :] // 64).astype(np.float32)
     dim = head_count * 64
-    rows = np.arange(2 * dim)
-    spread = ((rows[:, None] % dim) // 64 == np.arange(128)[None, :] // 3).astype(np.float32)
     pieces = np.arange(dim * 2)
     source = pieces // 128 + 64 * ((pieces % 128) // 64)
     expand = (index[:, None] % 128 == source[None, :]).astype(np.float32)
-    return [jnp.asarray(t, BF16) for t in (pool, spread, expand)]
+    return [jnp.asarray(t, BF16) for t in (pool, expand)]
 
 
 def shards(
@@ -1418,18 +1404,18 @@
     height = band_rows * bands
     (row_cos, row_sin), (col_cos, col_sin) = turn_tables(height, width)
     turns = [jnp.asarray(t) for t in (row_cos, row_sin, col_cos, col_sin)]
-    pool, spread, expand = constants(head_count)
+    pool, expand = constants(head_count)
     (att, q, k, v, inverse, logs, w_qkv, scales, chosen), (maps, w_up_out, w_down) = attend_forward(
         tokens_in, attn_scale, cond, norm1_map, norm2_map, pool, turns, height, devices, bands,
         qkv_weight, up_weight, out_weight, down_weight, 0,
     )
     flat = lambda a: a.reshape(images, tokens, a.shape[-1])
     deep = lambda a: a.reshape(images, band_rows, width, a.shape[-1])
-    result, d_residual, d_att, deltas, grad_up_out, grad_down, d_scale_two = feed(
-        flat(tokens_in), flat(att), flat(cotangent), loss_weight, scales, w_up_out, w_down, spread
+    result, d_residual, d_att, grad_up_out, grad_down, d_scale_two = feed(
+        flat(tokens_in), flat(att), flat(cotangent), loss_weight, scales, w_up_out, w_down
     )
     grads = backward(
-        q, k, v, deep(d_att), logs, deep(deltas), tokens_in, inverse, deep(d_residual), attn_scale, w_qkv,
+        q, k, v, deep(d_att), logs, tokens_in, inverse, deep(d_residual), attn_scale, w_qkv,
         scales, d_scale_two, pool, expand, turns, chosen, maps, height, devices, bands,
         [grad_up_out, grad_down], up_weight.shape[1], images, 1,
     )

time: 212 us -> 204 us (0.962)
  Pallas kernels: 210 us -> 203 us
    pallas_call x1, Pallas kernels: 61.3 us -> 57.4 us  [feed(): pl.pallas_call(feed_kernel, grid=(images, tokens // tile), in_specs=[bloc...]
    pallas_call x1, Pallas kernels: 85.5 us -> 81.7 us  [backward(): pl.pallas_call(functools.partial(backward_kernel, height, images, devices...]
where the time goes in v4:
time: 204 us
  Pallas kernels  203 us (100%)
    pallas_call x1, Pallas kernels, backward(): pl.pallas_call(functools.partial(backward_kernel, height, images, devices...  81.7 us
    pallas_call x1, Pallas kernels, attend_forward(): pl.pallas_call(functools.partial(attend_kernel, height, images, devices,...  58.1 us
    pallas_call x1, Pallas kernels, feed(): pl.pallas_call(feed_kernel, grid=(images, tokens // tile), in_specs=[bloc...  57.4 us
    pallas_call x1, Pallas kernels, finish(): pl.pallas_call(functools.partial(finish_kernel, images), grid=(images,),...  5.77 us

profile of v4, /device:TPU:0, one launch (start us, length us, event | category | flops | bytes accessed | tf_op | source)
XLA Modules:
  0.0 203.8 jit_solution(12238472041933138951)
XLA Ops:
  0.6 58.1 %attend_forward.1 = (bf16[3,16,64,384]{3,2,1,0:T(8,128)(2,1)}, bf16[3,16,64,384]{3,2,1,0:T(8,128)(2,1)}, bf16[3,22,64,384]{3,2,1,0:T(8,128)(2,1)}, bf16[3,22,64,...) custom-call(bf16[3,16,64,384]{3,2,1,0:T(8,128)(2,1)} %refs_8_.2, ...), custom_call_target="tpu_custom_call" | custom-call | tf_op jit(solution)/shard_map/attend_forward/pallas_call | solution.py:730
  58.7 57.4 %feed.1 = (bf16[3,1024,384]{2,1,0:T(8,128)(2,1)}, f32[3,1024,384]{2,1,0:T(8,128)}, bf16[3,1024,384]{2,1,0:T(8,128)(2,1)}, bf16[384,3456]{1,0:T(8,128)(2,1)}, bf1...) custom-call(bf16[3,1024,384]{2,1,0:T(8,128)(2,1)} %bitcast.12, bf16[3,1024,384]{2,1,0:T(8,128)(2,1)} %bitcast.18, ...), custom_call_target="tpu_custom_call" | custom-call | tf_op jit(solution)/shard_map/feed/pallas_call | solution.py:899
  116.1 81.7 %backward.1 = (f32[3,16,64,384]{3,2,1,0:T(8,128)}, f32[12,3072]{1,0:T(8,128)}, f32[12,384]{1,0:T(8,128)}, f32[48,384]{1,0:T(8,128)}, f32[12,1152]{1,0:T(8,128)},...) custom-call(bf16[3,16,64,384]{3,2,1,0:T(8,128)(2,1)} %get-tuple-element.51.refs_0_.refs_6_, ...), custom_call_target="tpu_custom_call" | custom-call | tf_op jit(solution)/shard_map/backward/pallas_call | solution.py:1290
  197.8 5.8 %finish.1 = (f32[3,16,64,384]{3,2,1,0:T(8,128)}, f32[12,3072]{1,0:T(8,128)}, f32[12,384]{1,0:T(8,128)}, f32[48,384]{1,0:T(8,128)}, f32[12,1152]{1,0:T(8,128)}, /...) custom-call(f32[3,16,64,384]{3,2,1,0:T(8,128)} %get-tuple-element.64.refs_0_, ...), custom_call_target="tpu_custom_call" | custom-call | tf_op jit(solution)/shard_map/finish/pallas_call | solution.py:1357

commit v5 on v4

--- a/solution.py
+++ b/solution.py
@@ -539,8 +539,8 @@
         )
         wait()
         own[0]()
+        start(first)
         map_steps[0][0]()
-        start(first)
         first_row = band * band_rows
         build_turns(first_row, crow, srow, ccol, scol, cos_s, sin_s)
         build_key_features(first_row, height, width, feat_s)
@@ -1126,12 +1126,12 @@
 
     @pl.when(step == images)
     def _():
+        start(first)
+        band_in[band] = sums[...]
         tall = qkv_acc.shape[1]
         for d in range(devices):
             qkv_acc[d] = grad_qkv[d * tall : (d + 1) * tall].astype(BF16)
         last[0]()
-        start(first)
-        band_in[band] = sums[...]
         for c in range(groups):
             norm_back(images - 2, c)
         steps[-1]()

time: 204 us -> 204 us (level)
  no operation moved by 1% of the time
where the time goes in v5:
time: 204 us
  Pallas kernels  203 us (100%)
    pallas_call x1, Pallas kernels, backward(): pl.pallas_call(functools.partial(backward_kernel, height, images, devices...  81.6 us
    pallas_call x1, Pallas kernels, attend_forward(): pl.pallas_call(functools.partial(attend_kernel, height, images, devices,...  58.1 us
    pallas_call x1, Pallas kernels, feed(): pl.pallas_call(feed_kernel, grid=(images, tokens // tile), in_specs=[bloc...  57.4 us
    pallas_call x1, Pallas kernels, finish(): pl.pallas_call(functools.partial(finish_kernel, images), grid=(images,),...  5.77 us

profile of v5, /device:TPU:0, one launch (start us, length us, event | category | flops | bytes accessed | tf_op | source)
XLA Modules:
  0.0 203.7 jit_solution(14552404319180062014)
XLA Ops:
  0.6 58.1 %attend_forward.1 = (bf16[3,16,64,384]{3,2,1,0:T(8,128)(2,1)}, bf16[3,16,64,384]{3,2,1,0:T(8,128)(2,1)}, bf16[3,22,64,384]{3,2,1,0:T(8,128)(2,1)}, bf16[3,22,64,...) custom-call(bf16[3,16,64,384]{3,2,1,0:T(8,128)(2,1)} %refs_8_.2, ...), custom_call_target="tpu_custom_call" | custom-call | tf_op jit(solution)/shard_map/attend_forward/pallas_call | solution.py:730
  58.7 57.4 %feed.1 = (bf16[3,1024,384]{2,1,0:T(8,128)(2,1)}, f32[3,1024,384]{2,1,0:T(8,128)}, bf16[3,1024,384]{2,1,0:T(8,128)(2,1)}, bf16[384,3456]{1,0:T(8,128)(2,1)}, bf1...) custom-call(bf16[3,1024,384]{2,1,0:T(8,128)(2,1)} %bitcast.12, bf16[3,1024,384]{2,1,0:T(8,128)(2,1)} %bitcast.18, ...), custom_call_target="tpu_custom_call" | custom-call | tf_op jit(solution)/shard_map/feed/pallas_call | solution.py:899
  116.1 81.6 %backward.1 = (f32[3,16,64,384]{3,2,1,0:T(8,128)}, f32[12,3072]{1,0:T(8,128)}, f32[12,384]{1,0:T(8,128)}, f32[48,384]{1,0:T(8,128)}, f32[12,1152]{1,0:T(8,128)},...) custom-call(bf16[3,16,64,384]{3,2,1,0:T(8,128)(2,1)} %get-tuple-element.51.refs_0_.refs_6_, ...), custom_call_target="tpu_custom_call" | custom-call | tf_op jit(solution)/shard_map/backward/pallas_call | solution.py:1290
  197.7 5.8 %finish.1 = (f32[3,16,64,384]{3,2,1,0:T(8,128)}, f32[12,3072]{1,0:T(8,128)}, f32[12,384]{1,0:T(8,128)}, f32[48,384]{1,0:T(8,128)}, f32[12,1152]{1,0:T(8,128)}, /...) custom-call(f32[3,16,64,384]{3,2,1,0:T(8,128)} %get-tuple-element.64.refs_0_, ...), custom_call_target="tpu_custom_call" | custom-call | tf_op jit(solution)/shard_map/finish/pallas_call | solution.py:1357
